TPU v7x, 128 devices: a whole 4x4x4 slice. The times are simulated.
128 devices in a mesh: req: 16 (over z, y), mlp: 8 (over x, core).
Axes of the slice: x: 4, y: 4, z: 4, core: 2. Of those that a mesh axis runs over, the one named last changes fastest.
Arguments:
- tokens: bfloat16 [4096, 2048], P('req', 'mlp'), may hold values from -5 to 5
- attn_gain: float32 [2048], replicated, may hold values from 0.5 to 1.5
- mlp_gain: float32 [2048], replicated, may hold values from 0.5 to 1.5
- final_gain: float32 [2048], replicated, may hold values from 0.25 to 4
- q_gain: float32 [64], replicated, may hold values from 0.5 to 1.5
- k_gain: float32 [64], replicated, may hold values from 0.25 to 4
- w_query: bfloat16 [2048, 2048], P(None, 'mlp'), may hold values from -0.125 to 0.125
- w_keyval: bfloat16 [2048, 1024], P(None, 'mlp'), may hold values from -0.125 to 0.125
- w_out: bfloat16 [2048, 2048], P('mlp'), may hold values from -0.125 to 0.125
- w_gate: bfloat16 [2048, 8192], P(None, 'mlp'), may hold values from -0.125 to 0.125
- w_up: bfloat16 [2048, 8192], P(None, 'mlp'), may hold values from -0.125 to 0.125
- w_down: bfloat16 [8192, 2048], P('mlp'), may hold values from -0.0625 to 0.0625
- w_head: bfloat16 [2048, 65536], P('req', 'mlp'), may hold values from -0.42 to 0.42
- targets: int32 [4096], P('req'), may hold values from 0 to 65535
- req_lengths: int32 [16, 4], P('req'), may hold values from 1 to 128, 256 in all within a row
- req_tenant: int32 [16, 4], P('req'), may hold values from 0 to 3
- prefix_piece: int32 [16], replicated, may hold values from 0 to 15, each once
- prefix_kv: bfloat16 [16, 1024, 1024], P('req', None, 'mlp'), may hold values from -160 to 160
Outputs:
- hidden_out: bfloat16 [4096, 2048], P('req', 'mlp')
- logprob: float32 [4096], P('req')
Inputs may be any that keep to these rules, and one draw needn't show every extreme that they name: `req_lengths`: each row sums to 256; its longest request has exactly 128 tokens. `prefix_piece`: every piece number appears once; piece n is part n % 4 of the prefix of tenant n // 4.
All inputs are finite; a program needn't handle non-finite values.
Results may differ from a plain program's by a relative error of at most 0.023.
Values may be sent and summed in bfloat16 or wider, within the bound.
A program may use at most 128 MiB of HBM per device.

v0:
```python
import math

import jax
import jax.numpy as jnp
from jax import lax
from jax.sharding import PartitionSpec as P

TENANTS = 4
PLEN = 4096


EPS = 1e-05
LOG_THETA = math.log(1000000.0)
NEG = -1e30


def rms_norm(values, gain):
    return values * lax.rsqrt(jnp.mean(values * values, axis=-1, keepdims=True) + EPS) * gain


def rope_tables(position, size):
    half = size // 2
    freq = jnp.exp(jnp.arange(half, dtype=jnp.float32) * (-2.0 * LOG_THETA / size))
    angle = position[:, None] * freq[None, :]
    return (jnp.cos(angle), jnp.sin(angle))


def rotate(values, cosine, sine):
    half = values.shape[-1] // 2
    first = values[..., :half]
    second = values[..., half:]
    cosine = cosine[:, None, :]
    sine = sine[:, None, :]
    return jnp.concatenate(
        [first * cosine - second * sine, first * sine + second * cosine], axis=-1
    )


def row_layout(lengths, tenants, count):
    ends = jnp.cumsum(lengths)
    row_ids = jnp.arange(count, dtype=jnp.int32)
    request = jnp.sum((row_ids[:, None] >= ends[None, :]).astype(jnp.int32), axis=1)
    onehot = (request[:, None] == jnp.arange(lengths.shape[0], dtype=jnp.int32)[None, :]).astype(
        jnp.int32
    )
    starts = ends - lengths
    offset = row_ids - jnp.sum(onehot * starts[None, :], axis=1)
    tenant = jnp.sum(onehot * tenants[None, :], axis=1)
    return (request, offset, tenant)


def absorb(state, queries, keys, values, seen, scale):
    best, total, accum = state
    scores = jnp.einsum("kqd,knd->kqn", queries, keys, preferred_element_type=jnp.float32) * scale
    scores = jnp.where(seen[None], scores, NEG)
    new_best = jnp.maximum(best, jnp.max(scores, axis=-1))
    keep = jnp.exp(best - new_best)
    weights = jnp.where(seen[None], jnp.exp(scores - new_best[..., None]), 0.0)
    total = total * keep + jnp.sum(weights, axis=-1)
    accum = accum * keep[..., None] + jnp.einsum(
        "kqn,knd->kqd", weights.astype(jnp.bfloat16), values, preferred_element_type=jnp.float32
    )
    return (new_best, total, accum)


def body(
    tokens,
    attn_gain,
    mlp_gain,
    final_gain,
    q_gain,
    k_gain,
    w_query,
    w_keyval,
    w_out,
    w_gate,
    w_up,
    w_down,
    w_head,
    targets,
    req_lengths,
    req_tenant,
    prefix_piece,
    prefix_kv,
):
    rows = tokens.shape[0]
    head_size = q_gain.shape[0]
    local_kv = w_keyval.shape[1] // (2 * head_size)
    local_q = w_query.shape[1] // head_size
    group = local_q // local_kv
    split_count = lax.axis_size("req") // TENANTS
    scale = head_size ** (-0.5)
    stream = lax.all_gather(tokens, "mlp", axis=1, tiled=True)
    stream_f = stream.astype(jnp.float32)
    normed = rms_norm(stream_f, attn_gain).astype(jnp.bfloat16)
    query = jnp.dot(normed, w_query, preferred_element_type=jnp.float32).reshape(
        rows, local_q, head_size
    )
    keyval = jnp.dot(normed, w_keyval, preferred_element_type=jnp.float32).reshape(
        rows, local_kv, 2, head_size
    )
    request, offset, tenant = row_layout(req_lengths[0], req_tenant[0], rows)
    cosine, sine = rope_tables((PLEN + offset).astype(jnp.float32), head_size)
    query = rotate(rms_norm(query, q_gain), cosine, sine).astype(jnp.bfloat16)
    own_keys = (
        rotate(rms_norm(keyval[:, :, 0], k_gain), cosine, sine)
        .astype(jnp.bfloat16)
        .transpose(1, 0, 2)
    )
    own_vals = keyval[:, :, 1].astype(jnp.bfloat16).transpose(1, 0, 2)
    queries = (
        query.reshape(rows, local_kv, group, head_size)
        .transpose(1, 2, 0, 3)
        .reshape(local_kv, group * rows, head_size)
    )
    start_state = (
        jnp.full((local_kv, group * rows), NEG, jnp.float32),
        jnp.zeros((local_kv, group * rows), jnp.float32),
        jnp.zeros((local_kv, group * rows, head_size), jnp.float32),
    )
    piece = lax.all_gather(prefix_kv, "req", axis=0, tiled=True)
    slab = piece.shape[1]

    def one_piece(index, inner_state):
        block = lax.dynamic_index_in_dim(piece, index, 0, keepdims=False).reshape(
            slab, local_kv, 2, head_size
        )
        block_keys = block[:, :, 0].transpose(1, 0, 2)
        block_vals = block[:, :, 1].transpose(1, 0, 2)
        owner_tenant = (
            lax.dynamic_index_in_dim(prefix_piece, index, 0, keepdims=False) // split_count
        )
        seen = jnp.tile(tenant == owner_tenant, group)[:, None]
        return absorb(inner_state, queries, block_keys, block_vals, seen, scale)

    state = lax.fori_loop(0, piece.shape[0], one_piece, start_state)
    row_ids = jnp.arange(rows, dtype=jnp.int32)
    causal = (request[:, None] == request[None, :]) & (row_ids[None, :] <= row_ids[:, None])
    best, total, accum = absorb(
        state, queries, own_keys, own_vals, jnp.tile(causal, (group, 1)), scale
    )
    attended = (
        (accum / total[..., None])
        .reshape(local_kv, group, rows, head_size)
        .transpose(2, 0, 1, 3)
        .reshape(rows, local_q * head_size)
        .astype(jnp.bfloat16)
    )
    attn_proj = jnp.dot(attended, w_out, preferred_element_type=jnp.float32)
    attn_part = lax.psum_scatter(
        attn_proj.astype(jnp.bfloat16), "mlp", scatter_dimension=1, tiled=True
    ).astype(jnp.float32)
    mid_share = (tokens.astype(jnp.float32) + attn_part).astype(jnp.bfloat16)
    middle = lax.all_gather(mid_share, "mlp", axis=1, tiled=True)
    middle_f = middle.astype(jnp.float32)
    normed_mid = rms_norm(middle_f, mlp_gain).astype(jnp.bfloat16)
    gate = jnp.dot(normed_mid, w_gate, preferred_element_type=jnp.float32)
    upper = jnp.dot(normed_mid, w_up, preferred_element_type=jnp.float32)
    inner = (jax.nn.silu(gate) * upper).astype(jnp.bfloat16)
    down = jnp.dot(inner, w_down, preferred_element_type=jnp.float32)
    down_part = lax.psum_scatter(
        down.astype(jnp.bfloat16), "mlp", scatter_dimension=1, tiled=True
    ).astype(jnp.float32)
    out_share = (mid_share.astype(jnp.float32) + down_part).astype(jnp.bfloat16)
    hidden_full = lax.all_gather(out_share, "mlp", axis=1, tiled=True)
    normed_out = rms_norm(hidden_full.astype(jnp.float32), final_gain).astype(jnp.bfloat16)
    vocab_local = w_head.shape[1]
    logits = jnp.dot(
        normed_out,
        lax.all_gather(w_head, "req", axis=0, tiled=True),
        preferred_element_type=jnp.float32,
    )
    vocab_start = lax.axis_index("mlp") * vocab_local
    top = lax.pmax(jnp.max(logits, axis=1), "mlp")
    hit = targets[:, None] - vocab_start == jnp.arange(vocab_local, dtype=jnp.int32)[None, :]
    totals, picked = lax.psum(
        (
            jnp.sum(jnp.exp(logits - top[:, None]), axis=1),
            jnp.sum(jnp.where(hit, logits, 0.0), axis=1),
        ),
        "mlp",
    )
    logprob = picked - top - jnp.log(totals)
    return (out_share, logprob)


def solution(mesh):
    in_specs = (
        P("req", "mlp"),
        P(),
        P(),
        P(),
        P(),
        P(),
        P(None, "mlp"),
        P(None, "mlp"),
        P("mlp", None),
        P(None, "mlp"),
        P(None, "mlp"),
        P("mlp", None),
        P("req", "mlp"),
        P("req"),
        P("req", None),
        P("req", None),
        P(),
        P("req", None, "mlp"),
    )
    out_specs = (P("req", "mlp"), P("req"))
    return jax.shard_map(body, mesh=mesh, in_specs=in_specs, out_specs=out_specs, check_vma=False)
```

profile of v0, /device:TPU:1, one launch (start us, length us, event | category | flops | bytes accessed | tf_op | source)
XLA Modules:
  0.0 688.8 jit_solution(6187407375356977096)
XLA Ops:
  11.8 24.9 %all-gather.8.cloned.1.call-done = bf16[256,2048]{1,0:T(8,128)(2,1)} async-done(((bf16[256,256]{1,0:T(8,128)(2,1)}), bf16[256,2048]{1,0:T(8,128)(2,1)}) %all-gather.8.cloned.1.call-update) | async-done | bytes 1048592 | tf_op jit(solution)/shard_map/all_gather | solution.py:93
  43.5 47.6 %all-gather.6.cloned.1.call-done = bf16[16,1024,128]{2,1,0:T(8,128)(2,1)} async-done(((bf16[1,1024,128]{2,1,0:T(8,128)(2,1)}), bf16[16,1024,128]{2,1,0:T(8,128)(2,1)}) %all-gather.6.cloned.1.call-update) | async-done | bytes 4194320 | tf_op jit(solution)/shard_map/all_gather | solution.py:121
  91.1 210.3 %while.20 = (s32[]{:T(128)}, f32[1,1024]{1,0:T(1,128)S(1)}, f32[1,1024]{1,0:T(1,128)S(1)}, f32[1,1024,64]{1,2,0:T(8,128)}, s32[16]{0:T(128)S(1)}, /*index=5*/s32...) while((s32[]{:T(128)}, f32[1,1024]{1,0:T(1,128)S(1)}, ...), condition=%wide.region_9.10_spmd.clone, body=%wide.region_6.0_spmd.clone.sunk | while | flops 282268928 | bytes 31530828 | solution.py:136
  95.5 2.7 fusion.94
  98.2 3.3 fusion.96
  107.7 2.7 fusion.94
  110.5 3.3 fusion.96
  120.9 2.7 fusion.94
  123.7 3.3 fusion.96
  127.1 2.7 fusion.98
  134.1 2.7 fusion.94
  136.9 3.3 fusion.96
  147.4 2.7 fusion.94
  150.1 3.3 fusion.96
  153.5 2.7 fusion.98
  160.6 2.7 fusion.94
  163.3 3.3 fusion.96
  173.8 2.7 fusion.94
  176.5 3.3 fusion.96
  187.0 2.7 fusion.94
  189.7 3.3 fusion.96
  200.2 2.7 fusion.94
  202.9 3.3 fusion.96
  213.4 2.7 fusion.94
  216.1 3.3 fusion.96
  226.6 2.7 fusion.94
  229.3 3.3 fusion.96
  239.8 2.7 fusion.94
  242.5 3.3 fusion.96
  253.0 2.7 fusion.94
  255.7 3.3 fusion.96
  266.2 2.7 fusion.94
  268.9 3.3 fusion.96
  279.4 2.7 fusion.94
  282.1 3.3 fusion.96
  292.6 2.7 fusion.94
  295.3 3.3 fusion.96
  304.6 28.8 %reduce-scatter.3.cloned.1.call-done = bf16[256,256]{1,0:T(8,128)(2,1)} async-done(((bf16[256,2048]{1,0:T(8,128)(2,1)}), bf16[256,256]{1,0:T(8,128)(2,1)}) %reduce-scatter.3.cloned.1.call-update) | async-done | bytes 131088 | tf_op jit(solution)/shard_map/reduce_scatter | solution.py:150
  335.0 25.8 %all-gather.10.cloned.1.call-done = bf16[256,2048]{1,0:T(8,128)(2,1)} async-done(((bf16[256,256]{1,0:T(8,128)(2,1)}), bf16[256,2048]{1,0:T(8,128)(2,1)}) %all-gather.10.cloned.1.call-update) | async-done | bytes 1048592 | tf_op jit(solution)/shard_map/all_gather | solution.py:154
  362.5 4.8 fusion.46
  367.3 7.3 %convolution_convert_fusion = bf16[256,2048]{1,0:T(8,128)(2,1)} fusion(bf16[1024,2048]{1,0:T(8,128)(2,1)} %param.31, bf16[2048,1024]{1,0:T(8,128)(2,1)} %param.30, f32[256,1024]{1,0:T(8,128)} %fusion.46, bf16[256,2048]{1,0:T(8,128)(2,1)S(1)} %copy-done.5, f32[2048]{0:T(1024)S(1)} %copy-done.11, f32[256]{0:T(256)S(1)} %add_rsqrt_fusion.2), kind=kOutput, calls=%fused_computation.34 | convolution fusion | flops 2151677952 | bytes 11543552 | tf_op jit(solution)/shard_map/dot_general | solution.py:160
  374.7 29.8 %reduce-scatter.5.cloned.1.call-done = bf16[256,256]{1,0:T(8,128)(2,1)} async-done(((bf16[256,2048]{1,0:T(8,128)(2,1)}), bf16[256,256]{1,0:T(8,128)(2,1)}) %reduce-scatter.5.cloned.1.call-update) | async-done | bytes 131088 | tf_op jit(solution)/shard_map/reduce_scatter | solution.py:161
  406.9 25.1 %all-gather.12.cloned.1.call-done = bf16[256,2048]{1,0:T(8,128)(2,1)} async-done(((bf16[256,256]{1,0:T(8,128)(2,1)}), bf16[256,2048]{1,0:T(8,128)(2,1)}) %all-gather.12.cloned.1.call-update) | async-done | bytes 1048592 | tf_op jit(solution)/shard_map/all_gather | solution.py:165
  433.5 198.5 %all-gather.14.cloned.1.call-done = bf16[2048,8192]{1,0:T(8,128)(2,1)} async-done(((bf16[128,8192]{1,0:T(8,128)(2,1)}), bf16[2048,8192]{1,0:T(8,128)(2,1)}) %all-gather.14.cloned.1.call-update) | async-done | bytes 33554448 | tf_op jit(solution)/shard_map/all_gather | solution.py:170
  632.0 17.4 %fusion.77 = (f32[256]{0:T(256)S(1)}, f32[256,8192]{1,0:T(8,128)}) fusion(bf16[2048,8192]{1,0:T(8,128)(2,1)} %all-gather.14.cloned.1.call-done, bf16[256,2048]{1,0:T(8,128)(2,1)} %all-gather.12.cloned.1.call-done, f32[2048]{0:T(1024)S(1)} %copy-done.12, f32[256]{0:T(256)S(1)} %add_rsqrt_fusion.1), kind=kOutput, calls=%fused_computation.123 | convolution fusion | flops 8594128896 | bytes 43001856 | tf_op jit(solution)/shard_map/dot_general | solution.py:168
  649.3 12.4 %pmax.7 = f32[256]{0:T(256)S(1)} all-reduce(f32[256]{0:T(256)S(1)} %get-tuple-element.289), channel_id=1, replica_groups=mesh['req'=16,'mlp'=8] {'mlp'}, use_global_device_ids=true, to_apply=%region_20.21 | all-reduce | flops 256 | bytes 2048 | tf_op jit(solution)/shard_map/pmax | solution.py:174
  661.8 5.1 select_reduce_fusion
  666.9 14.5 %all-reduce = (f32[256]{0:T(256)S(1)}, f32[256]{0:T(256)S(1)}) all-reduce(f32[256]{0:T(256)S(1)} %get-tuple-element.250, f32[256]{0:T(256)S(1)} %get-tuple-element.249), channel_id=1, replica_groups=mesh['req'=16,'mlp'=8] {'mlp'}, use_global_device_ids=true, to_apply=%region_22.23 | all-reduce | flops 512 | bytes 4096 | tf_op jit(solution)/shard_map/psum | solution.py:176
  (272 shorter events, 88.3 us)
Async XLA Ops:
  7.2 295.9 %copy-start = (bf16[256,2048]{1,0:T(8,128)(2,1)S(1)}, bf16[256,2048]{1,0:T(8,128)(2,1)}, u32[]{:S(2)}) copy-start(bf16[256,2048]{1,0:T(8,128)(2,1)} %param.28) | copy-start | bytes 3145732
  7.2 34.0 %copy-start.10 = (f32[2048]{0:T(1024)S(1)}, f32[2048]{0:T(1024)}, u32[]{:S(2)}) copy-start(f32[2048]{0:T(1024)} %param.21) | copy-start | bytes 24580
  7.2 33.4 %copy-start.8 = (f32[64]{0:T(128)S(1)}, f32[64]{0:T(128)}, u32[]{:S(2)}) copy-start(f32[64]{0:T(128)} %param.24) | copy-start | bytes 772
  7.2 29.5 %all-gather.8.cloned.1.call-start = ((), (), s32[]{:S(2)}) async-start(), calls=%async_computation.3 | async-start | bytes 1179648 | tf_op jit(solution)/shard_map/all_gather | solution.py:93
  7.9 83.2 %all-gather.6.cloned.1.call-start = ((), (), s32[]{:S(2)}) async-start(), calls=%async_computation.2 | async-start | bytes 4456448 | tf_op jit(solution)/shard_map/all_gather | solution.py:121
  8.7 324.7 %reduce-scatter.3.cloned.1.call-start = ((), (), s32[]{:S(2)}) async-start(), calls=%async_computation.4 | async-start | bytes 1179648 | tf_op jit(solution)/shard_map/reduce_scatter | solution.py:150
  11.8 31.1 %copy-start.9 = (f32[64]{0:T(128)S(1)}, f32[64]{0:T(128)}, u32[]{:S(2)}) copy-start(f32[64]{0:T(128)} %param.25) | copy-start | bytes 772
  36.7 4.5 copy-start.4
  38.3 52.8 %copy-start.13 = (s32[16]{0:T(128)S(1)}, s32[16]{0:T(128)}, u32[]{:S(2)}) copy-start(s32[16]{0:T(128)} %param.36) | copy-start | bytes 196
  98.2 3.4 copy-start.2
  110.5 3.4 copy-start.2
  123.7 3.4 copy-start.2
  136.9 3.4 copy-start.2
  150.1 3.4 copy-start.2
  163.3 3.4 copy-start.2
  176.5 3.4 copy-start.2
  189.7 3.4 copy-start.2
  202.9 3.4 copy-start.2
  216.1 3.4 copy-start.2
  229.3 3.4 copy-start.2
  242.5 3.4 copy-start.2
  255.7 3.4 copy-start.2
  268.9 3.4 copy-start.2
  282.1 3.4 copy-start.2
  295.3 3.4 copy-start.2
  301.4 31.9 %copy-start.6 = (bf16[256,256]{1,0:T(8,128)(2,1)S(1)}, bf16[256,256]{1,0:T(8,128)(2,1)}, u32[]{:S(2)}) copy-start(bf16[256,256]{1,0:T(8,128)(2,1)} %param.20) | copy-start | bytes 393220
  301.7 60.8 %copy-start.11 = (f32[2048]{0:T(1024)S(1)}, f32[2048]{0:T(1024)}, u32[]{:S(2)}) copy-start(f32[2048]{0:T(1024)} %param.22) | copy-start | bytes 24580
  304.6 56.3 %all-gather.10.cloned.1.call-start = ((), (), s32[]{:S(2)}) async-start(), calls=%async_computation.5 | async-start | bytes 1179648 | tf_op jit(solution)/shard_map/all_gather | solution.py:154
  335.0 69.5 %reduce-scatter.5.cloned.1.call-start = ((), (), s32[]{:S(2)}) async-start(), calls=%async_computation.6 | async-start | bytes 1179648 | tf_op jit(solution)/shard_map/reduce_scatter | solution.py:161
  360.9 6.4 copy-start.5
  367.3 37.2 %copy-start.3 = (bf16[256,256]{1,0:T(8,128)(2,1)S(1)}, bf16[256,256]{1,0:T(8,128)(2,1)}, u32[]{:S(2)}) copy-start(bf16[256,256]{1,0:T(8,128)(2,1)} %add_convert_fusion.1) | copy-start | bytes 393220
  367.3 39.6 %copy-start.7 = (s32[256]{0:T(256)S(1)}, s32[256]{0:T(256)}, u32[]{:S(2)}) copy-start(s32[256]{0:T(256)} %param.33) | copy-start | bytes 3076
  374.6 257.3 %copy-start.12 = (f32[2048]{0:T(1024)S(1)}, f32[2048]{0:T(1024)}, u32[]{:S(2)}) copy-start(f32[2048]{0:T(1024)} %param.23) | copy-start | bytes 24580
  374.7 57.3 %all-gather.12.cloned.1.call-start = ((), (), s32[]{:S(2)}) async-start(), calls=%async_computation.7 | async-start | bytes 1179648 | tf_op jit(solution)/shard_map/all_gather | solution.py:165
  406.1 225.8 %all-gather.14.cloned.1.call-start = ((), (), s32[]{:S(2)}) async-start(), calls=%async_computation.8 | async-start | bytes 35651584 | tf_op jit(solution)/shard_map/all_gather | solution.py:170
  661.8 20.2 %copy-start.1 = (bf16[256,2048]{1,0:T(8,128)(2,1)S(1)}, bf16[256,2048]{1,0:T(8,128)(2,1)}, u32[]{:S(2)}) copy-start(bf16[256,2048]{1,0:T(8,128)(2,1)} %param.28) | copy-start | bytes 3145732
Sparse Core Ops, SparseCore 0:
  9.7 26.9 all-gather.7
  38.8 52.2 all-gather.5
  304.7 28.6 reduce-scatter.2
  335.5 25.3 all-gather.9
  374.8 29.6 reduce-scatter.4
  406.6 25.3 all-gather.11
  434.1 197.7 all-gather.13
where the time goes:
time: 691 us; the launch traced here: 689 us
  waiting for transfers between devices  382 us (55%)
  matrix products  122 us (18%)
  other arithmetic  70.8 us (10%)
  loops' own time  42.2 us (6%)
  local copies, waits for them, and re-layouts  29.7 us (4%)
  blocking collectives  27 us (4%)
  between operations  14.4 us (2%)
    all_gather x1, waiting for transfers between devices, body(): lax.all_gather(w_head, 'req', axis=0, tiled=True)  198 us
    reduce_sum x17, other arithmetic, absorb(): total = total * keep + jnp.sum(weights, axis=-1)  53.3 us
    all_gather x1, waiting for transfers between devices, body(): piece = lax.all_gather(prefix_kv, 'req', axis=0, tiled=True)  47.6 us
    dot_general x17, matrix products, absorb(): jnp.einsum('kqd,knd->kqn', queries, keys, preferred_element_type=jnp.floa...  43.9 us
    dot_general x17, matrix products, absorb(): jnp.einsum('kqn,knd->kqd', weights.astype(jnp.bfloat16), values, preferre...  43.1 us
    another operation x1, loops' own time, body(): state = lax.fori_loop(0, piece.shape[0], one_piece, start_state)  42.2 us
    reduce_scatter x1, waiting for transfers between devices, body(): lax.psum_scatter(down.astype(jnp.bfloat16), 'mlp', scatter_dimension=1, t...  29.8 us
    reduce_scatter x1, waiting for transfers between devices, body(): lax.psum_scatter(attn_proj.astype(jnp.bfloat16), 'mlp', scatter_dimension...  28.8 us
  transfers between devices with their start and end apart: 7, of which 7 were waited for; matrix products, arithmetic and copies ran while one was open for 2% of the time, Pallas kernels for 0%

commit v1 on v0

v1 whole, which is shorter than its diff:
```python
import functools
import math

import jax
import jax.numpy as jnp
from jax import lax
from jax.experimental import pallas as pl
from jax.experimental.pallas import tpu as pltpu
from jax.sharding import Mesh
from jax.sharding import PartitionSpec as P

TENANTS = 4
PLEN = 4096
BLOCK = 64

EPS = 1e-05
LOG_THETA = math.log(1000000.0)
NEG = -1e30


def rms_norm(values, gain):
    return values * lax.rsqrt(jnp.mean(values * values, axis=-1, keepdims=True) + EPS) * gain


def rope_tables(position, size):
    half = size // 2
    freq = jnp.exp(jnp.arange(half, dtype=jnp.float32) * (-2.0 * LOG_THETA / size))
    angle = position[:, None] * freq[None, :]
    return (jnp.cos(angle), jnp.sin(angle))


def rotate(values, cosine, sine):
    half = values.shape[-1] // 2
    first = values[..., :half]
    second = values[..., half:]
    cosine = cosine[:, None, :]
    sine = sine[:, None, :]
    return jnp.concatenate(
        [first * cosine - second * sine, first * sine + second * cosine], axis=-1
    )


def row_layout(lengths, count):
    ends = jnp.cumsum(lengths)
    row_ids = jnp.arange(count, dtype=jnp.int32)
    request = jnp.sum((row_ids[:, None] >= ends[None, :]).astype(jnp.int32), axis=1)
    onehot = (request[:, None] == jnp.arange(lengths.shape[0], dtype=jnp.int32)[None, :]).astype(
        jnp.int32
    )
    starts = ends - lengths
    offset = row_ids - jnp.sum(onehot * starts[None, :], axis=1)
    return (starts, ends, offset)


def dot_nt(a, b):
    return lax.dot_general(a, b, (((1,), (1,)), ((), ())), preferred_element_type=jnp.float32)


def attention_kernel(requests, split, start_ref, end_ref, tenant_ref, slot_ref,
                     q_ref, own_ref, kv_ref, out_ref, best_ref, total_ref, accum_ref):
    block = pl.program_id(0)
    queries = q_ref[0]
    count = queries.shape[0]
    rows = own_ref.shape[0]
    row = (lax.broadcasted_iota(jnp.int32, (count, 1), 0) & (BLOCK - 1)) + block * BLOCK
    col = lax.broadcasted_iota(jnp.int32, (1, rows), 1)
    row_request = jnp.zeros((count, 1), jnp.int32)
    col_request = jnp.zeros((1, rows), jnp.int32)
    for r in range(requests):
        row_request += (row >= end_ref[r]).astype(jnp.int32)
        col_request += (col >= end_ref[r]).astype(jnp.int32)
    seen = (row_request == col_request) & (col <= row)
    own = own_ref[...]
    scores = jnp.where(seen, dot_nt(queries, own), NEG)
    best = jnp.max(scores, axis=1, keepdims=True)
    weights = jnp.where(seen, jnp.exp(scores - best), 0.0)
    best_ref[...] = best
    total_ref[...] = jnp.sum(weights, axis=1, keepdims=True)
    accum_ref[...] = jnp.dot(weights.astype(jnp.bfloat16), own, preferred_element_type=jnp.float32)
    for r in range(requests):

        @pl.when((end_ref[r] > block * BLOCK) & (start_ref[r] < block * BLOCK + BLOCK))
        def _():
            inside = row_request == r
            tenant = tenant_ref[r]

            def piece(index, carry):
                keyval = kv_ref[slot_ref[tenant * split + index]]
                part = dot_nt(queries, keyval)
                old = best_ref[...]
                new = jnp.where(inside, jnp.maximum(old, jnp.max(part, axis=1, keepdims=True)), old)
                keep = jnp.exp(old - new)
                piece_weights = jnp.exp(part - jnp.where(inside, new, -NEG))
                best_ref[...] = new
                total_ref[...] = total_ref[...] * keep + jnp.sum(piece_weights, axis=1, keepdims=True)
                accum_ref[...] = accum_ref[...] * keep + jnp.dot(
                    piece_weights.astype(jnp.bfloat16), keyval, preferred_element_type=jnp.float32
                )
                return carry

            lax.fori_loop(0, split, piece, 0)

    out_ref[0] = (accum_ref[...] / total_ref[...]).astype(jnp.bfloat16)


def attention(starts, ends, tenants, slots, queries, own, pieces):
    blocks, count, width = queries.shape
    smem = pl.BlockSpec(memory_space=pltpu.SMEM)
    return pl.pallas_call(
        functools.partial(attention_kernel, starts.shape[0], slots.shape[0] // TENANTS),
        grid=(blocks,),
        in_specs=[smem, smem, smem, smem,
                  pl.BlockSpec((1, count, width), lambda i: (i, 0, 0)),
                  pl.BlockSpec(own.shape, lambda i: (0, 0)),
                  pl.BlockSpec(pieces.shape, lambda i: (0, 0, 0), pipeline_mode=pl.Buffered(1))],
        out_specs=pl.BlockSpec((1, count, width), lambda i: (i, 0, 0)),
        out_shape=jax.ShapeDtypeStruct((blocks, count, width), jnp.bfloat16),
        scratch_shapes=[pltpu.VMEM((count, 1), jnp.float32), pltpu.VMEM((count, 1), jnp.float32),
                        pltpu.VMEM((count, width), jnp.float32)],
        cost_estimate=pl.CostEstimate(flops=4 * 1024 * 4096 * 128 * 2, bytes_accessed=5 << 20,
                                      transcendentals=1 << 23),
        name="attention",
    )(starts, ends, tenants, slots, queries, own, pieces)


def spread_head(w_head, ny):
    me = lax.axis_index("y")
    depth, vocab = w_head.shape
    part = vocab // ny
    mine = lax.dynamic_slice_in_dim(w_head, me * part, part, 1)
    slab = jnp.zeros((ny * depth, part), w_head.dtype)
    slab = lax.dynamic_update_slice_in_dim(slab, mine, me * depth, 0)
    for shift in range(1, ny):
        give = lax.dynamic_slice_in_dim(w_head, ((me + shift) % ny) * part, part, 1)
        got = lax.ppermute(give, "y", [(i, (i + shift) % ny) for i in range(ny)])
        slab = lax.dynamic_update_slice_in_dim(slab, got, ((me - shift) % ny) * depth, 0)
    return lax.all_gather(slab, "z", axis=0, tiled=True)


def body(
    tokens,
    attn_gain,
    mlp_gain,
    final_gain,
    q_gain,
    k_gain,
    w_query,
    w_keyval,
    w_out,
    w_gate,
    w_up,
    w_down,
    w_head,
    targets,
    req_lengths,
    req_tenant,
    prefix_piece,
    prefix_kv,
):
    rows = tokens.shape[0]
    head_size = q_gain.shape[0]
    local_q = w_query.shape[1] // head_size
    ny = lax.axis_size("y")
    scale = head_size ** (-0.5)
    blocks = rows // BLOCK
    stream = lax.all_gather(tokens, "mlp", axis=1, tiled=True)
    pieces = lax.all_gather(prefix_kv, ("z", "y"), axis=0, tiled=True)
    head = spread_head(w_head, ny)

    normed = rms_norm(stream.astype(jnp.float32), attn_gain).astype(jnp.bfloat16)
    query = jnp.dot(normed, w_query, preferred_element_type=jnp.float32).reshape(
        rows, local_q, head_size
    )
    keyval = jnp.dot(normed, w_keyval, preferred_element_type=jnp.float32).reshape(
        rows, 1, 2, head_size
    )
    starts, ends, offset = row_layout(req_lengths[0], rows)
    cosine, sine = rope_tables((PLEN + offset).astype(jnp.float32), head_size)
    query = rotate(rms_norm(query, q_gain), cosine, sine).astype(jnp.bfloat16) * jnp.bfloat16(scale)
    own = jnp.concatenate(
        [rotate(rms_norm(keyval[:, :, 0], k_gain), cosine, sine)[:, 0], keyval[:, 0, 1]], axis=-1
    ).astype(jnp.bfloat16)
    queries = (
        query.reshape(blocks, BLOCK, local_q, head_size)
        .transpose(0, 2, 1, 3)
        .reshape(blocks, local_q * BLOCK, head_size)
    )
    queries = jnp.pad(queries, ((0, 0), (0, 0), (0, head_size)))
    order = jnp.arange(prefix_piece.shape[0], dtype=jnp.int32)
    slots = jnp.sum(
        jnp.where(prefix_piece[None, :] == order[:, None], order[None, :], 0), axis=1
    ).astype(jnp.int32)
    out = attention(starts, ends, req_tenant[0], slots, queries, own, pieces)
    attended = (
        out[:, :, head_size:]
        .reshape(blocks, local_q, BLOCK, head_size)
        .transpose(0, 2, 1, 3)
        .reshape(rows, local_q * head_size)
    )
    attn_proj = jnp.dot(attended, w_out, preferred_element_type=jnp.float32)
    attn_part = lax.psum_scatter(
        attn_proj.astype(jnp.bfloat16), "mlp", scatter_dimension=1, tiled=True
    ).astype(jnp.float32)
    mid_share = (tokens.astype(jnp.float32) + attn_part).astype(jnp.bfloat16)
    middle = lax.all_gather(mid_share, "mlp", axis=1, tiled=True)
    normed_mid = rms_norm(middle.astype(jnp.float32), mlp_gain).astype(jnp.bfloat16)
    gate = jnp.dot(normed_mid, w_gate, preferred_element_type=jnp.float32)
    upper = jnp.dot(normed_mid, w_up, preferred_element_type=jnp.float32)
    inner = (jax.nn.silu(gate) * upper).astype(jnp.bfloat16)
    down = jnp.dot(inner, w_down, preferred_element_type=jnp.float32)
    down_part = lax.psum_scatter(
        down.astype(jnp.bfloat16), "mlp", scatter_dimension=1, tiled=True
    ).astype(jnp.float32)
    out_share = (mid_share.astype(jnp.float32) + down_part).astype(jnp.bfloat16)
    near = lax.all_gather(out_share, "y", axis=0, tiled=True)
    hidden_full = lax.all_gather(near, "mlp", axis=1, tiled=True)
    normed_out = rms_norm(hidden_full.astype(jnp.float32), final_gain).astype(jnp.bfloat16)
    wanted = lax.all_gather(targets, "y", axis=0, tiled=True)
    logits = jnp.dot(normed_out, head, preferred_element_type=jnp.float32)
    vocab_local = head.shape[1]
    vocab_start = (lax.axis_index("mlp") * ny + lax.axis_index("y")) * vocab_local
    top = jnp.max(logits, axis=1)
    hit = wanted[:, None] - vocab_start == jnp.arange(vocab_local, dtype=jnp.int32)[None, :]
    stats = jnp.stack(
        [
            top,
            jnp.sum(jnp.exp(logits - top[:, None]), axis=1),
            jnp.sum(jnp.where(hit, logits, 0.0), axis=1),
        ]
    )
    every = lax.all_gather(stats, ("y", "mlp"), axis=0)
    every = lax.dynamic_slice_in_dim(every, lax.axis_index("y") * rows, rows, 2)
    top = jnp.max(every[:, 0], axis=0)
    total = jnp.sum(every[:, 1] * jnp.exp(every[:, 0] - top[None, :]), axis=0)
    logprob = jnp.sum(every[:, 2], axis=0) - top - jnp.log(total)
    return (out_share, logprob)


def solution(mesh):
    req = ("z", "y")
    in_specs = (
        P(req, "mlp"),
        P(),
        P(),
        P(),
        P(),
        P(),
        P(None, "mlp"),
        P(None, "mlp"),
        P("mlp", None),
        P(None, "mlp"),
        P(None, "mlp"),
        P("mlp", None),
        P(req, "mlp"),
        P(req),
        P(req, None),
        P(req, None),
        P(),
        P(req, None, "mlp"),
    )
    out_specs = (P(req, "mlp"), P(req))
    split = Mesh(mesh.devices.reshape(4, 4, -1), ("z", "y", "mlp"))
    return jax.shard_map(body, mesh=split, in_specs=in_specs, out_specs=out_specs, check_vma=False)
```

time: 691 us -> 408 us (0.59)
  waiting for transfers between devices: 382 us -> 260 us
  matrix products: 122 us -> 27.8 us
  other arithmetic: 70.8 us -> 18.5 us
  loops' own time: 42.2 us -> 0 us
  Pallas kernels: 0 us -> 24.6 us
  local copies, waits for them, and re-layouts: 29.7 us -> 10.7 us
  blocking collectives: 27 us -> 45.6 us
    all_gather x3, waiting for transfers between devices: 271 us -> 129 us  [the longest x1 82.1 us: spread_head(): return lax.all_gather(slab, 'z', axis=0, tiled=True)]
    dot_general x35 -> x1, matrix products: 104 us -> 12.8 us  [body(): logits = jnp.dot(normed_out, head, preferred_element_type=jnp.float32)]
    reduce_sum x19 -> x4, other arithmetic: 59.1 us -> 4.05 us  [the longest x1 2.57 us: body(): jnp.sum(jnp.exp(logits - top[:, None]), axis=1)]
    all_gather x0 -> x3, blocking collectives: none -> 45.6 us  [the longest x1 25.3 us: body(): every = lax.all_gather(stats, ('y', 'mlp'), axis=0)]
    another operation x1 -> x0, loops' own time: 42.2 us -> none  [body(): state = lax.fori_loop(0, piece.shape[0], one_piece, start_state)]
    pallas_call x0 -> x1, Pallas kernels: none -> 24.6 us  [attention(): pl.pallas_call(functools.partial(attention_kernel, starts.shape[0], slots...]
    dynamic_slice x48 -> x1, local copies, waits for them, and re-layouts: 27.2 us -> 2.83 us  [spread_head(): give = lax.dynamic_slice_in_dim(w_head, (me + shift) % ny * part, part, 1)]
    ppermute x0 -> x3, waiting for transfers between devices: none -> 18.8 us  [spread_head(): got = lax.ppermute(give, 'y', [(i, (i + shift) % ny) for i in range(ny)])]
  transfers between devices with their start and end apart: 7 -> 10, of which waited for: 7 -> 9; matrix products, arithmetic and copies ran while one was open for 2% -> 5% of each run, Pallas kernels for 0% -> 0%
where the time goes in v1:
time: 408 us; the launch traced here: 407 us
  waiting for transfers between devices  260 us (64%)
  blocking collectives  45.6 us (11%)
  matrix products  27.8 us (7%)
  Pallas kernels  24.6 us (6%)
  other arithmetic  18.5 us (5%)
  between operations  14.6 us (4%)
  local copies, waits for them, and re-layouts  10.7 us (3%)
  starting transfers between devices  5.06 us (1%)
    all_gather x1, waiting for transfers between devices, spread_head(): return lax.all_gather(slab, 'z', axis=0, tiled=True)  82.1 us
    all_gather x1, waiting for transfers between devices, body(): pieces = lax.all_gather(prefix_kv, ('z', 'y'), axis=0, tiled=True)  46.6 us
    reduce_scatter x1, waiting for transfers between devices, body(): lax.psum_scatter(attn_proj.astype(jnp.bfloat16), 'mlp', scatter_dimension...  32 us
    reduce_scatter x1, waiting for transfers between devices, body(): lax.psum_scatter(down.astype(jnp.bfloat16), 'mlp', scatter_dimension=1, t...  29.8 us
    all_gather x1, waiting for transfers between devices, body(): middle = lax.all_gather(mid_share, 'mlp', axis=1, tiled=True)  25.8 us
    all_gather x1, blocking collectives, body(): every = lax.all_gather(stats, ('y', 'mlp'), axis=0)  25.3 us
    pallas_call x1, Pallas kernels, attention(): pl.pallas_call(functools.partial(attention_kernel, starts.shape[0], slots...  24.6 us
    all_gather x1, waiting for transfers between devices, body(): stream = lax.all_gather(tokens, 'mlp', axis=1, tiled=True)  23.6 us
  transfers between devices with their start and end apart: 10, of which 9 were waited for; matrix products, arithmetic and copies ran while one was open for 5% of the time, Pallas kernels for 0%

profile of v1, /device:TPU:1, one launch (start us, length us, event | category | flops | bytes accessed | tf_op | source)
XLA Modules:
  0.0 407.0 jit_solution(12387043216743139696)
XLA Ops:
  7.2 0.7 all-gather.9.cloned.1.call-update
  8.0 0.7 all-gather.11.cloned.1.call-update
  8.7 0.8 reduce-window.4
  9.6 1.4 select_reduce_fusion.1.slot_ref
  11.0 0.7 fusion.37
  11.8 1.2 bitcast_subtract_fusion.2.start_ref
  13.1 23.6 %all-gather.9.cloned.1.call-done = bf16[256,2048]{1,0:T(8,128)(2,1)} async-done(((bf16[256,256]{1,0:T(8,128)(2,1)}), bf16[256,2048]{1,0:T(8,128)(2,1)}) %all-gather.9.cloned.1.call-update) | async-done | bytes 1048592 | tf_op jit(solution)/shard_map/all_gather | solution.py:166
  36.7 1.6 fusion.7
  38.3 1.9 fusion.19
  40.3 0.7 multiply_reduce_fusion
  41.5 0.2 fusion.23
  41.7 0.2 copy.36
  42.1 0.7 pad.4.q_ref
  43.1 0.6 fusion.29
  43.8 0.7 pad_maximum_fusion.own_ref
  44.5 46.6 %all-gather.11.cloned.1.call-done.kv_ref = bf16[16,1024,128]{2,1,0:T(8,128)(2,1)} async-done(((bf16[1,1024,128]{2,1,0:T(8,128)(2,1)}), bf16[16,1024,128]{2,1,0:T(8,128)(2,1)}) %all-gather.11.cloned.1.call-update) | async-done | bytes 4194320 | tf_op jit(solution)/shard_map/all_gather | solution.py:167
  91.1 24.6 %attention.1 = bf16[4,256,128]{2,1,0:T(8,128)(2,1)} custom-call(s32[4]{0:T(128)} %bitcast_subtract_fusion.2.start_ref, s32[4]{0:T(128)} %bitcast.78, s32[4]{0:T(128)} %bitcast.76, s32[16]{0:T(128)} %select_reduce_fusion.1.slot_ref, bf16[4,256,128]{2,1,0:T(8,128)(2,1)} %pad.4.q_ref, bf16[256,128]{1,0:T(8,128)(2,1)} %pad_maximum_fusion.own_ref, ...), custom_call_target="tpu_custom_call" | custom-call | flops 4294967296 | bytes 5242880 | tf_op jit(solution)/shard_map/attention/pallas_call | solution.py:109
  115.7 1.1 slice.48
  117.0 0.2 reshape.271
  117.2 1.4 convolution_convert_fusion.1
  118.8 32.0 %reduce-scatter.3.cloned.1.call-done = bf16[256,256]{1,0:T(8,128)(2,1)} async-done(((bf16[256,2048]{1,0:T(8,128)(2,1)}), bf16[256,256]{1,0:T(8,128)(2,1)}) %reduce-scatter.3.cloned.1.call-update) | async-done | bytes 131088 | tf_op jit(solution)/shard_map/reduce_scatter | solution.py:201
  150.8 1.6 add_convert_fusion.1
  152.4 25.8 %all-gather.13.cloned.1.call-done = bf16[256,2048]{1,0:T(8,128)(2,1)} async-done(((bf16[256,256]{1,0:T(8,128)(2,1)}), bf16[256,2048]{1,0:T(8,128)(2,1)}) %all-gather.13.cloned.1.call-update) | async-done | bytes 1048592 | tf_op jit(solution)/shard_map/all_gather | solution.py:205
  178.2 1.5 fusion.10
  179.8 3.9 fusion.17
  183.7 7.1 %convolution_convert_fusion = bf16[256,2048]{1,0:T(8,128)(2,1)} fusion(bf16[1024,2048]{1,0:T(8,128)(2,1)} %param.29, bf16[2048,1024]{1,0:T(8,128)(2,1)} %param.28, f32[256,1024]{1,0:T(8,128)S(1)} %fusion.17, bf16[256,2048]{1,0:T(8,128)(2,1)S(1)} %copy-done.4, f32[2048]{0:T(1024)S(1)} %copy-done.12, f32[256]{0:T(256)S(1)} %add_rsqrt_fusion.2), kind=kOutput, calls=%fused_computation.15 | convolution fusion | flops 2151677952 | bytes 11543552 | tf_op jit(solution)/shard_map/dot_general | solution.py:210
  190.9 29.8 %reduce-scatter.5.cloned.1.call-done = bf16[256,256]{1,0:T(8,128)(2,1)} async-done(((bf16[256,2048]{1,0:T(8,128)(2,1)}), bf16[256,256]{1,0:T(8,128)(2,1)}) %reduce-scatter.5.cloned.1.call-update) | async-done | bytes 131088 | tf_op jit(solution)/shard_map/reduce_scatter | solution.py:211
  220.6 0.9 add_convert_fusion
  221.6 11.0 %all_gather.30 = bf16[1024,256]{1,0:T(8,128)(2,1)} all-gather(bf16[256,256]{1,0:T(8,128)(2,1)S(1)} %add_convert_fusion), channel_id=1, replica_groups=mesh['z'=4,'y'=4,'mlp'=8] {'y'}, dimensions={0}, use_global_device_ids=true | all-gather | bytes 655360 | tf_op jit(solution)/shard_map/all_gather | solution.py:215
  232.7 0.2 broadcast_in_dim.15
  233.0 2.8 constant_dynamic-slice_fusion.1
  235.8 2.1 collective-permute-start
  237.9 2.4 collective-permute-start.1
  240.3 0.3 collective-permute-start.2
  240.6 5.4 %collective-permute-done = bf16[128,2048]{1,0:T(8,128)(2,1)} collective-permute-done((bf16[128,2048]{1,0:T(8,128)(2,1)}, bf16[128,2048]{1,0:T(8,128)(2,1)}, u32[]{:S(2)}, u32[]{:S(2)}) %collective-permute-start) | collective-permute-done | bytes 524320 | tf_op jit(solution)/shard_map/ppermute | solution.py:135
  246.0 1.1 constant_dynamic-update-slice_fusion.2
  247.1 11.6 %collective-permute-done.1 = bf16[128,2048]{1,0:T(8,128)(2,1)} collective-permute-done((bf16[128,2048]{1,0:T(8,128)(2,1)}, bf16[128,2048]{1,0:T(8,128)(2,1)}, u32[]{:S(2)}, u32[]{:S(2)}) %collective-permute-start.1) | collective-permute-done | bytes 524320 | tf_op jit(solution)/shard_map/ppermute | solution.py:135
  258.8 1.1 constant_dynamic-update-slice_fusion.1
  259.9 1.8 collective-permute-done.2
  261.6 1.1 constant_dynamic-update-slice_fusion
  262.7 1.4 copy-done.1
  264.1 9.2 %all-gather.1 = s32[4,1,256]{2,1,0:T(1,128)S(1)} all-gather(s32[1,1,256]{2,1,0:T(1,128)S(1)} %bitcast.74), channel_id=1, replica_groups=mesh['z'=4,'y'=4,'mlp'=8] {'y'}, dimensions={0}, use_global_device_ids=true | all-gather | bytes 5120 | tf_op jit(solution)/shard_map/all_gather | solution.py:218
  273.4 3.1 fusion
  276.5 82.1 %all-gather.17.cloned.1.call-done = bf16[2048,2048]{1,0:T(8,128)(2,1)} async-done(((bf16[512,2048]{1,0:T(8,128)(2,1)}), bf16[2048,2048]{1,0:T(8,128)(2,1)}) %all-gather.17.cloned.1.call-update) | async-done | bytes 8388624 | tf_op jit(solution)/shard_map/all_gather | solution.py:137
  358.6 12.8 %fusion.40 = (f32[1024]{0:T(1024)S(1)}, f32[1024,2048]{1,0:T(8,128)S(1)}) fusion(bf16[2048,2048]{1,0:T(8,128)(2,1)} %all-gather.17.cloned.1.call-done, bf16[1024,2048]{1,0:T(8,128)(2,1)} %all-gather.15.cloned.1.call-done, f32[2048]{0:T(1024)S(1)} %copy-done.13, f32[1024]{0:T(1024)S(1)} %add_rsqrt_fusion), kind=kOutput, calls=%fused_computation.93 | convolution fusion | flops 8600419328 | bytes 20987904 | tf_op jit(solution)/shard_map/dot_general | solution.py:219
  371.4 2.6 exponential_reduce_fusion
  374.0 25.3 %all-gather.2 = f32[32,3,1024]{2,1,0:T(4,128)S(1)} all-gather(f32[1,3,1024]{2,1,0:T(4,128)S(1)} %maximum_bitcast_fusion.1), channel_id=2, replica_groups=mesh['z'=4,'y'=4,'mlp'=8] {'y','mlp'}, dimensions={0}, use_global_device_ids=true | all-gather | bytes 405504 | tf_op jit(solution)/shard_map/all_gather | solution.py:231
  399.6 0.6 log_subtract_fusion
  (68 shorter events, 2.2 us)
Async XLA Ops:
  7.2 110.1 %copy-start = (bf16[256,2048]{1,0:T(8,128)(2,1)S(1)}, bf16[256,2048]{1,0:T(8,128)(2,1)}, u32[]{:S(2)}) copy-start(bf16[256,2048]{1,0:T(8,128)(2,1)} %param.26) | copy-start | bytes 3145732
  7.2 33.1 %copy-start.11 = (f32[2048]{0:T(1024)S(1)}, f32[2048]{0:T(1024)}, u32[]{:S(2)}) copy-start(f32[2048]{0:T(1024)} %param.19) | copy-start | bytes 24580
  7.2 33.1 %copy-start.10 = (bf16[2048,256]{1,0:T(8,128)(2,1)S(1)}, bf16[2048,256]{1,0:T(8,128)(2,1)}, u32[]{:S(2)}) copy-start(bf16[2048,256]{1,0:T(8,128)(2,1)} %param.24) | copy-start | bytes 3145732
  7.2 29.5 %all-gather.9.cloned.1.call-start = ((), (), s32[]{:S(2)}) async-start(), calls=%async_computation.2 | async-start | bytes 1179648 | tf_op jit(solution)/shard_map/all_gather | solution.py:166
  7.9 83.2 %all-gather.11.cloned.1.call-start = ((), (), s32[]{:S(2)}) async-start(), calls=%async_computation.3 | async-start | bytes 4456448 | tf_op jit(solution)/shard_map/all_gather | solution.py:167
  8.7 142.1 %reduce-scatter.3.cloned.1.call-start = ((), (), s32[]{:S(2)}) async-start(), calls=%async_computation.4 | async-start | bytes 1179648 | tf_op jit(solution)/shard_map/reduce_scatter | solution.py:201
  9.6 31.5 %copy-start.14 = (s32[4,1]{0,1:T(1,128)}, s32[4,1]{0,1:T(1,128)S(1)}, u32[]{:S(2)}) copy-start(s32[4,1]{0,1:T(1,128)S(1)} %reduce-window.4) | copy-start | bytes 52
  36.7 3.6 copy-start.3
  40.3 0.8 copy-start.8
  41.0 2.0 copy-start.9
  116.8 34.0 %copy-start.6 = (bf16[256,256]{1,0:T(8,128)(2,1)S(1)}, bf16[256,256]{1,0:T(8,128)(2,1)}, u32[]{:S(2)}) copy-start(bf16[256,256]{1,0:T(8,128)(2,1)} %param.18) | copy-start | bytes 393220
  117.2 62.5 %copy-start.12 = (f32[2048]{0:T(1024)S(1)}, f32[2048]{0:T(1024)}, u32[]{:S(2)}) copy-start(f32[2048]{0:T(1024)} %param.20) | copy-start | bytes 24580
  118.7 59.5 %all-gather.13.cloned.1.call-start = ((), (), s32[]{:S(2)}) async-start(), calls=%async_computation.5 | async-start | bytes 1179648 | tf_op jit(solution)/shard_map/all_gather | solution.py:205
  152.4 68.2 %reduce-scatter.5.cloned.1.call-start = ((), (), s32[]{:S(2)}) async-start(), calls=%async_computation.6 | async-start | bytes 1179648 | tf_op jit(solution)/shard_map/reduce_scatter | solution.py:211
  179.8 3.9 copy-start.4
  183.7 37.0 %copy-start.2 = (bf16[256,256]{1,0:T(8,128)(2,1)S(1)}, bf16[256,256]{1,0:T(8,128)(2,1)}, u32[]{:S(2)}) copy-start(bf16[256,256]{1,0:T(8,128)(2,1)} %add_convert_fusion.1) | copy-start | bytes 393220
  190.8 82.6 %all-gather.15.cloned.1.call-start = ((), (), s32[]{:S(2)}) async-start(), calls=%async_computation.7 | async-start | bytes 4718592 | tf_op jit(solution)/shard_map/all_gather | solution.py:216
  221.6 14.2 %copy-start.5 = (bf16[256,256]{1,0:T(8,128)(2,1)}, bf16[256,256]{1,0:T(8,128)(2,1)S(1)}, u32[]{:S(2)}) copy-start(bf16[256,256]{1,0:T(8,128)(2,1)S(1)} %add_convert_fusion) | copy-start | bytes 393220
  232.6 126.0 %all-gather.17.cloned.1.call-start = ((), (), s32[]{:S(2)}) async-start(), calls=%async_computation.8 | async-start | bytes 10485760 | tf_op jit(solution)/shard_map/all_gather | solution.py:137
  235.8 10.2 %collective-permute-start = (bf16[128,2048]{1,0:T(8,128)(2,1)}, bf16[128,2048]{1,0:T(8,128)(2,1)}, u32[]{:S(2)}, u32[]{:S(2)}) collective-permute-start(bf16[128,2048]{1,0:T(8,128)(2,1)} %get-tuple-element.7), channel_id=1, source_target_pairs={{0,8},{8,16},{16,24},{24,0},{1,9},{9,17},{17,25},{25,1},{2,10},{10... | collective-permute-start | bytes 1572872 | tf_op jit(solution)/shard_map/ppermute | solution.py:135
  237.9 20.8 %collective-permute-start.1 = (bf16[128,2048]{1,0:T(8,128)(2,1)}, bf16[128,2048]{1,0:T(8,128)(2,1)}, u32[]{:S(2)}, u32[]{:S(2)}) collective-permute-start(bf16[128,2048]{1,0:T(8,128)(2,1)} %get-tuple-element.9), channel_id=1, source_target_pairs={{0,16},{8,24},{16,0},{24,8},{1,17},{9,25},{17,1},{25,9},{2,18},{10... | collective-permute-start | bytes 1572872 | tf_op jit(solution)/shard_map/ppermute | solution.py:135
  240.3 21.3 %collective-permute-start.2 = (bf16[128,2048]{1,0:T(8,128)(2,1)}, bf16[128,2048]{1,0:T(8,128)(2,1)}, u32[]{:S(2)}, u32[]{:S(2)}) collective-permute-start(bf16[128,2048]{1,0:T(8,128)(2,1)} %get-tuple-element.6), channel_id=1, source_target_pairs={{0,24},{8,0},{16,8},{24,16},{1,25},{9,1},{17,9},{25,17},{2,26},{10... | collective-permute-start | bytes 1572872 | tf_op jit(solution)/shard_map/ppermute | solution.py:135
  247.1 17.0 %copy-start.7 = (s32[256]{0:T(256)S(1)}, s32[256]{0:T(256)}, u32[]{:S(2)}) copy-start(s32[256]{0:T(256)} %param.31) | copy-start | bytes 3076
  262.7 1.4 copy-start.1
  273.4 85.2 %copy-start.13 = (f32[2048]{0:T(1024)S(1)}, f32[2048]{0:T(1024)}, u32[]{:S(2)}) copy-start(f32[2048]{0:T(1024)} %param.21) | copy-start | bytes 24580
Sparse Core Ops, SparseCore 0:
  9.7 26.9 all-gather.8
  38.8 52.2 all-gather.10
  118.8 31.9 reduce-scatter.2
  152.9 25.3 all-gather.12
  190.9 29.6 reduce-scatter.4
  232.7 40.2 all-gather.14
  274.7 83.8 all-gather.16

commit v2 on v1

v2 whole, which is shorter than its diff:
```python
import functools
import math

import jax
import jax.numpy as jnp
from jax import lax
from jax.experimental import pallas as pl
from jax.experimental.pallas import tpu as pltpu
from jax.sharding import Mesh
from jax.sharding import PartitionSpec as P

TENANTS = 4
PLEN = 4096
BLOCK = 64
EPS = 1e-05
LOG_THETA = math.log(1000000.0)
NEG = -1e30
RING = 4
MESH = pl.DeviceIdType.MESH
F32 = jnp.float32
BF16 = jnp.bfloat16


def dot(a, b):
    return jnp.dot(a, b, preferred_element_type=F32)


def dot_nt(a, b):
    return lax.dot_general(a, b, (((1,), (1,)), ((), ())), preferred_element_type=F32)


def remote(src, dst, send_sem, recv_sem, **device):
    return pltpu.make_async_remote_copy(
        src_ref=src, dst_ref=dst, send_sem=send_sem, recv_sem=recv_sem,
        device_id=device, device_id_type=MESH,
    )


def arrived(ref, sem):
    pltpu.make_async_copy(ref, ref, sem).wait()


def greet(peers):
    barrier = pltpu.get_barrier_semaphore()
    for peer in peers:
        pl.semaphore_signal(barrier, inc=1, device_id=peer, device_id_type=MESH)
    pl.semaphore_wait(barrier, len(peers))


def ring_of(axis, core):
    me = lax.axis_index(axis)
    ahead = lax.rem(me + 1 + 2 * core, RING)
    back = lax.rem(me + 3 + 2 * core, RING)
    far = lax.rem(me + 2, RING)
    return (me, ahead, back, far)


class Gather:
    def __init__(self, slots, send, recv):
        self.slots, self.send, self.recv, self.sent = slots, send, recv, []
        self.core = lax.axis_index("c")
        self.x, self.ahead, self.back, self.far = ring_of("x", self.core)

    def push(self, at, core, src=None, **device):
        slot = 2 * at + core
        copy = remote(self.slots.at[slot] if src is None else src, self.slots.at[slot],
                      self.send.at[len(self.sent)], self.recv.at[slot], **device)
        copy.start()
        self.sent.append(copy)

    def wait(self, at, core):
        slot = 2 * at + core
        arrived(self.slots.at[slot], self.recv.at[slot])

    def open(self, src=None):
        self.push(self.x, self.core, src, x=self.ahead)
        self.push(self.x, self.core, src, x=self.back)
        self.push(self.x, self.core, src, c=1 - self.core)

    def relay(self):
        self.wait(self.back, self.core)
        self.push(self.back, self.core, x=self.ahead)
        self.push(self.back, self.core, c=1 - self.core)
        self.wait(self.ahead, self.core)
        self.push(self.ahead, self.core, c=1 - self.core)

    def close(self):
        self.wait(self.far, self.core)
        self.push(self.far, self.core, c=1 - self.core)
        for x in (self.x, self.back, self.ahead, self.far):
            self.wait(x, 1 - self.core)

    def finish(self):
        for copy in self.sent:
            copy.wait_send()


def scatter_sum(partial, stage, paired, inbox, send, pair_sem, in_sem):
    core = lax.axis_index("c")
    x, ahead, back, far = ring_of("x", core)
    sent = []

    def push(value, dst, recv, **device):
        index = len(sent)
        stage[index] = value.astype(BF16)
        copy = remote(stage.at[index], dst, send.at[index], recv, **device)
        copy.start()
        sent.append(copy)

    def chip(to):
        mine = partial(2 * to + core)
        arrived(paired.at[to], pair_sem.at[to])
        return mine + paired[to].astype(F32)

    for to in (far, back, ahead, x):
        push(partial(2 * to + 1 - core), paired.at[to], pair_sem.at[to], c=1 - core)
    push(chip(far), inbox.at[2], in_sem.at[2], x=ahead)
    push(chip(back), inbox.at[1], in_sem.at[1], x=back)
    value = chip(ahead)
    arrived(inbox.at[2], in_sem.at[2])
    push(value + inbox[2].astype(F32), inbox.at[0], in_sem.at[0], x=ahead)
    value = chip(x)
    for slot in (1, 0):
        arrived(inbox.at[slot], in_sem.at[slot])
        value += inbox[slot].astype(F32)
    for copy in sent:
        copy.wait_send()
    return value


def normalise(blocks, gain_ref, normed):
    count, rows, width = blocks.shape
    square = jnp.zeros((rows, 1), F32)
    for m in range(count):
        value = blocks[m].astype(F32)
        square += jnp.sum(value * value, axis=1, keepdims=True)
    factor = lax.rsqrt(square / (count * width) + EPS)
    for m in range(count):
        columns = slice(m * width, (m + 1) * width)
        normed[:, columns] = (blocks[m].astype(F32) * factor * gain_ref[:, columns]).astype(BF16)


def x_peers():
    core = lax.axis_index("c")
    _, ahead, back, _ = ring_of("x", core)
    return [dict(x=ahead), dict(x=back), dict(c=1 - core)]


def entry_kernel(requests, scale, length_ref, tok_ref, gain_ref, qgain_ref, kgain_ref, wq_ref,
                 wkv_ref, prefix_ref, q_out, own_out, pieces, stream, normed, send, recv,
                 psend, precv, local_sem):
    core = lax.axis_index("c")
    rows = tok_ref.shape[0]
    size = qgain_ref.shape[1]
    half = prefix_ref.shape[1] // 2
    y, y_ahead, y_back, y_far = ring_of("y", core)
    z, z_ahead, z_back, z_far = ring_of("z", core)
    greet(x_peers() + [dict(y=y_ahead), dict(y=y_back), dict(z=z_ahead), dict(z=z_back)])

    sent = []

    def view(part, pz, py):
        return pieces.at[pz * RING + py, pl.ds(part * half, half)]

    def push(part, pz, py, src=None, **device):
        slot = pz * RING + py
        copy = remote(view(part, pz, py) if src is None else src, view(part, pz, py),
                      psend.at[len(sent)], precv.at[part, slot], **device)
        copy.start()
        sent.append(copy)

    def wait(part, pz, py):
        arrived(view(part, pz, py), precv.at[part, pz * RING + py])

    first = [prefix_ref.at[0, pl.ds(part * half, half)] for part in range(2)]
    gather = Gather(stream, send, recv)
    gather.open(tok_ref)
    push(0, z, y, first[0], y=y_ahead)
    push(0, z, y, first[0], y=y_back)
    push(1, z, y, first[1], z=z_ahead)
    push(1, z, y, first[1], z=z_back)
    push(0, z, y, first[0], z=z_ahead)
    push(0, z, y, first[0], z=z_back)
    push(1, z, y, first[1], y=y_ahead)
    push(1, z, y, first[1], y=y_back)
    keep = [pltpu.make_async_copy(prefix_ref.at[0], pieces.at[z * RING + y], local_sem.at[0]),
            pltpu.make_async_copy(tok_ref, stream.at[2 * gather.x + core], local_sem.at[1])]
    for copy in keep:
        copy.start()

    wait(0, z, y_back)
    push(0, z, y_back, y=y_ahead)
    push(0, z, y_back, z=z_ahead)
    push(0, z, y_back, z=z_back)
    wait(1, z_back, y)
    push(1, z_back, y, z=z_ahead)
    push(1, z_back, y, y=y_ahead)
    push(1, z_back, y, y=y_back)
    wait(0, z, y_ahead)
    push(0, z, y_ahead, z=z_ahead)
    push(0, z, y_ahead, z=z_back)
    wait(1, z_ahead, y)
    push(1, z_ahead, y, y=y_ahead)
    push(1, z_ahead, y, y=y_back)
    gather.relay()
    wait(0, z, y_far)
    push(0, z, y_far, z=z_ahead)
    push(0, z, y_far, z=z_back)
    wait(1, z_far, y)
    push(1, z_far, y, y=y_ahead)
    push(1, z_far, y, y=y_back)

    row = lax.broadcasted_iota(jnp.int32, (rows, 1), 0)
    offset = row
    end = 0
    for r in range(requests):
        end = end + length_ref[0, r]
        offset = offset - jnp.where(row >= end, length_ref[0, r], 0)
    lane = lax.broadcasted_iota(jnp.int32, (1, size), 1)
    freq = jnp.exp((lane & (size // 2 - 1)).astype(F32) * (-2.0 * LOG_THETA / size))
    angle = (PLEN + offset).astype(F32) * freq
    cosine, sine = jnp.cos(angle), jnp.sin(angle)

    def turned(value, gain):
        value = value * lax.rsqrt(jnp.mean(value * value, axis=1, keepdims=True) + EPS) * gain
        other = jnp.concatenate([-value[:, size // 2:], value[:, : size // 2]], axis=1)
        return (value * cosine + other * sine).astype(BF16)

    keep[1].wait()
    gather.close()
    normalise(stream, gain_ref, normed)

    far_z = [(py, z_back, z_ahead) for py in (y, y_far)] + [(py, z_ahead, z_back) for py in (y_back, y_ahead)]
    far_y = [(pz, y_back, y_ahead) for pz in (z, z_far)] + [(pz, y_ahead, y_back) for pz in (z_back, z_ahead)]
    order = (0, 2, 3, 1)
    for i in order:
        py, come, go = far_z[i]
        wait(0, come, py)
        push(0, come, py, z=go)
        pz, come, go = far_y[i]
        wait(1, pz, come)
        push(1, pz, come, y=go)

    query = dot(normed[...], wq_ref[...])
    keyval = dot(normed[...], wkv_ref[...])
    heads = query.shape[1] // size
    zero = jnp.zeros((rows, size), BF16)
    for h in range(heads):
        value = turned(query[:, h * size:(h + 1) * size], qgain_ref[...])
        value = jnp.concatenate([value * jnp.asarray(scale, BF16), zero], axis=1)
        for i in range(rows // BLOCK):
            q_out[i, h * BLOCK:(h + 1) * BLOCK, :] = value[i * BLOCK:(i + 1) * BLOCK]
    own_out[...] = jnp.concatenate(
        [turned(keyval[:, :size], kgain_ref[...]), keyval[:, size:].astype(BF16)], axis=1
    )

    for py, come, go in far_z:
        wait(0, go, py)
    for pz, come, go in far_y:
        wait(1, pz, go)
    for py, come, go in far_z:
        wait(0, z_far, py)
    for pz, come, go in far_y:
        wait(1, pz, y_far)
    keep[0].wait()
    gather.finish()
    for copy in sent:
        copy.wait_send()


def vmem():
    return pl.BlockSpec(memory_space=pltpu.VMEM)


def hbm():
    return pl.BlockSpec(memory_space=pl.ANY)


def smem():
    return pl.BlockSpec(memory_space=pltpu.SMEM)


def entry(lengths, tokens, attn_gain, q_gain, k_gain, w_query, w_keyval, prefix_kv):
    rows, width = tokens.shape
    size = q_gain.shape[1]
    heads = w_query.shape[1] // size
    count = RING * RING
    return pl.pallas_call(
        functools.partial(entry_kernel, lengths.shape[1], size ** (-0.5)),
        in_specs=[smem()] + [vmem()] * 7,
        out_specs=[vmem(), vmem(), hbm()],
        out_shape=[jax.ShapeDtypeStruct((rows // BLOCK, heads * BLOCK, 2 * size), BF16),
                   jax.ShapeDtypeStruct((rows, 2 * size), BF16),
                   jax.ShapeDtypeStruct((count,) + prefix_kv.shape[1:], BF16)],
        scratch_shapes=[pltpu.VMEM((8, rows, width), BF16), pltpu.VMEM((rows, 8 * width), BF16),
                        pltpu.SemaphoreType.DMA((7,)), pltpu.SemaphoreType.DMA((8,)),
                        pltpu.SemaphoreType.DMA((30,)), pltpu.SemaphoreType.DMA((2, count)),
                        pltpu.SemaphoreType.DMA((2,))],
        compiler_params=pltpu.CompilerParams(collective_id=1, has_side_effects=True),
        cost_estimate=pl.CostEstimate(flops=30 << 30, bytes_accessed=8 << 20, transcendentals=0),
        name="entry",
    )(lengths, tokens, attn_gain, q_gain, k_gain, w_query, w_keyval, prefix_kv)


def attention_kernel(requests, split, length_ref, tenant_ref, piece_ref,
                     q_ref, own_ref, kv_ref, out_ref, best_ref, total_ref, accum_ref, slot_ref):
    block = pl.program_id(0)
    queries = q_ref[0]
    count = queries.shape[0]
    rows = own_ref.shape[0]
    size = own_ref.shape[1] // 2
    for j in range(kv_ref.shape[0]):
        slot_ref[piece_ref[j]] = j
    row = (lax.broadcasted_iota(jnp.int32, (count, 1), 0) & (BLOCK - 1)) + block * BLOCK
    col = lax.broadcasted_iota(jnp.int32, (1, rows), 1)
    row_request = jnp.zeros((count, 1), jnp.int32)
    col_request = jnp.zeros((1, rows), jnp.int32)
    ends = []
    for r in range(requests):
        ends.append(length_ref[0, r] + (ends[-1] if ends else 0))
        row_request += (row >= ends[r]).astype(jnp.int32)
        col_request += (col >= ends[r]).astype(jnp.int32)
    seen = (row_request == col_request) & (col <= row)
    own = own_ref[...]
    scores = jnp.where(seen, dot_nt(queries, own), NEG)
    best = jnp.max(scores, axis=1, keepdims=True)
    weights = jnp.where(seen, jnp.exp(scores - best), 0.0)
    best_ref[...] = best
    total_ref[...] = jnp.sum(weights, axis=1, keepdims=True)
    accum_ref[...] = dot(weights.astype(BF16), own)
    for r in range(requests):
        begin = ends[r] - length_ref[0, r]

        @pl.when((ends[r] > block * BLOCK) & (begin < block * BLOCK + BLOCK))
        def _():
            inside = row_request == r
            tenant = tenant_ref[0, r]

            def piece(index, carry):
                keyval = kv_ref[slot_ref[tenant * split + index]]
                part = dot_nt(queries, keyval)
                old = best_ref[...]
                new = jnp.where(inside, jnp.maximum(old, jnp.max(part, axis=1, keepdims=True)), old)
                keep = jnp.exp(old - new)
                piece_weights = jnp.exp(part - jnp.where(inside, new, -NEG))
                best_ref[...] = new
                total_ref[...] = total_ref[...] * keep + jnp.sum(piece_weights, axis=1, keepdims=True)
                accum_ref[...] = accum_ref[...] * keep + dot(piece_weights.astype(BF16), keyval)
                return carry

            lax.fori_loop(0, split, piece, 0)

    out = accum_ref[...] / total_ref[...]
    heads = [out[h * BLOCK:(h + 1) * BLOCK, size:] for h in range(count // BLOCK)]
    out_ref[...] = jnp.concatenate(heads, axis=1).astype(BF16)


def attention(lengths, tenants, prefix_piece, queries, own, pieces):
    blocks, count, width = queries.shape
    rows = own.shape[0]
    columns = count // BLOCK * width // 2
    return pl.pallas_call(
        functools.partial(attention_kernel, lengths.shape[1], pieces.shape[0] // TENANTS),
        grid=(blocks,),
        in_specs=[smem(), smem(), smem(),
                  pl.BlockSpec((1, count, width), lambda i: (i, 0, 0)),
                  pl.BlockSpec(own.shape, lambda i: (0, 0)),
                  pl.BlockSpec(pieces.shape, lambda i: (0, 0, 0), pipeline_mode=pl.Buffered(1))],
        out_specs=pl.BlockSpec((BLOCK, columns), lambda i: (i, 0)),
        out_shape=jax.ShapeDtypeStruct((rows, columns), BF16),
        scratch_shapes=[pltpu.VMEM((count, 1), F32), pltpu.VMEM((count, 1), F32),
                        pltpu.VMEM((count, width), F32), pltpu.SMEM((pieces.shape[0],), jnp.int32)],
        cost_estimate=pl.CostEstimate(flops=24 << 30, bytes_accessed=5 << 20, transcendentals=0),
        name="attention",
    )(lengths, tenants, prefix_piece, queries, own, pieces)


def layer_kernel(att_ref, tok_ref, gain_ref, wo_ref, wg_hbm, wu_hbm, wd_hbm, out_ref,
                 wg, wu, wd, stage, paired, inbox, stage2, paired2, inbox2, mid, normed, inner,
                 load, send, pair_sem, in_sem, send2, pair_sem2, in_sem2, gsend, grecv):
    width = tok_ref.shape[1]
    loads = [pltpu.make_async_copy(src, dst, load.at[i])
             for i, (src, dst) in enumerate(((wg_hbm, wg), (wu_hbm, wu), (wd_hbm, wd)))]
    for copy in loads:
        copy.start()
    greet(x_peers())

    def columns(index):
        return pl.ds(pl.multiple_of(index * width, width), width)

    att = att_ref[...]
    value = scatter_sum(lambda d: dot(att, wo_ref[:, columns(d)]),
                        stage, paired, inbox, send, pair_sem, in_sem)
    share = (tok_ref[...].astype(F32) + value).astype(BF16)
    gather = Gather(mid, gsend, grecv)
    mine = 2 * gather.x + gather.core
    mid[mine] = share
    gather.open()
    gather.relay()
    gather.close()
    normalise(mid, gain_ref, normed)
    loads[0].wait()
    loads[1].wait()
    for t in range(inner.shape[1] // width):
        tile = slice(t * width, (t + 1) * width)
        gate = dot(normed[...], wg[:, tile])
        upper = dot(normed[...], wu[:, tile])
        inner[:, tile] = (gate / (1.0 + jnp.exp(-gate)) * upper).astype(BF16)
    loads[2].wait()
    value = scatter_sum(lambda d: dot(inner[...], wd[:, columns(d)]),
                        stage2, paired2, inbox2, send2, pair_sem2, in_sem2)
    out_ref[...] = (mid[mine].astype(F32) + value).astype(BF16)
    gather.finish()


def layer(attended, tokens, mlp_gain, w_out, w_gate, w_up, w_down):
    rows, width = tokens.shape
    units = w_gate.shape[1]
    block = (rows, width)
    dma = pltpu.SemaphoreType.DMA

    def blocks(n):
        return pltpu.VMEM((n,) + block, BF16)

    return pl.pallas_call(
        layer_kernel,
        in_specs=[vmem()] * 4 + [hbm()] * 3,
        out_specs=vmem(),
        out_shape=jax.ShapeDtypeStruct(block, BF16),
        scratch_shapes=[pltpu.VMEM(w_gate.shape, BF16), pltpu.VMEM(w_up.shape, BF16),
                        pltpu.VMEM(w_down.shape, BF16),
                        blocks(7), blocks(4), blocks(3), blocks(7), blocks(4), blocks(3), blocks(8),
                        pltpu.VMEM((rows, 8 * width), BF16), pltpu.VMEM((rows, units), BF16),
                        dma((3,)), dma((7,)), dma((4,)), dma((3,)), dma((7,)), dma((4,)), dma((3,)),
                        dma((7,)), dma((8,))],
        compiler_params=pltpu.CompilerParams(collective_id=2, has_side_effects=True,
                                             vmem_limit_bytes=48 << 20),
        cost_estimate=pl.CostEstimate(flops=40 << 30, bytes_accessed=14 << 20, transcendentals=0),
        name="layer",
    )(attended, tokens, mlp_gain, w_out, w_gate, w_up, w_down)


def head_kernel(share_ref, gain_ref, target_ref, near_w, ahead_w, back_w, far_a, far_b, out_ref,
                weight, hidden, normed, logits, wanted, stat, stat_y, stat_m,
                load, gsend, grecv, ysend, yrecv, tsend, trecv, ssend, srecv, msend, mrecv):
    core = lax.axis_index("c")
    rows = share_ref.shape[0]
    vocab = weight.shape[1]
    depth = near_w.shape[0] // RING
    x, x_ahead, x_back, x_far = ring_of("x", core)
    y, y_ahead, y_back, y_far = ring_of("y", core)
    z = lax.axis_index("z")
    mine = 2 * x + core
    loads = []

    def fetch(src, row, from_z, shift):
        to = (from_z * RING + lax.rem(y + RING - shift, RING)) * depth
        copy = pltpu.make_async_copy(
            src.at[pl.ds(row, depth)], weight.at[pl.ds(pl.multiple_of(to, depth), depth)],
            load.at[len(loads)])
        copy.start()
        loads.append(copy)

    up, down, over = lax.rem(z + 1, RING), lax.rem(z + 3, RING), lax.rem(z + 2, RING)
    for s in range(RING):
        fetch(near_w, s * depth, z, s)
        fetch(ahead_w, s * depth, up, s)
        fetch(back_w, s * depth, down, s)
        fetch(far_a if s < 2 else far_b, (s % 2) * depth, over, s)

    others = [dict(x=lax.rem(x + i // 2, RING), c=lax.rem(core + i % 2, 2)) for i in range(1, 8)]
    greet([dict(y=y_ahead), dict(y=y_back), dict(y=y_far)] + others)
    sent = []

    def push(src, dst, sems, recv, **device):
        copy = remote(src, dst, sems, recv, **device)
        copy.start()
        sent.append(copy)

    gathers = {}

    def gather_of(index, group):
        gathers[index] = Gather(hidden.at[group], gsend.at[index], grecv.at[group])
        return gathers[index]

    first = gather_of(0, y)
    push(share_ref, hidden.at[y, mine], ysend.at[0], yrecv.at[0], y=y_ahead)
    push(share_ref, hidden.at[y, mine], ysend.at[1], yrecv.at[1], y=y_back)
    first.open(share_ref)
    for i, to in enumerate((y_ahead, y_back, y_far)):
        push(target_ref, wanted.at[y], tsend.at[i], trecv.at[i], y=to)
    hidden[y, mine] = share_ref[...]
    wanted[y] = target_ref[...]

    arrived(hidden.at[y_back, mine], yrecv.at[0])
    push(hidden.at[y_back, mine], hidden.at[y_back, mine], ysend.at[2], yrecv.at[2], y=y_ahead)
    arrived(hidden.at[y_ahead, mine], yrecv.at[1])
    y_down, y_up = lax.rem(y + 3, RING), lax.rem(y + 1, RING)
    gather_of(1, y_down).open()
    gather_of(2, y_up).open()
    first.relay()
    arrived(hidden.at[y_far, mine], yrecv.at[2])
    gather_of(3, y_far).open()
    first.close()
    for i, group in enumerate((y_back, y_ahead, y_far)):
        arrived(wanted.at[group], trecv.at[i])
    for copy in loads:
        copy.wait()

    tile = 512
    eye = (lax.broadcasted_iota(jnp.int32, (rows, rows), 0)
           == lax.broadcasted_iota(jnp.int32, (rows, rows), 1))
    start = (mine * RING + y) * vocab
    column = lax.broadcasted_iota(jnp.int32, (1, vocab), 1)

    def to_row(value):
        return jnp.sum(jnp.where(eye, value, 0.0), axis=0, keepdims=True)

    for index, group in enumerate((y, y_down, y_up, y_far)):
        if index:
            gathers[index].close()
        normalise(hidden.at[group], gain_ref, normed)
        if index < 3:
            gathers[index + 1].relay()
        for t in range(vocab // tile):
            logits[:, t * tile:(t + 1) * tile] = dot(normed[...], weight[:, t * tile:(t + 1) * tile])
        value = logits[...]
        top = jnp.max(value, axis=1, keepdims=True)
        total = jnp.sum(jnp.exp(value - top), axis=1, keepdims=True)
        target = jnp.sum(jnp.where(eye, wanted[group], 0), axis=1, keepdims=True)
        picked = jnp.sum(jnp.where(target - start == column, value, 0.0), axis=1, keepdims=True)
        stat[group, 0:1, :] = to_row(top)
        stat[group, 1:2, :] = to_row(total)
        stat[group, 2:3, :] = to_row(picked)
        if index:
            push(stat.at[group], stat_y.at[y], ssend.at[index - 1], srecv.at[y], y=group)

    stat_y[y] = stat[y]
    for group in (y_back, y_ahead, y_far):
        arrived(stat_y.at[group], srecv.at[group])

    def merge(parts, count):
        top = parts[0, 0:1, :]
        for i in range(1, count):
            top = jnp.maximum(top, parts[i, 0:1, :])
        total = jnp.zeros_like(top)
        picked = jnp.zeros_like(top)
        for i in range(count):
            total += parts[i, 1:2, :] * jnp.exp(parts[i, 0:1, :] - top)
            picked += parts[i, 2:3, :]
        return (top, total, picked)

    for i, value in enumerate(merge(stat_y, RING)):
        stat_m[mine, i:i + 1, :] = value
    for i, peer in enumerate(others):
        push(stat_m.at[mine], stat_m.at[mine], msend.at[i], mrecv.at[mine], **peer)
    for peer in others:
        slot = 2 * peer["x"] + peer["c"]
        arrived(stat_m.at[slot], mrecv.at[slot])
    top, total, picked = merge(stat_m, 8)
    out_ref[...] = picked - top - jnp.log(total)
    for gather in gathers.values():
        gather.finish()
    for copy in sent:
        copy.wait_send()


def head(share, final_gain, targets, slabs):
    rows, width = share.shape
    vocab = slabs[0].shape[1]
    dma = pltpu.SemaphoreType.DMA
    stats = (8, rows)
    return pl.pallas_call(
        head_kernel,
        in_specs=[vmem()] * 3 + [hbm()] * 5,
        out_specs=vmem(),
        out_shape=jax.ShapeDtypeStruct((1, rows), F32),
        scratch_shapes=[pltpu.VMEM((8 * width, vocab), BF16), pltpu.VMEM((RING, 8, rows, width), BF16),
                        pltpu.VMEM((rows, 8 * width), BF16), pltpu.VMEM((rows, vocab), F32),
                        pltpu.VMEM((RING, 1, rows), jnp.int32), pltpu.VMEM((RING,) + stats, F32),
                        pltpu.VMEM((RING,) + stats, F32), pltpu.VMEM((8,) + stats, F32),
                        dma((16,)), dma((4, 7)), dma((4, 8)), dma((3,)), dma((3,)), dma((3,)), dma((3,)),
                        dma((3,)), dma((4,)), dma((7,)), dma((8,))],
        compiler_params=pltpu.CompilerParams(collective_id=3, has_side_effects=True,
                                             vmem_limit_bytes=48 << 20),
        cost_estimate=pl.CostEstimate(flops=30 << 30, bytes_accessed=9 << 20, transcendentals=0),
        name="head",
    )(share, final_gain, targets, *slabs)


def spread_head(w_head):
    y = lax.axis_index("y")
    part = w_head.shape[1] // RING
    got = []
    for shift in range(RING):
        give = lax.dynamic_slice_in_dim(w_head, lax.rem(y + shift, RING) * part, part, 1)
        if shift:
            give = lax.ppermute(give, "y", [(i, (i + shift) % RING) for i in range(RING)])
        got.append(give)
    slab = jnp.concatenate(got, axis=0)
    up = [(i, (i + 1) % RING) for i in range(RING)]
    down = [(i, (i + 3) % RING) for i in range(RING)]
    back = lax.ppermute(slab, "z", up)
    ahead = lax.ppermute(slab, "z", down)
    middle = slab.shape[0] // 2
    far_a = lax.ppermute(back[:middle], "z", up)
    far_b = lax.ppermute(ahead[middle:], "z", down)
    return (slab, ahead, back, far_a, far_b)


def body(tokens, attn_gain, mlp_gain, final_gain, q_gain, k_gain, w_query, w_keyval, w_out, w_gate,
         w_up, w_down, w_head, targets, req_lengths, req_tenant, prefix_piece, prefix_kv):
    slabs = spread_head(w_head)
    queries, own, pieces = entry(req_lengths, tokens, attn_gain[None], q_gain[None], k_gain[None],
                                 w_query, w_keyval, prefix_kv)
    attended = attention(req_lengths, req_tenant, prefix_piece, queries, own, pieces)
    share = layer(attended, tokens, mlp_gain[None], w_out, w_gate, w_up, w_down)
    logprob = head(share, final_gain[None], targets[None], slabs)
    return (share, logprob[0])


def solution(mesh):
    req = ("z", "y")
    mlp = ("x", "c")
    in_specs = (
        P(req, mlp), P(), P(), P(), P(), P(), P(None, mlp), P(None, mlp), P(mlp, None),
        P(None, mlp), P(None, mlp), P(mlp, None), P(req, mlp), P(req), P(req, None), P(req, None),
        P(), P(req, None, mlp),
    )
    out_specs = (P(req, mlp), P(req))
    split = Mesh(mesh.devices.reshape(RING, RING, RING, 2), ("z", "y", "x", "c"))
    return jax.shard_map(body, mesh=split, in_specs=in_specs, out_specs=out_specs, check_vma=False)
```

time: 408 us -> 203 us (0.50)
  waiting for transfers between devices: 260 us -> 19.8 us
  Pallas kernels: 24.6 us -> 164 us
  blocking collectives: 45.6 us -> 0 us
  matrix products: 27.8 us -> 0 us
  other arithmetic: 18.5 us -> 1.37 us
  between operations: 14.6 us -> 0.81 us
  starting transfers between devices: 5.06 us -> 9.31 us
    all_gather x5 -> x0, waiting for transfers between devices: 178 us -> none  [the longest x1 82.1 us: spread_head(): return lax.all_gather(slab, 'z', axis=0, tiled=True)]
    pallas_call x1 -> x4, Pallas kernels: 24.6 us -> 164 us  [the longest x1 50.6 us: entry(): pl.pallas_call(functools.partial(entry_kernel, lengths.shape[1], size **...]
    reduce_scatter x2 -> x0, waiting for transfers between devices: 61.8 us -> none  [the longest x1 32 us: body(): lax.psum_scatter(attn_proj.astype(jnp.bfloat16), 'mlp', scatter_dimension...]
    all_gather x3 -> x0, blocking collectives: 45.6 us -> none  [the longest x1 25.3 us: body(): every = lax.all_gather(stats, ('y', 'mlp'), axis=0)]
    dot_general x6 -> x0, matrix products: 27.8 us -> none  [the longest x1 12.8 us: body(): logits = jnp.dot(normed_out, head, preferred_element_type=jnp.float32)]
    reduce_sum x9 -> x0, other arithmetic: 10.4 us -> none  [the longest x4 6.28 us: rms_norm(): jnp.mean(values * values, axis=-1, keepdims=True) + EPS]
    ppermute x3 -> x7, starting transfers between devices: 4.78 us -> 9.31 us  [the longest x3 4.67 us: spread_head(): lax.ppermute(give, 'y', [(i, (i + shift) % RING) for i in range(RING)])]
    ppermute x3 -> x7, waiting for transfers between devices: 18.8 us -> 19.8 us  [the longest x1 19.8 us: spread_head(): back = lax.ppermute(slab, 'z', up)]
  transfers between devices with their start and end apart: 10 -> 7, of which waited for: 9 -> 1; matrix products, arithmetic and copies ran while one was open for 5% -> 1% of each run, Pallas kernels for 0% -> 57%
where the time goes in v2:
time: 203 us; the launch traced here: 202 us
  Pallas kernels  164 us (81%)
  waiting for transfers between devices  19.8 us (10%)
  starting transfers between devices  9.31 us (5%)
  local copies, waits for them, and re-layouts  7.24 us (4%)
    pallas_call x1, Pallas kernels, entry(): pl.pallas_call(functools.partial(entry_kernel, lengths.shape[1], size **...  50.6 us
    pallas_call x1, Pallas kernels, head(): pl.pallas_call(head_kernel, in_specs=[vmem()] * 3 + [hbm()] * 5, out_spec...  48.7 us
    pallas_call x1, Pallas kernels, layer(): pl.pallas_call(layer_kernel, in_specs=[vmem()] * 4 + [hbm()] * 3, out_spe...  36.4 us
    pallas_call x1, Pallas kernels, attention(): pl.pallas_call(functools.partial(attention_kernel, lengths.shape[1], piec...  28.1 us
    ppermute x1, waiting for transfers between devices, spread_head(): back = lax.ppermute(slab, 'z', up)  19.8 us
    ppermute x3, starting transfers between devices, spread_head(): lax.ppermute(give, 'y', [(i, (i + shift) % RING) for i in range(RING)])  4.67 us
  transfers between devices with their start and end apart: 7, of which 1 were waited for; matrix products, arithmetic and copies ran while one was open for 1% of the time, Pallas kernels for 57%

profile of v2, /device:TPU:1, one launch (start us, length us, event | category | flops | bytes accessed | tf_op | source)
XLA Modules:
  0.0 202.4 jit_solution(17992959097339241164)
XLA Ops:
  0.7 1.7 constant_dynamic-slice_fusion.3
  2.3 3.6 %collective-permute-start.2 = (bf16[128,2048]{1,0:T(8,128)(2,1)S(1)}, bf16[128,2048]{1,0:T(8,128)(2,1)S(1)}, u32[]{:S(2)}, u32[]{:S(2)}) collective-permute-start(bf16[128,2048]{1,0:T(8,128)(2,1)S(1)} %get-tuple-element.10), channel_id=1, source_target_pairs={{0,24},{8,0},{16,8},{24,16},{1,25},{9,1},{17,9},{25,17},{2,26},{10... | collective-permute-start | bytes 1572872 | tf_op jit(solution)/shard_map/ppermute | solution.py:598
  6.0 0.3 collective-permute-start.1
  6.3 0.7 collective-permute-start
  7.0 50.6 %entry.1 = (bf16[4,256,128]{2,1,0:T(8,128)(2,1)}, bf16[256,128]{1,0:T(8,128)(2,1)}, bf16[16,1024,128]{2,1,0:T(8,128)(2,1)}) custom-call(s32[1,4]{1,0:T(1,128)} %length_ref.3, bf16[256,256]{1,0:T(8,128)(2,1)} %tok_ref.3, f32[1,2048]{1,0:T(1,128)} %bitcast.11, f32[1,64]{1,0:T(1,128)} %bitcast.12, f32[1,64]{1,0:T(1,128)} %bitcast.13, bf16[2048,256]{1,0:T(8,128)(2,1)} %wq_ref.1, ...), custom_call_target="tpu_custom_call" | custom-call | flops 32212254720 | bytes 8388608 | tf_op jit(solution)/shard_map/entry/pallas_call | solution.py:288
  57.6 0.0 collective-permute-done.2
  57.7 0.0 collective-permute-done.1
  57.7 0.0 copy-start.7
  57.7 0.0 collective-permute-done
  57.7 0.8 copy-done.7
  58.5 1.4 pad_maximum_fusion.near_w
  59.8 1.7 collective-permute-start.3
  61.5 0.0 collective-permute-start.4
  61.5 0.0 copy-start.1
  61.5 0.0 copy-start.2
  61.5 0.0 copy-start.3
  61.5 28.1 %attention.1.att_ref = bf16[256,256]{1,0:T(8,128)(2,1)} custom-call(s32[1,4]{1,0:T(1,128)} %length_ref.3, s32[1,4]{1,0:T(1,128)} %tenant_ref.1, s32[16]{0:T(128)} %piece_ref.1, bf16[4,256,128]{2,1,0:T(8,128)(2,1)} %get-tuple-element.5.q_ref, bf16[256,128]{1,0:T(8,128)(2,1)} %get-tuple-element.6.own_ref, bf16[16,1024,128]{2,1,0:T(8,128)(2,1)} %get-tuple-element.7.kv_ref), custom_call_target="tpu_custom_call" | custom-call | flops 25769803776 | bytes 5242880 | tf_op jit(solution)/shard_map/attention/pallas_call | solution.py:362
  89.7 0.0 copy-start
  89.7 19.8 %collective-permute-done.4.back_w = bf16[512,2048]{1,0:T(8,128)(2,1)} collective-permute-done((bf16[512,2048]{1,0:T(8,128)(2,1)S(1)}, bf16[512,2048]{1,0:T(8,128)(2,1)}, u32[]{:S(2)}, u32[]{:S(2)}) %collective-permute-start.4) | collective-permute-done | bytes 2097184 | tf_op jit(solution)/shard_map/ppermute | solution.py:603
  109.5 1.3 slice.8
  110.8 0.1 collective-permute-start.5
  110.9 0.0 collective-permute-done.3.ahead_w
  110.9 1.3 slice.9
  112.2 2.9 %collective-permute-start.6 = (bf16[256,2048]{1,0:T(8,128)(2,1)S(1)}, bf16[256,2048]{1,0:T(8,128)(2,1)S(1)}, u32[]{:S(2)}, u32[]{:S(2)}) collective-permute-start(bf16[256,2048]{1,0:T(8,128)(2,1)S(1)} %slice.9), channel_id=1, source_target_pairs={{0,96},{32,0},{64,32},{96,64},{1,97},{33,1},{65,33},{97,65},{2,98}... | collective-permute-start | bytes 3145736 | tf_op jit(solution)/shard_map/ppermute | solution.py:607
  115.1 0.0 copy-done.1
  115.1 0.0 copy-done.2
  115.1 0.0 copy-done.3
  115.1 0.0 copy-done
  115.1 0.0 copy-start.6
  115.2 0.9 copy-done.6
  116.0 0.0 copy-start.4
  116.1 0.0 copy-start.5
  116.1 36.4 %layer.1.share_ref = bf16[256,256]{1,0:T(8,128)(2,1)S(1)} custom-call(bf16[256,256]{1,0:T(8,128)(2,1)S(1)} %copy-done.6, bf16[256,256]{1,0:T(8,128)(2,1)S(1)} %copy-done.2, f32[1,2048]{1,0:T(1,128)S(1)} %bitcast.8, bf16[256,2048]{1,0:T(8,128)(2,1)S(1)} %copy-done.1, bf16[2048,1024]{1,0:T(8,128)(2,1)S(1)} %copy-done, bf16[2048,1024]{1,0:T(8,128)(2,1)} %wu_hbm.1, ...), custom_call_target="tpu_custom_call" | custom-call | flops 42949672960 | bytes 14680064 | tf_op jit(solution)/shard_map/layer/pallas_call | solution.py:425
  152.4 0.0 collective-permute-done.5.far_a
  152.4 0.0 collective-permute-done.6.far_b
  152.5 0.0 copy-done.4
  152.5 0.0 copy-done.5
  152.5 48.7 %head.1 = f32[1,256]{1,0:T(1,128)S(1)} custom-call(bf16[256,256]{1,0:T(8,128)(2,1)S(1)} %layer.1.share_ref, f32[1,2048]{1,0:T(1,128)S(1)} %bitcast.9, s32[1,256]{1,0:T(1,128)S(1)} %bitcast.10, bf16[512,2048]{1,0:T(8,128)(2,1)S(1)} %pad_maximum_fusion.near_w, bf16[512,2048]{1,0:T(8,128)(2,1)} %collective-permute-done.3.ahead_w, ...), custom_call_target="tpu_custom_call" | custom-call | flops 32212254720 | bytes 9437184 | tf_op jit(solution)/shard_map/head/pallas_call | solution.py:573
  201.2 0.7 copy.22
  201.8 0.6 copy.23
Async XLA Ops:
  2.3 55.3 %collective-permute-start.2 = (bf16[128,2048]{1,0:T(8,128)(2,1)S(1)}, bf16[128,2048]{1,0:T(8,128)(2,1)S(1)}, u32[]{:S(2)}, u32[]{:S(2)}) collective-permute-start(bf16[128,2048]{1,0:T(8,128)(2,1)S(1)} %get-tuple-element.10), channel_id=1, source_target_pairs={{0,24},{8,0},{16,8},{24,16},{1,25},{9,1},{17,9},{25,17},{2,26},{10... | collective-permute-start | bytes 1572872 | tf_op jit(solution)/shard_map/ppermute | solution.py:598
  6.0 51.7 %collective-permute-start.1 = (bf16[128,2048]{1,0:T(8,128)(2,1)S(1)}, bf16[128,2048]{1,0:T(8,128)(2,1)S(1)}, u32[]{:S(2)}, u32[]{:S(2)}) collective-permute-start(bf16[128,2048]{1,0:T(8,128)(2,1)S(1)} %get-tuple-element.11), channel_id=1, source_target_pairs={{0,16},{8,24},{16,0},{24,8},{1,17},{9,25},{17,1},{25,9},{2,18},{10... | collective-permute-start | bytes 1572872 | tf_op jit(solution)/shard_map/ppermute | solution.py:598
  6.3 51.4 %collective-permute-start = (bf16[128,2048]{1,0:T(8,128)(2,1)S(1)}, bf16[128,2048]{1,0:T(8,128)(2,1)}, u32[]{:S(2)}, u32[]{:S(2)}) collective-permute-start(bf16[128,2048]{1,0:T(8,128)(2,1)S(1)} %get-tuple-element.9), channel_id=1, source_target_pairs={{0,8},{8,16},{16,24},{24,0},{1,9},{9,17},{17,25},{25,1},{2,10},{10... | collective-permute-start | bytes 1572872 | tf_op jit(solution)/shard_map/ppermute | solution.py:598
  57.7 0.8 copy-start.7
  59.8 51.0 %collective-permute-start.3 = (bf16[512,2048]{1,0:T(8,128)(2,1)S(1)}, bf16[512,2048]{1,0:T(8,128)(2,1)}, u32[]{:S(2)}, u32[]{:S(2)}) collective-permute-start(bf16[512,2048]{1,0:T(8,128)(2,1)S(1)} %pad_maximum_fusion.near_w), channel_id=1, source_target_pairs={{0,96},{32,0},{64,32},{96,64},{1,97},{33,1},{65,33},{97,65},{2,98}... | collective-permute-start | bytes 6291464 | tf_op jit(solution)/shard_map/ppermute | solution.py:604
  61.5 48.0 %collective-permute-start.4 = (bf16[512,2048]{1,0:T(8,128)(2,1)S(1)}, bf16[512,2048]{1,0:T(8,128)(2,1)}, u32[]{:S(2)}, u32[]{:S(2)}) collective-permute-start(bf16[512,2048]{1,0:T(8,128)(2,1)S(1)} %pad_maximum_fusion.near_w), channel_id=1, source_target_pairs={{0,32},{32,64},{64,96},{96,0},{1,33},{33,65},{65,97},{97,1},{2,34}... | collective-permute-start | bytes 6291464 | tf_op jit(solution)/shard_map/ppermute | solution.py:603
  61.5 53.6 %copy-start.1 = (bf16[256,2048]{1,0:T(8,128)(2,1)S(1)}, bf16[256,2048]{1,0:T(8,128)(2,1)}, u32[]{:S(2)}) copy-start(bf16[256,2048]{1,0:T(8,128)(2,1)} %wo_ref.1) | copy-start | bytes 3145732
  61.5 53.6 %copy-start.2 = (bf16[256,256]{1,0:T(8,128)(2,1)S(1)}, bf16[256,256]{1,0:T(8,128)(2,1)}, u32[]{:S(2)}) copy-start(bf16[256,256]{1,0:T(8,128)(2,1)} %tok_ref.3) | copy-start | bytes 393220
  61.5 53.6 %copy-start.3 = (f32[2048]{0:T(1024)S(1)}, f32[2048]{0:T(1024)}, u32[]{:S(2)}) copy-start(f32[2048]{0:T(1024)} %param.20) | copy-start | bytes 24580
  89.7 25.5 %copy-start = (bf16[2048,1024]{1,0:T(8,128)(2,1)S(1)}, bf16[2048,1024]{1,0:T(8,128)(2,1)}, u32[]{:S(2)}) copy-start(bf16[2048,1024]{1,0:T(8,128)(2,1)} %wg_hbm.1) | copy-start | bytes 12582916
  110.8 41.6 %collective-permute-start.5 = (bf16[256,2048]{1,0:T(8,128)(2,1)S(1)}, bf16[256,2048]{1,0:T(8,128)(2,1)S(1)}, u32[]{:S(2)}, u32[]{:S(2)}) collective-permute-start(bf16[256,2048]{1,0:T(8,128)(2,1)S(1)} %slice.8), channel_id=1, source_target_pairs={{0,32},{32,64},{64,96},{96,0},{1,33},{33,65},{65,97},{97,1},{2,34}... | collective-permute-start | bytes 3145736 | tf_op jit(solution)/shard_map/ppermute | solution.py:606
  112.2 40.2 %collective-permute-start.6 = (bf16[256,2048]{1,0:T(8,128)(2,1)S(1)}, bf16[256,2048]{1,0:T(8,128)(2,1)S(1)}, u32[]{:S(2)}, u32[]{:S(2)}) collective-permute-start(bf16[256,2048]{1,0:T(8,128)(2,1)S(1)} %slice.9), channel_id=1, source_target_pairs={{0,96},{32,0},{64,32},{96,64},{1,97},{33,1},{65,33},{97,65},{2,98}... | collective-permute-start | bytes 3145736 | tf_op jit(solution)/shard_map/ppermute | solution.py:607
  115.1 0.9 copy-start.6
  116.0 36.4 %copy-start.4 = (f32[2048]{0:T(1024)S(1)}, f32[2048]{0:T(1024)}, u32[]{:S(2)}) copy-start(f32[2048]{0:T(1024)} %param.21) | copy-start | bytes 24580
  116.1 36.4 %copy-start.5 = (s32[256]{0:T(256)S(1)}, s32[256]{0:T(256)}, u32[]{:S(2)}) copy-start(s32[256]{0:T(256)} %param.31) | copy-start | bytes 3076

commit v3 on v2

--- a/solution.py
+++ b/solution.py
@@ -147,8 +147,8 @@
 
 
 def entry_kernel(requests, scale, length_ref, tok_ref, gain_ref, qgain_ref, kgain_ref, wq_ref,
-                 wkv_ref, prefix_ref, q_out, own_out, pieces, stream, normed, send, recv,
-                 psend, precv, local_sem):
+                 wkv_ref, prefix_ref, head_ref, q_out, own_out, pieces, head_out, passing, stream,
+                 normed, send, recv, psend, precv, wsend, wrecv, local_sem):
     core = lax.axis_index("c")
     rows = tok_ref.shape[0]
     size = qgain_ref.shape[1]
@@ -183,6 +183,26 @@
     push(0, z, y, first[0], z=z_back)
     push(1, z, y, first[1], y=y_ahead)
     push(1, z, y, first[1], y=y_back)
+
+    given = []
+    part_words = head_out.shape[2]
+
+    def words(index):
+        return head_ref.at[:, pl.ds(pl.multiple_of(index * part_words, part_words), part_words)]
+
+    def piece(pz, py):
+        return head_out.at[pz * RING + py]
+
+    def give(index, src, dst, **device):
+        copy = remote(src, dst, wsend.at[index], wrecv.at[index], **device)
+        copy.start()
+        given.append(copy)
+
+    give(2, words(y_far), passing, y=y_ahead)
+    give(4, words(y), piece(z, y), z=z_ahead)
+    give(5, words(y), piece(z, y), z=z_back)
+    give(0, words(y_ahead), piece(z, y), y=y_ahead)
+    give(1, words(y_back), piece(z, y), y=y_back)
     keep = [pltpu.make_async_copy(prefix_ref.at[0], pieces.at[z * RING + y], local_sem.at[0]),
             pltpu.make_async_copy(tok_ref, stream.at[2 * gather.x + core], local_sem.at[1])]
     for copy in keep:
@@ -241,6 +261,11 @@
         wait(1, pz, come)
         push(1, pz, come, y=go)
 
+    arrived(passing, wrecv.at[2])
+    give(3, passing, piece(z, y_back), y=y_ahead)
+    arrived(piece(z_back, y), wrecv.at[4])
+    give(6, piece(z_back, y), piece(z_back, y), z=z_ahead)
+
     query = dot(normed[...], wq_ref[...])
     keyval = dot(normed[...], wkv_ref[...])
     heads = query.shape[1] // size
@@ -262,9 +287,14 @@
         wait(0, z_far, py)
     for pz, come, go in far_y:
         wait(1, pz, y_far)
+    arrived(piece(z, y_back), wrecv.at[0])
+    arrived(piece(z, y_ahead), wrecv.at[1])
+    arrived(piece(z, y_far), wrecv.at[3])
+    arrived(piece(z_ahead, y), wrecv.at[5])
+    arrived(piece(z_far, y), wrecv.at[6])
     keep[0].wait()
     gather.finish()
-    for copy in sent:
+    for copy in sent + given:
         copy.wait_send()
 
 
@@ -280,26 +310,30 @@
     return pl.BlockSpec(memory_space=pltpu.SMEM)
 
 
-def entry(lengths, tokens, attn_gain, q_gain, k_gain, w_query, w_keyval, prefix_kv):
+def entry(lengths, tokens, attn_gain, q_gain, k_gain, w_query, w_keyval, prefix_kv, w_head):
     rows, width = tokens.shape
     size = q_gain.shape[1]
     heads = w_query.shape[1] // size
     count = RING * RING
+    quarter = (w_head.shape[0], w_head.shape[1] // RING)
     return pl.pallas_call(
         functools.partial(entry_kernel, lengths.shape[1], size ** (-0.5)),
-        in_specs=[smem()] + [vmem()] * 7,
-        out_specs=[vmem(), vmem(), hbm()],
+        in_specs=[smem()] + [vmem()] * 7 + [hbm()],
+        out_specs=[vmem(), vmem(), hbm(), hbm(), hbm()],
         out_shape=[jax.ShapeDtypeStruct((rows // BLOCK, heads * BLOCK, 2 * size), BF16),
                    jax.ShapeDtypeStruct((rows, 2 * size), BF16),
-                   jax.ShapeDtypeStruct((count,) + prefix_kv.shape[1:], BF16)],
+                   jax.ShapeDtypeStruct((count,) + prefix_kv.shape[1:], BF16),
+                   jax.ShapeDtypeStruct((count,) + quarter, BF16),
+                   jax.ShapeDtypeStruct(quarter, BF16)],
         scratch_shapes=[pltpu.VMEM((8, rows, width), BF16), pltpu.VMEM((rows, 8 * width), BF16),
                         pltpu.SemaphoreType.DMA((7,)), pltpu.SemaphoreType.DMA((8,)),
                         pltpu.SemaphoreType.DMA((30,)), pltpu.SemaphoreType.DMA((2, count)),
+                        pltpu.SemaphoreType.DMA((7,)), pltpu.SemaphoreType.DMA((7,)),
                         pltpu.SemaphoreType.DMA((2,))],
         compiler_params=pltpu.CompilerParams(collective_id=1, has_side_effects=True),
         cost_estimate=pl.CostEstimate(flops=30 << 30, bytes_accessed=8 << 20, transcendentals=0),
         name="entry",
-    )(lengths, tokens, attn_gain, q_gain, k_gain, w_query, w_keyval, prefix_kv)
+    )(lengths, tokens, attn_gain, q_gain, k_gain, w_query, w_keyval, prefix_kv, w_head)
 
 
 def attention_kernel(requests, split, length_ref, tenant_ref, piece_ref,
@@ -375,29 +409,72 @@
     )(lengths, tenants, prefix_piece, queries, own, pieces)
 
 
-def layer_kernel(att_ref, tok_ref, gain_ref, wo_ref, wg_hbm, wu_hbm, wd_hbm, out_ref,
-                 wg, wu, wd, stage, paired, inbox, stage2, paired2, inbox2, mid, normed, inner,
-                 load, send, pair_sem, in_sem, send2, pair_sem2, in_sem2, gsend, grecv):
-    width = tok_ref.shape[1]
-    loads = [pltpu.make_async_copy(src, dst, load.at[i])
-             for i, (src, dst) in enumerate(((wg_hbm, wg), (wu_hbm, wu), (wd_hbm, wd)))]
-    for copy in loads:
+def finish_kernel(att_ref, tok_ref, gain_ref, wo_ref, last_gain_ref, target_ref, wg_hbm, wu_hbm, wd_hbm,
+                  head_hbm, pieces_hbm, out_ref, log_ref,
+                  wg, wu, wd, stage, paired, inbox, stage2, paired2, inbox2, mid, normed, inner,
+                  weight, hidden, logits, wanted, stat, stat_y, stat_m,
+                  load, send, pair_sem, in_sem, send2, pair_sem2, in_sem2, msend, mrecv,
+                  gsend, grecv, ysend, yrecv, tsend, trecv, ssend, srecv, ksend, krecv,
+                  zsend, zrecv):
+    core = lax.axis_index("c")
+    rows, width = tok_ref.shape
+    depth, vocab = pieces_hbm.shape[1:]
+    x, x_ahead, x_back, x_far = ring_of("x", core)
+    y, y_ahead, y_back, y_far = ring_of("y", core)
+    z, z_ahead, z_back, z_far = ring_of("z", core)
+    mine = 2 * x + core
+    sent = []
+
+    def push(src, dst, send_sem, recv_sem, **device):
+        copy = remote(src, dst, send_sem, recv_sem, **device)
         copy.start()
-    greet(x_peers())
-
-    def columns(index):
-        return pl.ds(pl.multiple_of(index * width, width), width)
+        sent.append(copy)
+
+    def columns(index, count):
+        return pl.ds(pl.multiple_of(index * count, count), count)
+
+    def place(pz, py):
+        return weight.at[columns(pz * RING + py, depth)]
+
+    loads = []
+
+    def fetch(src, dst):
+        copy = pltpu.make_async_copy(src, dst, load.at[len(loads)])
+        copy.start()
+        loads.append(copy)
+
+    fetch(wg_hbm, wg)
+    fetch(wu_hbm, wu)
+    fetch(wd_hbm, wd)
+    fetch(head_hbm.at[:, columns(y, vocab)], place(z, y))
+    for pz in (z_ahead, z_back, z_far):
+        fetch(pieces_hbm.at[pz * RING + y], place(pz, y))
+    rest = (y_back, y_ahead, y_far)
+    for py in rest:
+        fetch(pieces_hbm.at[z * RING + py], place(z, py))
+    others = [dict(x=lax.rem(x + i // 2, RING), c=lax.rem(core + i % 2, 2)) for i in range(1, 8)]
+    greet([dict(y=y_ahead), dict(y=y_back), dict(y=y_far), dict(z=z_ahead), dict(z=z_back)] + others)
+
+    for i, py in enumerate(rest):
+        source = pieces_hbm.at[z * RING + py]
+        push(source, place(z, py), zsend.at[i, 0], zrecv.at[i, 0], z=z_ahead)
+        push(source, place(z, py), zsend.at[i, 1], zrecv.at[i, 1], z=z_back)
+    for i, to in enumerate((y_ahead, y_back, y_far)):
+        push(target_ref, wanted.at[y], tsend.at[i], trecv.at[i], y=to)
+    wanted[y] = target_ref[...]
+
+    def head_relay(i):
+        arrived(place(z_back, rest[i]), zrecv.at[i, 0])
+        push(place(z_back, rest[i]), place(z_back, rest[i]), zsend.at[i, 2], zrecv.at[i, 2], z=z_ahead)
 
     att = att_ref[...]
-    value = scatter_sum(lambda d: dot(att, wo_ref[:, columns(d)]),
+    value = scatter_sum(lambda d: dot(att, wo_ref[:, columns(d, width)]),
                         stage, paired, inbox, send, pair_sem, in_sem)
-    share = (tok_ref[...].astype(F32) + value).astype(BF16)
-    gather = Gather(mid, gsend, grecv)
-    mine = 2 * gather.x + gather.core
-    mid[mine] = share
-    gather.open()
-    gather.relay()
-    gather.close()
+    middle = Gather(mid, msend, mrecv)
+    mid[mine] = (tok_ref[...].astype(F32) + value).astype(BF16)
+    middle.open()
+    middle.relay()
+    middle.close()
     normalise(mid, gain_ref, normed)
     loads[0].wait()
     loads[1].wait()
@@ -407,75 +484,12 @@
         upper = dot(normed[...], wu[:, tile])
         inner[:, tile] = (gate / (1.0 + jnp.exp(-gate)) * upper).astype(BF16)
     loads[2].wait()
-    value = scatter_sum(lambda d: dot(inner[...], wd[:, columns(d)]),
+    head_relay(0)
+    value = scatter_sum(lambda d: dot(inner[...], wd[:, columns(d, width)]),
                         stage2, paired2, inbox2, send2, pair_sem2, in_sem2)
-    out_ref[...] = (mid[mine].astype(F32) + value).astype(BF16)
-    gather.finish()
-
-
-def layer(attended, tokens, mlp_gain, w_out, w_gate, w_up, w_down):
-    rows, width = tokens.shape
-    units = w_gate.shape[1]
-    block = (rows, width)
-    dma = pltpu.SemaphoreType.DMA
-
-    def blocks(n):
-        return pltpu.VMEM((n,) + block, BF16)
-
-    return pl.pallas_call(
-        layer_kernel,
-        in_specs=[vmem()] * 4 + [hbm()] * 3,
-        out_specs=vmem(),
-        out_shape=jax.ShapeDtypeStruct(block, BF16),
-        scratch_shapes=[pltpu.VMEM(w_gate.shape, BF16), pltpu.VMEM(w_up.shape, BF16),
-                        pltpu.VMEM(w_down.shape, BF16),
-                        blocks(7), blocks(4), blocks(3), blocks(7), blocks(4), blocks(3), blocks(8),
-                        pltpu.VMEM((rows, 8 * width), BF16), pltpu.VMEM((rows, units), BF16),
-                        dma((3,)), dma((7,)), dma((4,)), dma((3,)), dma((7,)), dma((4,)), dma((3,)),
-                        dma((7,)), dma((8,))],
-        compiler_params=pltpu.CompilerParams(collective_id=2, has_side_effects=True,
-                                             vmem_limit_bytes=48 << 20),
-        cost_estimate=pl.CostEstimate(flops=40 << 30, bytes_accessed=14 << 20, transcendentals=0),
-        name="layer",
-    )(attended, tokens, mlp_gain, w_out, w_gate, w_up, w_down)
-
-
-def head_kernel(share_ref, gain_ref, target_ref, near_w, ahead_w, back_w, far_a, far_b, out_ref,
-                weight, hidden, normed, logits, wanted, stat, stat_y, stat_m,
-                load, gsend, grecv, ysend, yrecv, tsend, trecv, ssend, srecv, msend, mrecv):
-    core = lax.axis_index("c")
-    rows = share_ref.shape[0]
-    vocab = weight.shape[1]
-    depth = near_w.shape[0] // RING
-    x, x_ahead, x_back, x_far = ring_of("x", core)
-    y, y_ahead, y_back, y_far = ring_of("y", core)
-    z = lax.axis_index("z")
-    mine = 2 * x + core
-    loads = []
-
-    def fetch(src, row, from_z, shift):
-        to = (from_z * RING + lax.rem(y + RING - shift, RING)) * depth
-        copy = pltpu.make_async_copy(
-            src.at[pl.ds(row, depth)], weight.at[pl.ds(pl.multiple_of(to, depth), depth)],
-            load.at[len(loads)])
-        copy.start()
-        loads.append(copy)
-
-    up, down, over = lax.rem(z + 1, RING), lax.rem(z + 3, RING), lax.rem(z + 2, RING)
-    for s in range(RING):
-        fetch(near_w, s * depth, z, s)
-        fetch(ahead_w, s * depth, up, s)
-        fetch(back_w, s * depth, down, s)
-        fetch(far_a if s < 2 else far_b, (s % 2) * depth, over, s)
-
-    others = [dict(x=lax.rem(x + i // 2, RING), c=lax.rem(core + i % 2, 2)) for i in range(1, 8)]
-    greet([dict(y=y_ahead), dict(y=y_back), dict(y=y_far)] + others)
-    sent = []
-
-    def push(src, dst, sems, recv, **device):
-        copy = remote(src, dst, sems, recv, **device)
-        copy.start()
-        sent.append(copy)
+    share = (mid[mine].astype(F32) + value).astype(BF16)
+    out_ref[...] = share
+    hidden[y, mine] = share
 
     gathers = {}
 
@@ -483,14 +497,12 @@
         gathers[index] = Gather(hidden.at[group], gsend.at[index], grecv.at[group])
         return gathers[index]
 
+    own = hidden.at[y, mine]
     first = gather_of(0, y)
-    push(share_ref, hidden.at[y, mine], ysend.at[0], yrecv.at[0], y=y_ahead)
-    push(share_ref, hidden.at[y, mine], ysend.at[1], yrecv.at[1], y=y_back)
-    first.open(share_ref)
-    for i, to in enumerate((y_ahead, y_back, y_far)):
-        push(target_ref, wanted.at[y], tsend.at[i], trecv.at[i], y=to)
-    hidden[y, mine] = share_ref[...]
-    wanted[y] = target_ref[...]
+    push(own, own, ysend.at[0], yrecv.at[0], y=y_ahead)
+    push(own, own, ysend.at[1], yrecv.at[1], y=y_back)
+    first.open()
+    head_relay(1)
 
     arrived(hidden.at[y_back, mine], yrecv.at[0])
     push(hidden.at[y_back, mine], hidden.at[y_back, mine], ysend.at[2], yrecv.at[2], y=y_ahead)
@@ -501,11 +513,15 @@
     first.relay()
     arrived(hidden.at[y_far, mine], yrecv.at[2])
     gather_of(3, y_far).open()
+    head_relay(2)
     first.close()
     for i, group in enumerate((y_back, y_ahead, y_far)):
         arrived(wanted.at[group], trecv.at[i])
-    for copy in loads:
+    for copy in loads[3:]:
         copy.wait()
+    for i, py in enumerate(rest):
+        arrived(place(z_ahead, py), zrecv.at[i, 1])
+        arrived(place(z_far, py), zrecv.at[i, 2])
 
     tile = 512
     eye = (lax.broadcasted_iota(jnp.int32, (rows, rows), 0)
@@ -519,7 +535,7 @@
     for index, group in enumerate((y, y_down, y_up, y_far)):
         if index:
             gathers[index].close()
-        normalise(hidden.at[group], gain_ref, normed)
+        normalise(hidden.at[group], last_gain_ref, normed)
         if index < 3:
             gathers[index + 1].relay()
         for t in range(vocab // tile):
@@ -553,69 +569,62 @@
     for i, value in enumerate(merge(stat_y, RING)):
         stat_m[mine, i:i + 1, :] = value
     for i, peer in enumerate(others):
-        push(stat_m.at[mine], stat_m.at[mine], msend.at[i], mrecv.at[mine], **peer)
+        push(stat_m.at[mine], stat_m.at[mine], ksend.at[i], krecv.at[mine], **peer)
     for peer in others:
         slot = 2 * peer["x"] + peer["c"]
-        arrived(stat_m.at[slot], mrecv.at[slot])
+        arrived(stat_m.at[slot], krecv.at[slot])
     top, total, picked = merge(stat_m, 8)
-    out_ref[...] = picked - top - jnp.log(total)
+    log_ref[...] = picked - top - jnp.log(total)
+    middle.finish()
     for gather in gathers.values():
         gather.finish()
     for copy in sent:
         copy.wait_send()
 
 
-def head(share, final_gain, targets, slabs):
-    rows, width = share.shape
-    vocab = slabs[0].shape[1]
+def finish(attended, tokens, mlp_gain, w_out, final_gain, targets, w_gate, w_up, w_down, w_head, pieces):
+    rows, width = tokens.shape
+    units = w_gate.shape[1]
+    block = (rows, width)
+    vocab = pieces.shape[2]
     dma = pltpu.SemaphoreType.DMA
     stats = (8, rows)
+
+    def blocks(n):
+        return pltpu.VMEM((n,) + block, BF16)
+
     return pl.pallas_call(
-        head_kernel,
-        in_specs=[vmem()] * 3 + [hbm()] * 5,
-        out_specs=vmem(),
-        out_shape=jax.ShapeDtypeStruct((1, rows), F32),
-        scratch_shapes=[pltpu.VMEM((8 * width, vocab), BF16), pltpu.VMEM((RING, 8, rows, width), BF16),
-                        pltpu.VMEM((rows, 8 * width), BF16), pltpu.VMEM((rows, vocab), F32),
+        finish_kernel,
+        in_specs=[vmem()] * 6 + [hbm()] * 5,
+        out_specs=[vmem(), vmem()],
+        out_shape=[jax.ShapeDtypeStruct(block, BF16), jax.ShapeDtypeStruct((1, rows), F32)],
+        scratch_shapes=[pltpu.VMEM(w_gate.shape, BF16), pltpu.VMEM(w_up.shape, BF16),
+                        pltpu.VMEM(w_down.shape, BF16),
+                        blocks(7), blocks(4), blocks(3), blocks(7), blocks(4), blocks(3), blocks(8),
+                        pltpu.VMEM((rows, 8 * width), BF16), pltpu.VMEM((rows, units), BF16),
+                        pltpu.VMEM((8 * width, vocab), BF16), pltpu.VMEM((RING, 8) + block, BF16),
+                        pltpu.VMEM((rows, vocab), F32),
                         pltpu.VMEM((RING, 1, rows), jnp.int32), pltpu.VMEM((RING,) + stats, F32),
                         pltpu.VMEM((RING,) + stats, F32), pltpu.VMEM((8,) + stats, F32),
-                        dma((16,)), dma((4, 7)), dma((4, 8)), dma((3,)), dma((3,)), dma((3,)), dma((3,)),
-                        dma((3,)), dma((4,)), dma((7,)), dma((8,))],
-        compiler_params=pltpu.CompilerParams(collective_id=3, has_side_effects=True,
-                                             vmem_limit_bytes=48 << 20),
-        cost_estimate=pl.CostEstimate(flops=30 << 30, bytes_accessed=9 << 20, transcendentals=0),
-        name="head",
-    )(share, final_gain, targets, *slabs)
-
-
-def spread_head(w_head):
-    y = lax.axis_index("y")
-    part = w_head.shape[1] // RING
-    got = []
-    for shift in range(RING):
-        give = lax.dynamic_slice_in_dim(w_head, lax.rem(y + shift, RING) * part, part, 1)
-        if shift:
-            give = lax.ppermute(give, "y", [(i, (i + shift) % RING) for i in range(RING)])
-        got.append(give)
-    slab = jnp.concatenate(got, axis=0)
-    up = [(i, (i + 1) % RING) for i in range(RING)]
-    down = [(i, (i + 3) % RING) for i in range(RING)]
-    back = lax.ppermute(slab, "z", up)
-    ahead = lax.ppermute(slab, "z", down)
-    middle = slab.shape[0] // 2
-    far_a = lax.ppermute(back[:middle], "z", up)
-    far_b = lax.ppermute(ahead[middle:], "z", down)
-    return (slab, ahead, back, far_a, far_b)
+                        dma((10,)), dma((7,)), dma((4,)), dma((3,)), dma((7,)), dma((4,)), dma((3,)),
+                        dma((7,)), dma((8,)),
+                        dma((4, 7)), dma((4, 8)), dma((3,)), dma((3,)), dma((3,)), dma((3,)),
+                        dma((3,)), dma((4,)), dma((7,)), dma((8,)), dma((3, 3)), dma((3, 3))],
+        compiler_params=pltpu.CompilerParams(collective_id=2, has_side_effects=True,
+                                             vmem_limit_bytes=56 << 20),
+        cost_estimate=pl.CostEstimate(flops=60 << 30, bytes_accessed=24 << 20, transcendentals=0),
+        name="finish",
+    )(attended, tokens, mlp_gain, w_out, final_gain, targets, w_gate, w_up, w_down, w_head, pieces)
 
 
 def body(tokens, attn_gain, mlp_gain, final_gain, q_gain, k_gain, w_query, w_keyval, w_out, w_gate,
          w_up, w_down, w_head, targets, req_lengths, req_tenant, prefix_piece, prefix_kv):
-    slabs = spread_head(w_head)
-    queries, own, pieces = entry(req_lengths, tokens, attn_gain[None], q_gain[None], k_gain[None],
-                                 w_query, w_keyval, prefix_kv)
+    queries, own, pieces, slabs, _ = entry(
+        req_lengths, tokens, attn_gain[None], q_gain[None], k_gain[None], w_query, w_keyval,
+        prefix_kv, w_head)
     attended = attention(req_lengths, req_tenant, prefix_piece, queries, own, pieces)
-    share = layer(attended, tokens, mlp_gain[None], w_out, w_gate, w_up, w_down)
-    logprob = head(share, final_gain[None], targets[None], slabs)
+    share, logprob = finish(attended, tokens, mlp_gain[None], w_out, final_gain[None], targets[None],
+                            w_gate, w_up, w_down, w_head, slabs)
     return (share, logprob[0])
 
 

time: 203 us -> 172 us (0.85)
  waiting for transfers between devices: 19.8 us -> 0 us
  starting transfers between devices: 9.31 us -> 0 us
  local copies, waits for them, and re-layouts: 7.24 us -> 2.79 us
  Pallas kernels: 164 us -> 168 us
    ppermute x7 -> x0, waiting for transfers between devices: 19.8 us -> none  [the longest x1 19.8 us: spread_head(): back = lax.ppermute(slab, 'z', up)]
    ppermute x7 -> x0, starting transfers between devices: 9.31 us -> none  [the longest x3 4.67 us: spread_head(): lax.ppermute(give, 'y', [(i, (i + shift) % RING) for i in range(RING)])]
    pallas_call x1, Pallas kernels: 50.6 us -> 54 us  [entry(): pl.pallas_call(functools.partial(entry_kernel, lengths.shape[1], size **...]
    slice x2 -> x0, local copies, waits for them, and re-layouts: 2.65 us -> none  [the longest x1 1.32 us: spread_head(): far_b = lax.ppermute(ahead[middle:], 'z', down)]
    pallas_call x2 -> x1, Pallas kernels: 85.1 us -> 86.4 us  [finish(): pl.pallas_call(finish_kernel, in_specs=[vmem()] * 6 + [hbm()] * 5, out_sp...]
  transfers between devices with their start and end apart: 7 -> 0, of which waited for: 1 -> 0; matrix products, arithmetic and copies ran while one was open for 1% -> 0% of each run, Pallas kernels for 57% -> 0%
where the time goes in v3:
time: 172 us
  Pallas kernels  168 us (98%)
  local copies, waits for them, and re-layouts  2.79 us (2%)
    pallas_call x1, Pallas kernels, finish(): pl.pallas_call(finish_kernel, in_specs=[vmem()] * 6 + [hbm()] * 5, out_sp...  86.4 us
    pallas_call x1, Pallas kernels, entry(): pl.pallas_call(functools.partial(entry_kernel, lengths.shape[1], size **...  54 us
    pallas_call x1, Pallas kernels, attention(): pl.pallas_call(functools.partial(attention_kernel, lengths.shape[1], piec...  28.1 us

profile of v3, /device:TPU:1, one launch (start us, length us, event | category | flops | bytes accessed | tf_op | source)
XLA Modules:
  0.0 171.9 jit_solution(1529788579329372315)
XLA Ops:
  0.6 54.0 %entry.1 = (bf16[4,256,128]{2,1,0:T(8,128)(2,1)}, bf16[256,128]{1,0:T(8,128)(2,1)}, bf16[16,1024,128]{2,1,0:T(8,128)(2,1)}, bf16[16,128,2048]{2,1,0:T(8,128)(2,1)}, bf16[128,2048]{1,0:T(8,128)(2,1)}) custom-call(s32[1,4]{1,0:T(1,128)} %length_ref.3, bf16[256,256]{1,0:T(8,128)(2,1)} %tok_ref.3, f32[1,2048]{1,0:T(1,128)} %bitcast.8, f32[1,64]{1,0:T(1,128)} %bitcast.12, ...), custom_call_target="tpu_custom_call" | custom-call | flops 32212254720 | bytes 8388608 | tf_op jit(solution)/shard_map/entry/pallas_call | solution.py:319
  54.7 28.1 %attention.1.att_ref = bf16[256,256]{1,0:T(8,128)(2,1)} custom-call(s32[1,4]{1,0:T(1,128)} %length_ref.3, s32[1,4]{1,0:T(1,128)} %tenant_ref.1, s32[16]{0:T(128)} %piece_ref.1, bf16[4,256,128]{2,1,0:T(8,128)(2,1)} %get-tuple-element.8.q_ref, bf16[256,128]{1,0:T(8,128)(2,1)} %get-tuple-element.9.own_ref, bf16[16,1024,128]{2,1,0:T(8,128)(2,1)} %get-tuple-element.10.kv_ref), custom_call_target="tpu_custom_call" | custom-call | flops 25769803776 | bytes 5242880 | tf_op jit(solution)/shard_map/attention/pallas_call | solution.py:396
  82.7 86.4 %finish.1 = (bf16[256,256]{1,0:T(8,128)(2,1)}, f32[1,256]{1,0:T(1,128)}) custom-call(bf16[256,256]{1,0:T(8,128)(2,1)} %attention.1.att_ref, bf16[256,256]{1,0:T(8,128)(2,1)} %tok_ref.3, f32[1,2048]{1,0:T(1,128)} %bitcast.9, bf16[256,2048]{1,0:T(8,128)(2,1)} %wo_ref.1, f32[1,2048]{1,0:T(1,128)} %bitcast.10, s32[1,256]{1,0:T(1,128)} %bitcast.11, ...), custom_call_target="tpu_custom_call" | custom-call | flops 64424509440 | bytes 25165824 | tf_op jit(solution)/shard_map/finish/pallas_call | solution.py:596
  169.1 1.6 copy.22
  170.7 1.2 copy.23

commit v4 on v3

--- a/solution.py
+++ b/solution.py
@@ -476,6 +476,7 @@
     middle.relay()
     middle.close()
     normalise(mid, gain_ref, normed)
+    head_relay(0)
     loads[0].wait()
     loads[1].wait()
     for t in range(inner.shape[1] // width):
@@ -484,7 +485,7 @@
         upper = dot(normed[...], wu[:, tile])
         inner[:, tile] = (gate / (1.0 + jnp.exp(-gate)) * upper).astype(BF16)
     loads[2].wait()
-    head_relay(0)
+    head_relay(1)
     value = scatter_sum(lambda d: dot(inner[...], wd[:, columns(d, width)]),
                         stage2, paired2, inbox2, send2, pair_sem2, in_sem2)
     share = (mid[mine].astype(F32) + value).astype(BF16)
@@ -502,7 +503,7 @@
     push(own, own, ysend.at[0], yrecv.at[0], y=y_ahead)
     push(own, own, ysend.at[1], yrecv.at[1], y=y_back)
     first.open()
-    head_relay(1)
+    head_relay(2)
 
     arrived(hidden.at[y_back, mine], yrecv.at[0])
     push(hidden.at[y_back, mine], hidden.at[y_back, mine], ysend.at[2], yrecv.at[2], y=y_ahead)
@@ -513,7 +514,7 @@
     first.relay()
     arrived(hidden.at[y_far, mine], yrecv.at[2])
     gather_of(3, y_far).open()
-    head_relay(2)
+    gathers[1].relay()
     first.close()
     for i, group in enumerate((y_back, y_ahead, y_far)):
         arrived(wanted.at[group], trecv.at[i])
@@ -536,10 +537,12 @@
         if index:
             gathers[index].close()
         normalise(hidden.at[group], last_gain_ref, normed)
-        if index < 3:
-            gathers[index + 1].relay()
+        if index == 0:
+            gathers[2].relay()
         for t in range(vocab // tile):
             logits[:, t * tile:(t + 1) * tile] = dot(normed[...], weight[:, t * tile:(t + 1) * tile])
+        if index == 0:
+            gathers[3].relay()
         value = logits[...]
         top = jnp.max(value, axis=1, keepdims=True)
         total = jnp.sum(jnp.exp(value - top), axis=1, keepdims=True)

time: 172 us -> 169 us (0.983)
  Pallas kernels: 168 us -> 165 us
    pallas_call x1, Pallas kernels: 28.1 us -> 24.8 us  [attention(): pl.pallas_call(functools.partial(attention_kernel, lengths.shape[1], piec...]
where the time goes in v4:
time: 169 us
  Pallas kernels  165 us (98%)
  local copies, waits for them, and re-layouts  2.79 us (2%)
    pallas_call x1, Pallas kernels, finish(): pl.pallas_call(finish_kernel, in_specs=[vmem()] * 6 + [hbm()] * 5, out_sp...  86.5 us
    pallas_call x1, Pallas kernels, entry(): pl.pallas_call(functools.partial(entry_kernel, lengths.shape[1], size **...  54 us
    pallas_call x1, Pallas kernels, attention(): pl.pallas_call(functools.partial(attention_kernel, lengths.shape[1], piec...  24.8 us

profile of v4, /device:TPU:1, one launch (start us, length us, event | category | flops | bytes accessed | tf_op | source)
XLA Modules:
  0.0 168.8 jit_solution(14913860088739631793)
XLA Ops:
  0.6 54.0 %entry.1 = (bf16[4,256,128]{2,1,0:T(8,128)(2,1)}, bf16[256,128]{1,0:T(8,128)(2,1)}, bf16[16,1024,128]{2,1,0:T(8,128)(2,1)}, bf16[16,128,2048]{2,1,0:T(8,128)(2,1)}, bf16[128,2048]{1,0:T(8,128)(2,1)}) custom-call(s32[1,4]{1,0:T(1,128)} %length_ref.3, bf16[256,256]{1,0:T(8,128)(2,1)} %tok_ref.3, f32[1,2048]{1,0:T(1,128)} %bitcast.8, f32[1,64]{1,0:T(1,128)} %bitcast.12, ...), custom_call_target="tpu_custom_call" | custom-call | flops 32212254720 | bytes 8388608 | tf_op jit(solution)/shard_map/entry/pallas_call | solution.py:319
  54.7 24.8 %attention.1.att_ref = bf16[256,256]{1,0:T(8,128)(2,1)} custom-call(s32[1,4]{1,0:T(1,128)} %length_ref.3, s32[1,4]{1,0:T(1,128)} %tenant_ref.1, s32[16]{0:T(128)} %piece_ref.1, bf16[4,256,128]{2,1,0:T(8,128)(2,1)} %get-tuple-element.8.q_ref, bf16[256,128]{1,0:T(8,128)(2,1)} %get-tuple-element.9.own_ref, bf16[16,1024,128]{2,1,0:T(8,128)(2,1)} %get-tuple-element.10.kv_ref), custom_call_target="tpu_custom_call" | custom-call | flops 25769803776 | bytes 5242880 | tf_op jit(solution)/shard_map/attention/pallas_call | solution.py:396
  79.5 86.5 %finish.1 = (bf16[256,256]{1,0:T(8,128)(2,1)}, f32[1,256]{1,0:T(1,128)}) custom-call(bf16[256,256]{1,0:T(8,128)(2,1)} %attention.1.att_ref, bf16[256,256]{1,0:T(8,128)(2,1)} %tok_ref.3, f32[1,2048]{1,0:T(1,128)} %bitcast.9, bf16[256,2048]{1,0:T(8,128)(2,1)} %wo_ref.1, f32[1,2048]{1,0:T(1,128)} %bitcast.10, s32[1,256]{1,0:T(1,128)} %bitcast.11, ...), custom_call_target="tpu_custom_call" | custom-call | flops 64424509440 | bytes 25165824 | tf_op jit(solution)/shard_map/finish/pallas_call | solution.py:599
  166.0 1.6 copy.22
  167.5 1.2 copy.23

commit v5 on v4

--- a/solution.py
+++ b/solution.py
@@ -84,9 +84,15 @@
         self.wait(self.ahead, self.core)
         self.push(self.ahead, self.core, c=1 - self.core)
 
-    def close(self):
+    def last(self):
         self.wait(self.far, self.core)
         self.push(self.far, self.core, c=1 - self.core)
+
+    def close(self):
+        self.last()
+        self.rest()
+
+    def rest(self):
         for x in (self.x, self.back, self.ahead, self.far):
             self.wait(x, 1 - self.core)
 
@@ -147,7 +153,7 @@
 
 
 def entry_kernel(requests, scale, length_ref, tok_ref, gain_ref, qgain_ref, kgain_ref, wq_ref,
-                 wkv_ref, prefix_ref, head_ref, q_out, own_out, pieces, head_out, passing, stream,
+                 wkv_ref, prefix_ref, head_ref, q_out, own_out, pieces, head_out, stream,
                  normed, send, recv, psend, precv, wsend, wrecv, local_sem):
     core = lax.axis_index("c")
     rows = tok_ref.shape[0]
@@ -198,9 +204,8 @@
         copy.start()
         given.append(copy)
 
-    give(2, words(y_far), passing, y=y_ahead)
-    give(4, words(y), piece(z, y), z=z_ahead)
-    give(5, words(y), piece(z, y), z=z_back)
+    give(2, words(y), piece(z, y), z=z_ahead)
+    give(3, words(y), piece(z, y), z=z_back)
     give(0, words(y_ahead), piece(z, y), y=y_ahead)
     give(1, words(y_back), piece(z, y), y=y_back)
     keep = [pltpu.make_async_copy(prefix_ref.at[0], pieces.at[z * RING + y], local_sem.at[0]),
@@ -253,6 +258,8 @@
     far_z = [(py, z_back, z_ahead) for py in (y, y_far)] + [(py, z_ahead, z_back) for py in (y_back, y_ahead)]
     far_y = [(pz, y_back, y_ahead) for pz in (z, z_far)] + [(pz, y_ahead, y_back) for pz in (z_back, z_ahead)]
     order = (0, 2, 3, 1)
+    arrived(piece(z_back, y), wrecv.at[2])
+    give(4, piece(z_back, y), piece(z_back, y), z=z_ahead)
     for i in order:
         py, come, go = far_z[i]
         wait(0, come, py)
@@ -260,11 +267,6 @@
         pz, come, go = far_y[i]
         wait(1, pz, come)
         push(1, pz, come, y=go)
-
-    arrived(passing, wrecv.at[2])
-    give(3, passing, piece(z, y_back), y=y_ahead)
-    arrived(piece(z_back, y), wrecv.at[4])
-    give(6, piece(z_back, y), piece(z_back, y), z=z_ahead)
 
     query = dot(normed[...], wq_ref[...])
     keyval = dot(normed[...], wkv_ref[...])
@@ -289,9 +291,8 @@
         wait(1, pz, y_far)
     arrived(piece(z, y_back), wrecv.at[0])
     arrived(piece(z, y_ahead), wrecv.at[1])
-    arrived(piece(z, y_far), wrecv.at[3])
-    arrived(piece(z_ahead, y), wrecv.at[5])
-    arrived(piece(z_far, y), wrecv.at[6])
+    arrived(piece(z_ahead, y), wrecv.at[3])
+    arrived(piece(z_far, y), wrecv.at[4])
     keep[0].wait()
     gather.finish()
     for copy in sent + given:
@@ -319,16 +320,15 @@
     return pl.pallas_call(
         functools.partial(entry_kernel, lengths.shape[1], size ** (-0.5)),
         in_specs=[smem()] + [vmem()] * 7 + [hbm()],
-        out_specs=[vmem(), vmem(), hbm(), hbm(), hbm()],
+        out_specs=[vmem(), vmem(), hbm(), hbm()],
         out_shape=[jax.ShapeDtypeStruct((rows // BLOCK, heads * BLOCK, 2 * size), BF16),
                    jax.ShapeDtypeStruct((rows, 2 * size), BF16),
                    jax.ShapeDtypeStruct((count,) + prefix_kv.shape[1:], BF16),
-                   jax.ShapeDtypeStruct((count,) + quarter, BF16),
-                   jax.ShapeDtypeStruct(quarter, BF16)],
+                   jax.ShapeDtypeStruct((count,) + quarter, BF16)],
         scratch_shapes=[pltpu.VMEM((8, rows, width), BF16), pltpu.VMEM((rows, 8 * width), BF16),
                         pltpu.SemaphoreType.DMA((7,)), pltpu.SemaphoreType.DMA((8,)),
                         pltpu.SemaphoreType.DMA((30,)), pltpu.SemaphoreType.DMA((2, count)),
-                        pltpu.SemaphoreType.DMA((7,)), pltpu.SemaphoreType.DMA((7,)),
+                        pltpu.SemaphoreType.DMA((5,)), pltpu.SemaphoreType.DMA((5,)),
                         pltpu.SemaphoreType.DMA((2,))],
         compiler_params=pltpu.CompilerParams(collective_id=1, has_side_effects=True),
         cost_estimate=pl.CostEstimate(flops=30 << 30, bytes_accessed=8 << 20, transcendentals=0),
@@ -414,8 +414,8 @@
                   wg, wu, wd, stage, paired, inbox, stage2, paired2, inbox2, mid, normed, inner,
                   weight, hidden, logits, wanted, stat, stat_y, stat_m,
                   load, send, pair_sem, in_sem, send2, pair_sem2, in_sem2, msend, mrecv,
-                  gsend, grecv, ysend, yrecv, tsend, trecv, ssend, srecv, ksend, krecv,
-                  zsend, zrecv):
+                  gsend, grecv, ysend, tsend, trecv, ssend, srecv, ksend, krecv,
+                  zsend, zrecv, passing, wsend, wrecv):
     core = lax.axis_index("c")
     rows, width = tok_ref.shape
     depth, vocab = pieces_hbm.shape[1:]
@@ -450,15 +450,19 @@
     for pz in (z_ahead, z_back, z_far):
         fetch(pieces_hbm.at[pz * RING + y], place(pz, y))
     rest = (y_back, y_ahead, y_far)
-    for py in rest:
+    for py in rest[:2]:
         fetch(pieces_hbm.at[z * RING + py], place(z, py))
     others = [dict(x=lax.rem(x + i // 2, RING), c=lax.rem(core + i % 2, 2)) for i in range(1, 8)]
     greet([dict(y=y_ahead), dict(y=y_back), dict(y=y_far), dict(z=z_ahead), dict(z=z_back)] + others)
 
-    for i, py in enumerate(rest):
-        source = pieces_hbm.at[z * RING + py]
-        push(source, place(z, py), zsend.at[i, 0], zrecv.at[i, 0], z=z_ahead)
-        push(source, place(z, py), zsend.at[i, 1], zrecv.at[i, 1], z=z_back)
+    def head_open(i, source):
+        to = place(z, rest[i])
+        push(source, to, zsend.at[i, 0], zrecv.at[i, 0], z=z_ahead)
+        push(source, to, zsend.at[i, 1], zrecv.at[i, 1], z=z_back)
+
+    push(head_hbm.at[:, columns(y_far, vocab)], passing, wsend.at[0], wrecv.at[0], y=y_ahead)
+    for i in range(2):
+        head_open(i, pieces_hbm.at[z * RING + rest[i]])
     for i, to in enumerate((y_ahead, y_back, y_far)):
         push(target_ref, wanted.at[y], tsend.at[i], trecv.at[i], y=to)
     wanted[y] = target_ref[...]
@@ -473,9 +477,13 @@
     middle = Gather(mid, msend, mrecv)
     mid[mine] = (tok_ref[...].astype(F32) + value).astype(BF16)
     middle.open()
+    arrived(passing, wrecv.at[0])
+    push(passing, place(z, y_back), wsend.at[1], wrecv.at[1], y=y_ahead)
     middle.relay()
     middle.close()
     normalise(mid, gain_ref, normed)
+    arrived(place(z, y_far), wrecv.at[1])
+    head_open(2, place(z, y_far))
     head_relay(0)
     loads[0].wait()
     loads[1].wait()
@@ -492,30 +500,38 @@
     out_ref[...] = share
     hidden[y, mine] = share
 
-    gathers = {}
-
-    def gather_of(index, group):
-        gathers[index] = Gather(hidden.at[group], gsend.at[index], grecv.at[group])
-        return gathers[index]
-
-    own = hidden.at[y, mine]
-    first = gather_of(0, y)
-    push(own, own, ysend.at[0], yrecv.at[0], y=y_ahead)
-    push(own, own, ysend.at[1], yrecv.at[1], y=y_back)
+    first = Gather(hidden.at[y], gsend.at[0], grecv.at[y])
+    distant = Gather(hidden.at[y_far], gsend.at[1], grecv.at[y_far])
+    y_down, y_up = lax.rem(y + 3, RING), lax.rem(y + 1, RING)
+    moved = []
+
+    def hand(group, slot, **device):
+        push(hidden.at[group, slot], hidden.at[group, slot], ysend.at[len(moved)], grecv.at[group, slot],
+             **device)
+        moved.append(slot)
+
+    def spread(to):
+        hand(y, 2 * to + core, y=y_ahead)
+        hand(y, 2 * to + core, y=y_back)
+
+    def collect(group, to):
+        arrived(hidden.at[group, 2 * to + core], grecv.at[group, 2 * to + core])
+        hand(group, 2 * to + core, c=1 - core)
+
     first.open()
+    spread(x)
     head_relay(2)
-
-    arrived(hidden.at[y_back, mine], yrecv.at[0])
-    push(hidden.at[y_back, mine], hidden.at[y_back, mine], ysend.at[2], yrecv.at[2], y=y_ahead)
-    arrived(hidden.at[y_ahead, mine], yrecv.at[1])
-    y_down, y_up = lax.rem(y + 3, RING), lax.rem(y + 1, RING)
-    gather_of(1, y_down).open()
-    gather_of(2, y_up).open()
     first.relay()
-    arrived(hidden.at[y_far, mine], yrecv.at[2])
-    gather_of(3, y_far).open()
-    gathers[1].relay()
-    first.close()
+    spread(x_back)
+    spread(x_ahead)
+    collect(y_back, x)
+    hand(y_back, mine, y=y_ahead)
+    collect(y_ahead, x)
+    first.last()
+    spread(x_far)
+    arrived(hidden.at[y_far, mine], grecv.at[y_far, mine])
+    distant.open()
+    first.rest()
     for i, group in enumerate((y_back, y_ahead, y_far)):
         arrived(wanted.at[group], trecv.at[i])
     for copy in loads[3:]:
@@ -534,15 +550,24 @@
         return jnp.sum(jnp.where(eye, value, 0.0), axis=0, keepdims=True)
 
     for index, group in enumerate((y, y_down, y_up, y_far)):
-        if index:
-            gathers[index].close()
+        if index in (1, 2):
+            for to in range(RING):
+                slot = 2 * to + 1 - core
+                arrived(hidden.at[group, slot], grecv.at[group, slot])
+        if index == 3:
+            distant.rest()
         normalise(hidden.at[group], last_gain_ref, normed)
         if index == 0:
-            gathers[2].relay()
+            for to in (x_back, x_ahead):
+                collect(y_back, to)
+                collect(y_ahead, to)
+            distant.relay()
         for t in range(vocab // tile):
             logits[:, t * tile:(t + 1) * tile] = dot(normed[...], weight[:, t * tile:(t + 1) * tile])
         if index == 0:
-            gathers[3].relay()
+            collect(y_back, x_far)
+            collect(y_ahead, x_far)
+            distant.last()
         value = logits[...]
         top = jnp.max(value, axis=1, keepdims=True)
         total = jnp.sum(jnp.exp(value - top), axis=1, keepdims=True)
@@ -579,8 +604,8 @@
     top, total, picked = merge(stat_m, 8)
     log_ref[...] = picked - top - jnp.log(total)
     middle.finish()
-    for gather in gathers.values():
-        gather.finish()
+    first.finish()
+    distant.finish()
     for copy in sent:
         copy.wait_send()
 
@@ -609,10 +634,11 @@
                         pltpu.VMEM((rows, vocab), F32),
                         pltpu.VMEM((RING, 1, rows), jnp.int32), pltpu.VMEM((RING,) + stats, F32),
                         pltpu.VMEM((RING,) + stats, F32), pltpu.VMEM((8,) + stats, F32),
-                        dma((10,)), dma((7,)), dma((4,)), dma((3,)), dma((7,)), dma((4,)), dma((3,)),
+                        dma((9,)), dma((7,)), dma((4,)), dma((3,)), dma((7,)), dma((4,)), dma((3,)),
                         dma((7,)), dma((8,)),
-                        dma((4, 7)), dma((4, 8)), dma((3,)), dma((3,)), dma((3,)), dma((3,)),
-                        dma((3,)), dma((4,)), dma((7,)), dma((8,)), dma((3, 3)), dma((3, 3))],
+                        dma((2, 7)), dma((4, 8)), dma((17,)), dma((3,)), dma((3,)),
+                        dma((3,)), dma((4,)), dma((7,)), dma((8,)), dma((3, 3)), dma((3, 3)),
+                        pltpu.VMEM((w_head.shape[0], vocab), BF16), dma((2,)), dma((2,))],
         compiler_params=pltpu.CompilerParams(collective_id=2, has_side_effects=True,
                                              vmem_limit_bytes=56 << 20),
         cost_estimate=pl.CostEstimate(flops=60 << 30, bytes_accessed=24 << 20, transcendentals=0),
@@ -622,7 +648,7 @@
 
 def body(tokens, attn_gain, mlp_gain, final_gain, q_gain, k_gain, w_query, w_keyval, w_out, w_gate,
          w_up, w_down, w_head, targets, req_lengths, req_tenant, prefix_piece, prefix_kv):
-    queries, own, pieces, slabs, _ = entry(
+    queries, own, pieces, slabs = entry(
         req_lengths, tokens, attn_gain[None], q_gain[None], k_gain[None], w_query, w_keyval,
         prefix_kv, w_head)
     attended = attention(req_lengths, req_tenant, prefix_piece, queries, own, pieces)

time: 169 us -> 165 us (0.976)
  Pallas kernels: 165 us -> 161 us
    pallas_call x1, Pallas kernels: 54 us -> 49.2 us  [entry(): pl.pallas_call(functools.partial(entry_kernel, lengths.shape[1], size **...]
where the time goes in v5:
time: 165 us
  Pallas kernels  161 us (98%)
  local copies, waits for them, and re-layouts  2.79 us (2%)
    pallas_call x1, Pallas kernels, finish(): pl.pallas_call(finish_kernel, in_specs=[vmem()] * 6 + [hbm()] * 5, out_sp...  87.3 us
    pallas_call x1, Pallas kernels, entry(): pl.pallas_call(functools.partial(entry_kernel, lengths.shape[1], size **...  49.2 us
    pallas_call x1, Pallas kernels, attention(): pl.pallas_call(functools.partial(attention_kernel, lengths.shape[1], piec...  24.8 us

profile of v5, /device:TPU:1, one launch (start us, length us, event | category | flops | bytes accessed | tf_op | source)
XLA Modules:
  0.0 164.8 jit_solution(17967032288026780446)
XLA Ops:
  0.6 49.2 %entry.1 = (bf16[4,256,128]{2,1,0:T(8,128)(2,1)}, bf16[256,128]{1,0:T(8,128)(2,1)}, bf16[16,1024,128]{2,1,0:T(8,128)(2,1)}, bf16[16,128,2048]{2,1,0:T(8,128)(2,1)}) custom-call(s32[1,4]{1,0:T(1,128)} %length_ref.3, bf16[256,256]{1,0:T(8,128)(2,1)} %tok_ref.3, f32[1,2048]{1,0:T(1,128)} %bitcast.8, f32[1,64]{1,0:T(1,128)} %bitcast.12, f32[1,64]{1,0:T(1,128)} %bitcast.13, ...), custom_call_target="tpu_custom_call" | custom-call | flops 32212254720 | bytes 8388608 | tf_op jit(solution)/shard_map/entry/pallas_call | solution.py:320
  49.8 24.8 %attention.1.att_ref = bf16[256,256]{1,0:T(8,128)(2,1)} custom-call(s32[1,4]{1,0:T(1,128)} %length_ref.3, s32[1,4]{1,0:T(1,128)} %tenant_ref.1, s32[16]{0:T(128)} %piece_ref.1, bf16[4,256,128]{2,1,0:T(8,128)(2,1)} %get-tuple-element.8.q_ref, bf16[256,128]{1,0:T(8,128)(2,1)} %get-tuple-element.9.own_ref, bf16[16,1024,128]{2,1,0:T(8,128)(2,1)} %get-tuple-element.10.kv_ref), custom_call_target="tpu_custom_call" | custom-call | flops 25769803776 | bytes 5242880 | tf_op jit(solution)/shard_map/attention/pallas_call | solution.py:396
  74.7 87.3 %finish.1 = (bf16[256,256]{1,0:T(8,128)(2,1)}, f32[1,256]{1,0:T(1,128)}) custom-call(bf16[256,256]{1,0:T(8,128)(2,1)} %attention.1.att_ref, bf16[256,256]{1,0:T(8,128)(2,1)} %tok_ref.3, f32[1,2048]{1,0:T(1,128)} %bitcast.9, bf16[256,2048]{1,0:T(8,128)(2,1)} %wo_ref.1, f32[1,2048]{1,0:T(1,128)} %bitcast.10, s32[1,256]{1,0:T(1,128)} %bitcast.11, ...), custom_call_target="tpu_custom_call" | custom-call | flops 64424509440 | bytes 25165824 | tf_op jit(solution)/shard_map/finish/pallas_call | solution.py:624
  162.0 1.6 copy.22
  163.6 1.2 copy.23

commit v6 on v5

--- a/solution.py
+++ b/solution.py
@@ -204,10 +204,6 @@
         copy.start()
         given.append(copy)
 
-    give(2, words(y), piece(z, y), z=z_ahead)
-    give(3, words(y), piece(z, y), z=z_back)
-    give(0, words(y_ahead), piece(z, y), y=y_ahead)
-    give(1, words(y_back), piece(z, y), y=y_back)
     keep = [pltpu.make_async_copy(prefix_ref.at[0], pieces.at[z * RING + y], local_sem.at[0]),
             pltpu.make_async_copy(tok_ref, stream.at[2 * gather.x + core], local_sem.at[1])]
     for copy in keep:
@@ -234,6 +230,10 @@
     wait(1, z_far, y)
     push(1, z_far, y, y=y_ahead)
     push(1, z_far, y, y=y_back)
+    give(2, words(y), piece(z, y), z=z_ahead)
+    give(3, words(y), piece(z, y), z=z_back)
+    give(0, words(y_ahead), piece(z, y), y=y_ahead)
+    give(1, words(y_back), piece(z, y), y=y_back)
 
     row = lax.broadcasted_iota(jnp.int32, (rows, 1), 0)
     offset = row
@@ -370,19 +370,22 @@
             inside = row_request == r
             tenant = tenant_ref[0, r]
 
-            def piece(index, carry):
-                keyval = kv_ref[slot_ref[tenant * split + index]]
-                part = dot_nt(queries, keyval)
-                old = best_ref[...]
-                new = jnp.where(inside, jnp.maximum(old, jnp.max(part, axis=1, keepdims=True)), old)
-                keep = jnp.exp(old - new)
-                piece_weights = jnp.exp(part - jnp.where(inside, new, -NEG))
-                best_ref[...] = new
-                total_ref[...] = total_ref[...] * keep + jnp.sum(piece_weights, axis=1, keepdims=True)
-                accum_ref[...] = accum_ref[...] * keep + dot(piece_weights.astype(BF16), keyval)
-                return carry
-
-            lax.fori_loop(0, split, piece, 0)
+            old = best_ref[...]
+            keyvals = [kv_ref[slot_ref[tenant * split + index]] for index in range(split)]
+            parts = [dot_nt(queries, keyval) for keyval in keyvals]
+            new = old
+            for part in parts:
+                new = jnp.maximum(new, jnp.max(part, axis=1, keepdims=True))
+            new = jnp.where(inside, new, old)
+            keep = jnp.exp(old - new)
+            shift = jnp.where(inside, new, -NEG)
+            total = total_ref[...] * keep
+            accum = accum_ref[...] * keep
+            for part, keyval in zip(parts, keyvals):
+                piece_weights = jnp.exp(part - shift)
+                total += jnp.sum(piece_weights, axis=1, keepdims=True)
+                accum += dot(piece_weights.astype(BF16), keyval)
+            best_ref[...], total_ref[...], accum_ref[...] = new, total, accum
 
     out = accum_ref[...] / total_ref[...]
     heads = [out[h * BLOCK:(h + 1) * BLOCK, size:] for h in range(count // BLOCK)]
@@ -646,6 +649,21 @@
     )(attended, tokens, mlp_gain, w_out, final_gain, targets, w_gate, w_up, w_down, w_head, pieces)
 
 
+def results_kernel(share_ref, log_ref, share_out, log_out):
+    share_out[...] = share_ref[...]
+    log_out[...] = log_ref[0]
+
+
+def results(share, logprob):
+    return pl.pallas_call(
+        results_kernel,
+        in_specs=[vmem()] * 2,
+        out_specs=[vmem()] * 2,
+        out_shape=[jax.ShapeDtypeStruct(share.shape, BF16), jax.ShapeDtypeStruct(logprob.shape[1:], F32)],
+        name="results",
+    )(share, logprob)
+
+
 def body(tokens, attn_gain, mlp_gain, final_gain, q_gain, k_gain, w_query, w_keyval, w_out, w_gate,
          w_up, w_down, w_head, targets, req_lengths, req_tenant, prefix_piece, prefix_kv):
     queries, own, pieces, slabs = entry(
@@ -654,7 +672,7 @@
     attended = attention(req_lengths, req_tenant, prefix_piece, queries, own, pieces)
     share, logprob = finish(attended, tokens, mlp_gain[None], w_out, final_gain[None], targets[None],
                             w_gate, w_up, w_down, w_head, slabs)
-    return (share, logprob[0])
+    return tuple(results(share, logprob))
 
 
 def solution(mesh):

time: 165 us -> 155 us (0.939)
  Pallas kernels: 161 us -> 154 us
  local copies, waits for them, and re-layouts: 2.79 us -> 0 us
    pallas_call x1, Pallas kernels: 24.8 us -> 19.3 us  [attention(): pl.pallas_call(functools.partial(attention_kernel, lengths.shape[1], piec...]
    pallas_call x1, Pallas kernels: 87.3 us -> 83.7 us  [finish(): pl.pallas_call(finish_kernel, in_specs=[vmem()] * 6 + [hbm()] * 5, out_sp...]
    unnamed x2 -> x0, local copies, waits for them, and re-layouts: 2.79 us -> none
where the time goes in v6:
time: 155 us; the launch traced here: 154 us
  Pallas kernels  154 us (99%)
    pallas_call x1, Pallas kernels, finish(): pl.pallas_call(finish_kernel, in_specs=[vmem()] * 6 + [hbm()] * 5, out_sp...  83.7 us
    pallas_call x1, Pallas kernels, entry(): pl.pallas_call(functools.partial(entry_kernel, lengths.shape[1], size **...  49.2 us
    pallas_call x1, Pallas kernels, attention(): pl.pallas_call(functools.partial(attention_kernel, lengths.shape[1], piec...  19.3 us

profile of v6, /device:TPU:1, one launch (start us, length us, event | category | flops | bytes accessed | tf_op | source)
XLA Modules:
  0.0 154.4 jit_solution(8446465246560866829)
XLA Ops:
  0.6 49.2 %entry.1 = (bf16[4,256,128]{2,1,0:T(8,128)(2,1)}, bf16[256,128]{1,0:T(8,128)(2,1)}, bf16[16,1024,128]{2,1,0:T(8,128)(2,1)}, bf16[16,128,2048]{2,1,0:T(8,128)(2,1)}) custom-call(s32[1,4]{1,0:T(1,128)} %length_ref.3, bf16[256,256]{1,0:T(8,128)(2,1)} %tok_ref.3, f32[1,2048]{1,0:T(1,128)} %bitcast.6, f32[1,64]{1,0:T(1,128)} %bitcast.10, f32[1,64]{1,0:T(1,128)} %bitcast.11, ...), custom_call_target="tpu_custom_call" | custom-call | flops 32212254720 | bytes 8388608 | tf_op jit(solution)/shard_map/entry/pallas_call | solution.py:320
  49.9 19.3 %attention.1.att_ref = bf16[256,256]{1,0:T(8,128)(2,1)} custom-call(s32[1,4]{1,0:T(1,128)} %length_ref.3, s32[1,4]{1,0:T(1,128)} %tenant_ref.1, s32[16]{0:T(128)} %piece_ref.1, bf16[4,256,128]{2,1,0:T(8,128)(2,1)} %get-tuple-element.8.q_ref, bf16[256,128]{1,0:T(8,128)(2,1)} %get-tuple-element.9.own_ref, bf16[16,1024,128]{2,1,0:T(8,128)(2,1)} %get-tuple-element.10.kv_ref), custom_call_target="tpu_custom_call" | custom-call | flops 25769803776 | bytes 5242880 | tf_op jit(solution)/shard_map/attention/pallas_call | solution.py:399
  69.2 83.7 %finish.1 = (bf16[256,256]{1,0:T(8,128)(2,1)}, f32[1,256]{1,0:T(1,128)}) custom-call(bf16[256,256]{1,0:T(8,128)(2,1)} %attention.1.att_ref, bf16[256,256]{1,0:T(8,128)(2,1)} %tok_ref.3, f32[1,2048]{1,0:T(1,128)} %bitcast.7, bf16[256,2048]{1,0:T(8,128)(2,1)} %wo_ref.1, f32[1,2048]{1,0:T(1,128)} %bitcast.8, s32[1,256]{1,0:T(1,128)} %bitcast.9, ...), custom_call_target="tpu_custom_call" | custom-call | flops 64424509440 | bytes 25165824 | tf_op jit(solution)/shard_map/finish/pallas_call | solution.py:627
  152.8 1.6 %results.1 = (bf16[256,256]{1,0:T(8,128)(2,1)}, f32[256]{0:T(256)}) custom-call(bf16[256,256]{1,0:T(8,128)(2,1)} %get-tuple-element.12.share_ref, f32[1,256]{1,0:T(1,128)} %get-tuple-element.13.log_ref), custom_call_target="tpu_custom_call" | custom-call | tf_op jit(solution)/shard_map/results/pallas_call | solution.py:658

commit v7 on v6

--- a/solution.py
+++ b/solution.py
@@ -158,7 +158,8 @@
     core = lax.axis_index("c")
     rows = tok_ref.shape[0]
     size = qgain_ref.shape[1]
-    half = prefix_ref.shape[1] // 2
+    cut = prefix_ref.shape[1] * 3 // 8
+    spans = (pl.ds(0, cut), pl.ds(cut, prefix_ref.shape[1] - cut))
     y, y_ahead, y_back, y_far = ring_of("y", core)
     z, z_ahead, z_back, z_far = ring_of("z", core)
     greet(x_peers() + [dict(y=y_ahead), dict(y=y_back), dict(z=z_ahead), dict(z=z_back)])
@@ -166,7 +167,7 @@
     sent = []
 
     def view(part, pz, py):
-        return pieces.at[pz * RING + py, pl.ds(part * half, half)]
+        return pieces.at[pz * RING + py, spans[part]]
 
     def push(part, pz, py, src=None, **device):
         slot = pz * RING + py
@@ -178,7 +179,7 @@
     def wait(part, pz, py):
         arrived(view(part, pz, py), precv.at[part, pz * RING + py])
 
-    first = [prefix_ref.at[0, pl.ds(part * half, half)] for part in range(2)]
+    first = [prefix_ref.at[0, spans[part]] for part in range(2)]
     gather = Gather(stream, send, recv)
     gather.open(tok_ref)
     push(0, z, y, first[0], y=y_ahead)
@@ -523,13 +524,14 @@
 
     first.open()
     spread(x)
-    head_relay(2)
+    arrived(hidden.at[y_back, mine], grecv.at[y_back, mine])
+    hand(y_back, mine, y=y_ahead)
     first.relay()
     spread(x_back)
     spread(x_ahead)
-    collect(y_back, x)
-    hand(y_back, mine, y=y_ahead)
+    hand(y_back, mine, c=1 - core)
     collect(y_ahead, x)
+    head_relay(2)
     first.last()
     spread(x_far)
     arrived(hidden.at[y_far, mine], grecv.at[y_far, mine])
@@ -560,14 +562,13 @@
         if index == 3:
             distant.rest()
         normalise(hidden.at[group], last_gain_ref, normed)
+        for t in range(vocab // tile):
+            logits[:, t * tile:(t + 1) * tile] = dot(normed[...], weight[:, t * tile:(t + 1) * tile])
         if index == 0:
             for to in (x_back, x_ahead):
                 collect(y_back, to)
                 collect(y_ahead, to)
             distant.relay()
-        for t in range(vocab // tile):
-            logits[:, t * tile:(t + 1) * tile] = dot(normed[...], weight[:, t * tile:(t + 1) * tile])
-        if index == 0:
             collect(y_back, x_far)
             collect(y_ahead, x_far)
             distant.last()

time: 155 us -> 153 us (0.987)
  Pallas kernels: 154 us -> 152 us
    pallas_call x1, Pallas kernels: 49.2 us -> 46.7 us  [entry(): pl.pallas_call(functools.partial(entry_kernel, lengths.shape[1], size **...]
where the time goes in v7:
time: 153 us
  Pallas kernels  152 us (99%)
    pallas_call x1, Pallas kernels, finish(): pl.pallas_call(finish_kernel, in_specs=[vmem()] * 6 + [hbm()] * 5, out_sp...  84.6 us
    pallas_call x1, Pallas kernels, entry(): pl.pallas_call(functools.partial(entry_kernel, lengths.shape[1], size **...  46.7 us
    pallas_call x1, Pallas kernels, attention(): pl.pallas_call(functools.partial(attention_kernel, lengths.shape[1], piec...  19.3 us

profile of v7, /device:TPU:1, one launch (start us, length us, event | category | flops | bytes accessed | tf_op | source)
XLA Modules:
  0.0 152.8 jit_solution(5232313964965117589)
XLA Ops:
  0.6 46.7 %entry.1 = (bf16[4,256,128]{2,1,0:T(8,128)(2,1)}, bf16[256,128]{1,0:T(8,128)(2,1)}, bf16[16,1024,128]{2,1,0:T(8,128)(2,1)}, bf16[16,128,2048]{2,1,0:T(8,128)(2,1)}) custom-call(s32[1,4]{1,0:T(1,128)} %length_ref.3, bf16[256,256]{1,0:T(8,128)(2,1)} %tok_ref.3, f32[1,2048]{1,0:T(1,128)} %bitcast.6, f32[1,64]{1,0:T(1,128)} %bitcast.10, f32[1,64]{1,0:T(1,128)} %bitcast.11, ...), custom_call_target="tpu_custom_call" | custom-call | flops 32212254720 | bytes 8388608 | tf_op jit(solution)/shard_map/entry/pallas_call | solution.py:321
  47.3 19.3 %attention.1.att_ref = bf16[256,256]{1,0:T(8,128)(2,1)} custom-call(s32[1,4]{1,0:T(1,128)} %length_ref.3, s32[1,4]{1,0:T(1,128)} %tenant_ref.1, s32[16]{0:T(128)} %piece_ref.1, bf16[4,256,128]{2,1,0:T(8,128)(2,1)} %get-tuple-element.8.q_ref, bf16[256,128]{1,0:T(8,128)(2,1)} %get-tuple-element.9.own_ref, bf16[16,1024,128]{2,1,0:T(8,128)(2,1)} %get-tuple-element.10.kv_ref), custom_call_target="tpu_custom_call" | custom-call | flops 25769803776 | bytes 5242880 | tf_op jit(solution)/shard_map/attention/pallas_call | solution.py:400
  66.6 84.6 %finish.1 = (bf16[256,256]{1,0:T(8,128)(2,1)}, f32[1,256]{1,0:T(1,128)}) custom-call(bf16[256,256]{1,0:T(8,128)(2,1)} %attention.1.att_ref, bf16[256,256]{1,0:T(8,128)(2,1)} %tok_ref.3, f32[1,2048]{1,0:T(1,128)} %bitcast.7, bf16[256,2048]{1,0:T(8,128)(2,1)} %wo_ref.1, f32[1,2048]{1,0:T(1,128)} %bitcast.8, s32[1,256]{1,0:T(1,128)} %bitcast.9, ...), custom_call_target="tpu_custom_call" | custom-call | flops 64424509440 | bytes 25165824 | tf_op jit(solution)/shard_map/finish/pallas_call | solution.py:628
  151.2 1.6 %results.1 = (bf16[256,256]{1,0:T(8,128)(2,1)}, f32[256]{0:T(256)}) custom-call(bf16[256,256]{1,0:T(8,128)(2,1)} %get-tuple-element.12.share_ref, f32[1,256]{1,0:T(1,128)} %get-tuple-element.13.log_ref), custom_call_target="tpu_custom_call" | custom-call | tf_op jit(solution)/shard_map/results/pallas_call | solution.py:659

commit v8 on v7

--- a/solution.py
+++ b/solution.py
@@ -158,7 +158,7 @@
     core = lax.axis_index("c")
     rows = tok_ref.shape[0]
     size = qgain_ref.shape[1]
-    cut = prefix_ref.shape[1] * 3 // 8
+    cut = prefix_ref.shape[1] * 23 // 32
     spans = (pl.ds(0, cut), pl.ds(cut, prefix_ref.shape[1] - cut))
     y, y_ahead, y_back, y_far = ring_of("y", core)
     z, z_ahead, z_back, z_far = ring_of("z", core)
@@ -196,9 +196,6 @@
 
     def words(index):
         return head_ref.at[:, pl.ds(pl.multiple_of(index * part_words, part_words), part_words)]
-
-    def piece(pz, py):
-        return head_out.at[pz * RING + py]
 
     def give(index, src, dst, **device):
         copy = remote(src, dst, wsend.at[index], wrecv.at[index], **device)
@@ -231,10 +228,8 @@
     wait(1, z_far, y)
     push(1, z_far, y, y=y_ahead)
     push(1, z_far, y, y=y_back)
-    give(2, words(y), piece(z, y), z=z_ahead)
-    give(3, words(y), piece(z, y), z=z_back)
-    give(0, words(y_ahead), piece(z, y), y=y_ahead)
-    give(1, words(y_back), piece(z, y), y=y_back)
+    give(0, words(y_ahead), head_out.at[0], y=y_ahead)
+    give(1, words(y_back), head_out.at[1], y=y_back)
 
     row = lax.broadcasted_iota(jnp.int32, (rows, 1), 0)
     offset = row
@@ -259,8 +254,6 @@
     far_z = [(py, z_back, z_ahead) for py in (y, y_far)] + [(py, z_ahead, z_back) for py in (y_back, y_ahead)]
     far_y = [(pz, y_back, y_ahead) for pz in (z, z_far)] + [(pz, y_ahead, y_back) for pz in (z_back, z_ahead)]
     order = (0, 2, 3, 1)
-    arrived(piece(z_back, y), wrecv.at[2])
-    give(4, piece(z_back, y), piece(z_back, y), z=z_ahead)
     for i in order:
         py, come, go = far_z[i]
         wait(0, come, py)
@@ -290,10 +283,8 @@
         wait(0, z_far, py)
     for pz, come, go in far_y:
         wait(1, pz, y_far)
-    arrived(piece(z, y_back), wrecv.at[0])
-    arrived(piece(z, y_ahead), wrecv.at[1])
-    arrived(piece(z_ahead, y), wrecv.at[3])
-    arrived(piece(z_far, y), wrecv.at[4])
+    for i in range(2):
+        arrived(head_out.at[i], wrecv.at[i])
     keep[0].wait()
     gather.finish()
     for copy in sent + given:
@@ -325,11 +316,11 @@
         out_shape=[jax.ShapeDtypeStruct((rows // BLOCK, heads * BLOCK, 2 * size), BF16),
                    jax.ShapeDtypeStruct((rows, 2 * size), BF16),
                    jax.ShapeDtypeStruct((count,) + prefix_kv.shape[1:], BF16),
-                   jax.ShapeDtypeStruct((count,) + quarter, BF16)],
+                   jax.ShapeDtypeStruct((2,) + quarter, BF16)],
         scratch_shapes=[pltpu.VMEM((8, rows, width), BF16), pltpu.VMEM((rows, 8 * width), BF16),
                         pltpu.SemaphoreType.DMA((7,)), pltpu.SemaphoreType.DMA((8,)),
                         pltpu.SemaphoreType.DMA((30,)), pltpu.SemaphoreType.DMA((2, count)),
-                        pltpu.SemaphoreType.DMA((5,)), pltpu.SemaphoreType.DMA((5,)),
+                        pltpu.SemaphoreType.DMA((2,)), pltpu.SemaphoreType.DMA((2,)),
                         pltpu.SemaphoreType.DMA((2,))],
         compiler_params=pltpu.CompilerParams(collective_id=1, has_side_effects=True),
         cost_estimate=pl.CostEstimate(flops=30 << 30, bytes_accessed=8 << 20, transcendentals=0),
@@ -414,15 +405,15 @@
 
 
 def finish_kernel(att_ref, tok_ref, gain_ref, wo_ref, last_gain_ref, target_ref, wg_hbm, wu_hbm, wd_hbm,
-                  head_hbm, pieces_hbm, out_ref, log_ref,
+                  head_hbm, near_hbm, back_hbm, ahead_hbm, out_ref, log_ref,
                   wg, wu, wd, stage, paired, inbox, stage2, paired2, inbox2, mid, normed, inner,
                   weight, hidden, logits, wanted, stat, stat_y, stat_m,
                   load, send, pair_sem, in_sem, send2, pair_sem2, in_sem2, msend, mrecv,
                   gsend, grecv, ysend, tsend, trecv, ssend, srecv, ksend, krecv,
-                  zsend, zrecv, passing, wsend, wrecv):
+                  zsend, zrecv, passing, wsend, wrecv, fsend, frecv):
     core = lax.axis_index("c")
     rows, width = tok_ref.shape
-    depth, vocab = pieces_hbm.shape[1:]
+    depth, vocab = near_hbm.shape[1:]
     x, x_ahead, x_back, x_far = ring_of("x", core)
     y, y_ahead, y_back, y_far = ring_of("y", core)
     z, z_ahead, z_back, z_far = ring_of("z", core)
@@ -451,11 +442,12 @@
     fetch(wu_hbm, wu)
     fetch(wd_hbm, wd)
     fetch(head_hbm.at[:, columns(y, vocab)], place(z, y))
-    for pz in (z_ahead, z_back, z_far):
-        fetch(pieces_hbm.at[pz * RING + y], place(pz, y))
-    rest = (y_back, y_ahead, y_far)
-    for py in rest[:2]:
-        fetch(pieces_hbm.at[z * RING + py], place(z, py))
+    for i, py in enumerate((y_back, y_ahead)):
+        fetch(near_hbm.at[i], place(z, py))
+    for i, py in enumerate((y, y_back)):
+        fetch(back_hbm.at[pl.ds(i * depth, depth)], place(z_back, py))
+        fetch(ahead_hbm.at[pl.ds(i * depth, depth)], place(z_ahead, py))
+    rest = (y_ahead, y_far)
     others = [dict(x=lax.rem(x + i // 2, RING), c=lax.rem(core + i % 2, 2)) for i in range(1, 8)]
     greet([dict(y=y_ahead), dict(y=y_back), dict(y=y_far), dict(z=z_ahead), dict(z=z_back)] + others)
 
@@ -465,8 +457,9 @@
         push(source, to, zsend.at[i, 1], zrecv.at[i, 1], z=z_back)
 
     push(head_hbm.at[:, columns(y_far, vocab)], passing, wsend.at[0], wrecv.at[0], y=y_ahead)
-    for i in range(2):
-        head_open(i, pieces_hbm.at[z * RING + rest[i]])
+    head_open(0, near_hbm.at[1])
+    for i, py in enumerate((y, y_back)):
+        push(back_hbm.at[pl.ds(i * depth, depth)], place(z_back, py), fsend.at[i], frecv.at[i], z=z_ahead)
     for i, to in enumerate((y_ahead, y_back, y_far)):
         push(target_ref, wanted.at[y], tsend.at[i], trecv.at[i], y=to)
     wanted[y] = target_ref[...]
@@ -487,7 +480,7 @@
     middle.close()
     normalise(mid, gain_ref, normed)
     arrived(place(z, y_far), wrecv.at[1])
-    head_open(2, place(z, y_far))
+    head_open(1, place(z, y_far))
     head_relay(0)
     loads[0].wait()
     loads[1].wait()
@@ -497,7 +490,6 @@
         upper = dot(normed[...], wu[:, tile])
         inner[:, tile] = (gate / (1.0 + jnp.exp(-gate)) * upper).astype(BF16)
     loads[2].wait()
-    head_relay(1)
     value = scatter_sum(lambda d: dot(inner[...], wd[:, columns(d, width)]),
                         stage2, paired2, inbox2, send2, pair_sem2, in_sem2)
     share = (mid[mine].astype(F32) + value).astype(BF16)
@@ -531,7 +523,7 @@
     spread(x_ahead)
     hand(y_back, mine, c=1 - core)
     collect(y_ahead, x)
-    head_relay(2)
+    head_relay(1)
     first.last()
     spread(x_far)
     arrived(hidden.at[y_far, mine], grecv.at[y_far, mine])
@@ -541,6 +533,8 @@
         arrived(wanted.at[group], trecv.at[i])
     for copy in loads[3:]:
         copy.wait()
+    for i, py in enumerate((y, y_back)):
+        arrived(place(z_far, py), frecv.at[i])
     for i, py in enumerate(rest):
         arrived(place(z_ahead, py), zrecv.at[i, 1])
         arrived(place(z_far, py), zrecv.at[i, 2])
@@ -614,11 +608,12 @@
         copy.wait_send()
 
 
-def finish(attended, tokens, mlp_gain, w_out, final_gain, targets, w_gate, w_up, w_down, w_head, pieces):
+def finish(attended, tokens, mlp_gain, w_out, final_gain, targets, w_gate, w_up, w_down, w_head, near,
+           from_back, from_ahead):
     rows, width = tokens.shape
     units = w_gate.shape[1]
     block = (rows, width)
-    vocab = pieces.shape[2]
+    vocab = near.shape[2]
     dma = pltpu.SemaphoreType.DMA
     stats = (8, rows)
 
@@ -627,7 +622,7 @@
 
     return pl.pallas_call(
         finish_kernel,
-        in_specs=[vmem()] * 6 + [hbm()] * 5,
+        in_specs=[vmem()] * 6 + [hbm()] * 7,
         out_specs=[vmem(), vmem()],
         out_shape=[jax.ShapeDtypeStruct(block, BF16), jax.ShapeDtypeStruct((1, rows), F32)],
         scratch_shapes=[pltpu.VMEM(w_gate.shape, BF16), pltpu.VMEM(w_up.shape, BF16),
@@ -638,16 +633,18 @@
                         pltpu.VMEM((rows, vocab), F32),
                         pltpu.VMEM((RING, 1, rows), jnp.int32), pltpu.VMEM((RING,) + stats, F32),
                         pltpu.VMEM((RING,) + stats, F32), pltpu.VMEM((8,) + stats, F32),
-                        dma((9,)), dma((7,)), dma((4,)), dma((3,)), dma((7,)), dma((4,)), dma((3,)),
+                        dma((10,)), dma((7,)), dma((4,)), dma((3,)), dma((7,)), dma((4,)), dma((3,)),
                         dma((7,)), dma((8,)),
                         dma((2, 7)), dma((4, 8)), dma((17,)), dma((3,)), dma((3,)),
-                        dma((3,)), dma((4,)), dma((7,)), dma((8,)), dma((3, 3)), dma((3, 3)),
-                        pltpu.VMEM((w_head.shape[0], vocab), BF16), dma((2,)), dma((2,))],
+                        dma((3,)), dma((4,)), dma((7,)), dma((8,)), dma((2, 3)), dma((2, 3)),
+                        pltpu.VMEM((w_head.shape[0], vocab), BF16), dma((2,)), dma((2,)),
+                        dma((2,)), dma((2,))],
         compiler_params=pltpu.CompilerParams(collective_id=2, has_side_effects=True,
                                              vmem_limit_bytes=56 << 20),
         cost_estimate=pl.CostEstimate(flops=60 << 30, bytes_accessed=24 << 20, transcendentals=0),
         name="finish",
-    )(attended, tokens, mlp_gain, w_out, final_gain, targets, w_gate, w_up, w_down, w_head, pieces)
+    )(attended, tokens, mlp_gain, w_out, final_gain, targets, w_gate, w_up, w_down, w_head, near,
+      from_back, from_ahead)
 
 
 def results_kernel(share_ref, log_ref, share_out, log_out):
@@ -667,12 +664,18 @@
 
 def body(tokens, attn_gain, mlp_gain, final_gain, q_gain, k_gain, w_query, w_keyval, w_out, w_gate,
          w_up, w_down, w_head, targets, req_lengths, req_tenant, prefix_piece, prefix_kv):
-    queries, own, pieces, slabs = entry(
+    queries, own, pieces, near = entry(
         req_lengths, tokens, attn_gain[None], q_gain[None], k_gain[None], w_query, w_keyval,
         prefix_kv, w_head)
+    words = w_head.shape[1] // RING
+    mine = lax.dynamic_slice_in_dim(w_head, lax.axis_index("y") * words, words, 1)
+    pair = jnp.concatenate([mine, near[0]], axis=0)
+    ahead = [(2 * z + c, 2 * ((z + 1 + 2 * c) % RING) + c) for z in range(RING) for c in range(2)]
+    from_back = lax.ppermute(pair, ("z", "c"), ahead)
+    from_ahead = lax.ppermute(pair, ("z", "c"), [(b, a) for a, b in ahead])
     attended = attention(req_lengths, req_tenant, prefix_piece, queries, own, pieces)
     share, logprob = finish(attended, tokens, mlp_gain[None], w_out, final_gain[None], targets[None],
-                            w_gate, w_up, w_down, w_head, slabs)
+                            w_gate, w_up, w_down, w_head, near, from_back, from_ahead)
     return tuple(results(share, logprob))
 
 

time: 153 us -> 150 us (0.980)
  Pallas kernels: 152 us -> 137 us
  waiting for transfers between devices: 0 us -> 8.66 us
  local copies, waits for them, and re-layouts: 0 us -> 2.17 us
  starting transfers between devices: 0 us -> 1.92 us
    ppermute x0 -> x2, waiting for transfers between devices: none -> 8.66 us  [the longest x1 5.82 us: body(): from_ahead = lax.ppermute(pair, ('z', 'c'), [(b, a) for a, b in ahead])]
    pallas_call x1, Pallas kernels: 46.7 us -> 38.3 us  [entry(): pl.pallas_call(functools.partial(entry_kernel, lengths.shape[1], size **...]
    pallas_call x1, Pallas kernels: 84.6 us -> 79.4 us  [finish(): pl.pallas_call(finish_kernel, in_specs=[vmem()] * 6 + [hbm()] * 7, out_sp...]
    pallas_call x1, Pallas kernels: 19.3 us -> 17.3 us  [attention(): pl.pallas_call(functools.partial(attention_kernel, lengths.shape[1], piec...]
    ppermute x0 -> x2, starting transfers between devices: none -> 1.92 us  [the longest x1 1.92 us: body(): from_back = lax.ppermute(pair, ('z', 'c'), ahead)]
  transfers between devices with their start and end apart: 0 -> 2, of which waited for: 0 -> 2; matrix products, arithmetic and copies ran while one was open for 0% -> 0% of each run, Pallas kernels for 0% -> 12%
where the time goes in v8:
time: 150 us
  Pallas kernels  137 us (91%)
  waiting for transfers between devices  8.66 us (6%)
  local copies, waits for them, and re-layouts  2.17 us (1%)
  starting transfers between devices  1.92 us (1%)
    pallas_call x1, Pallas kernels, finish(): pl.pallas_call(finish_kernel, in_specs=[vmem()] * 6 + [hbm()] * 7, out_sp...  79.4 us
    pallas_call x1, Pallas kernels, entry(): pl.pallas_call(functools.partial(entry_kernel, lengths.shape[1], size **...  38.3 us
    pallas_call x1, Pallas kernels, attention(): pl.pallas_call(functools.partial(attention_kernel, lengths.shape[1], piec...  17.3 us
    ppermute x1, waiting for transfers between devices, body(): from_ahead = lax.ppermute(pair, ('z', 'c'), [(b, a) for a, b in ahead])  5.82 us
  transfers between devices with their start and end apart: 2, of which 2 were waited for; matrix products, arithmetic and copies ran while one was open for 0% of the time, Pallas kernels for 12%

profile of v8, /device:TPU:1, one launch (start us, length us, event | category | flops | bytes accessed | tf_op | source)
XLA Modules:
  0.0 150.2 jit_solution(15436954570812871837)
XLA Ops:
  0.6 38.3 %entry.1 = (bf16[4,256,128]{2,1,0:T(8,128)(2,1)}, bf16[256,128]{1,0:T(8,128)(2,1)}, bf16[16,1024,128]{2,1,0:T(8,128)(2,1)}, bf16[2,128,2048]{2,1,0:T(8,128)(2,1)}) custom-call(s32[1,4]{1,0:T(1,128)} %length_ref.3, bf16[256,256]{1,0:T(8,128)(2,1)} %tok_ref.3, f32[1,2048]{1,0:T(1,128)} %bitcast.8, f32[1,64]{1,0:T(1,128)} %bitcast.12, f32[1,64]{1,0:T(1,128)} %bitcast.13, ...), custom_call_target="tpu_custom_call" | custom-call | flops 32212254720 | bytes 8388608 | tf_op jit(solution)/shard_map/entry/pallas_call | solution.py:312
  39.0 1.1 slice_bitcast_fusion
  40.1 1.1 constant_dynamic-slice_fusion
  41.1 0.1 pad_maximum_fusion
  41.2 1.9 %collective-permute-start = (bf16[256,2048]{1,0:T(8,128)(2,1)S(1)}, bf16[256,2048]{1,0:T(8,128)(2,1)S(1)}, u32[]{:S(2)}, u32[]{:S(2)}) collective-permute-start(bf16[256,2048]{1,0:T(8,128)(2,1)S(1)} %pad_maximum_fusion), channel_id=1, source_target_pairs={{0,32},{1,97},{32,64},{33,1},{64,96},{65,33},{96,0},{97,65},{2,34}... | collective-permute-start | bytes 3145736 | tf_op jit(solution)/shard_map/ppermute | solution.py:674
  43.2 0.0 collective-permute-start.1
  43.2 17.3 %attention.1.att_ref = bf16[256,256]{1,0:T(8,128)(2,1)} custom-call(s32[1,4]{1,0:T(1,128)} %length_ref.3, s32[1,4]{1,0:T(1,128)} %tenant_ref.1, s32[16]{0:T(128)} %piece_ref.1, bf16[4,256,128]{2,1,0:T(8,128)(2,1)} %get-tuple-element.8.q_ref, bf16[256,128]{1,0:T(8,128)(2,1)} %get-tuple-element.9.own_ref, bf16[16,1024,128]{2,1,0:T(8,128)(2,1)} %get-tuple-element.10.kv_ref), custom_call_target="tpu_custom_call" | custom-call | flops 25769803776 | bytes 5242880 | tf_op jit(solution)/shard_map/attention/pallas_call | solution.py:391
  60.5 2.8 %collective-permute-done.back_hbm = bf16[256,2048]{1,0:T(8,128)(2,1)S(1)} collective-permute-done((bf16[256,2048]{1,0:T(8,128)(2,1)S(1)}, bf16[256,2048]{1,0:T(8,128)(2,1)S(1)}, u32[]{:S(2)}, u32[]{:S(2)}) %collective-permute-start) | collective-permute-done | bytes 1048608 | tf_op jit(solution)/shard_map/ppermute | solution.py:674
  63.3 0.0 copy-start
  63.3 5.8 %collective-permute-done.1.ahead_hbm = bf16[256,2048]{1,0:T(8,128)(2,1)} collective-permute-done((bf16[256,2048]{1,0:T(8,128)(2,1)S(1)}, bf16[256,2048]{1,0:T(8,128)(2,1)}, u32[]{:S(2)}, u32[]{:S(2)}) %collective-permute-start.1) | collective-permute-done | bytes 1048608 | tf_op jit(solution)/shard_map/ppermute | solution.py:675
  69.2 0.0 copy-done
  69.2 79.4 %finish.1 = (bf16[256,256]{1,0:T(8,128)(2,1)}, f32[1,256]{1,0:T(1,128)}) custom-call(bf16[256,256]{1,0:T(8,128)(2,1)} %attention.1.att_ref, bf16[256,256]{1,0:T(8,128)(2,1)} %tok_ref.3, f32[1,2048]{1,0:T(1,128)} %bitcast.9, bf16[256,2048]{1,0:T(8,128)(2,1)} %wo_ref.1, f32[1,2048]{1,0:T(1,128)} %bitcast.10, s32[1,256]{1,0:T(1,128)} %bitcast.11, ...), custom_call_target="tpu_custom_call" | custom-call | flops 64424509440 | bytes 25165824 | tf_op jit(solution)/shard_map/finish/pallas_call | solution.py:623
  148.6 1.6 %results.1 = (bf16[256,256]{1,0:T(8,128)(2,1)}, f32[256]{0:T(256)}) custom-call(bf16[256,256]{1,0:T(8,128)(2,1)} %get-tuple-element.12.share_ref, f32[1,256]{1,0:T(1,128)} %get-tuple-element.13.log_ref), custom_call_target="tpu_custom_call" | custom-call | tf_op jit(solution)/shard_map/results/pallas_call | solution.py:656
Async XLA Ops:
  41.2 22.1 %collective-permute-start = (bf16[256,2048]{1,0:T(8,128)(2,1)S(1)}, bf16[256,2048]{1,0:T(8,128)(2,1)S(1)}, u32[]{:S(2)}, u32[]{:S(2)}) collective-permute-start(bf16[256,2048]{1,0:T(8,128)(2,1)S(1)} %pad_maximum_fusion), channel_id=1, source_target_pairs={{0,32},{1,97},{32,64},{33,1},{64,96},{65,33},{96,0},{97,65},{2,34}... | collective-permute-start | bytes 3145736 | tf_op jit(solution)/shard_map/ppermute | solution.py:674
  43.2 26.0 %collective-permute-start.1 = (bf16[256,2048]{1,0:T(8,128)(2,1)S(1)}, bf16[256,2048]{1,0:T(8,128)(2,1)}, u32[]{:S(2)}, u32[]{:S(2)}) collective-permute-start(bf16[256,2048]{1,0:T(8,128)(2,1)S(1)} %pad_maximum_fusion), channel_id=1, source_target_pairs={{32,0},{97,1},{64,32},{1,33},{96,64},{33,65},{0,96},{65,97},{34,2}... | collective-permute-start | bytes 3145736 | tf_op jit(solution)/shard_map/ppermute | solution.py:675
  63.3 5.8 %copy-start = (bf16[256,2048]{1,0:T(8,128)(2,1)}, bf16[256,2048]{1,0:T(8,128)(2,1)S(1)}, u32[]{:S(2)}) copy-start(bf16[256,2048]{1,0:T(8,128)(2,1)S(1)} %collective-permute-done.back_hbm) | copy-start | bytes 3145732

commit v9 on v8

--- a/solution.py
+++ b/solution.py
@@ -153,7 +153,7 @@
 
 
 def entry_kernel(requests, scale, length_ref, tok_ref, gain_ref, qgain_ref, kgain_ref, wq_ref,
-                 wkv_ref, prefix_ref, head_ref, q_out, own_out, pieces, head_out, stream,
+                 wkv_ref, prefix_ref, head_ref, q_out, own_out, pieces, pair_out, other_out, quarter, stream,
                  normed, send, recv, psend, precv, wsend, wrecv, local_sem):
     core = lax.axis_index("c")
     rows = tok_ref.shape[0]
@@ -192,7 +192,7 @@
     push(1, z, y, first[1], y=y_back)
 
     given = []
-    part_words = head_out.shape[2]
+    part_words = pair_out.shape[2]
 
     def words(index):
         return head_ref.at[:, pl.ds(pl.multiple_of(index * part_words, part_words), part_words)]
@@ -203,7 +203,8 @@
         given.append(copy)
 
     keep = [pltpu.make_async_copy(prefix_ref.at[0], pieces.at[z * RING + y], local_sem.at[0]),
-            pltpu.make_async_copy(tok_ref, stream.at[2 * gather.x + core], local_sem.at[1])]
+            pltpu.make_async_copy(tok_ref, stream.at[2 * gather.x + core], local_sem.at[1]),
+            pltpu.make_async_copy(words(y), quarter, local_sem.at[2])]
     for copy in keep:
         copy.start()
 
@@ -228,8 +229,11 @@
     wait(1, z_far, y)
     push(1, z_far, y, y=y_ahead)
     push(1, z_far, y, y=y_back)
-    give(0, words(y_ahead), head_out.at[0], y=y_ahead)
-    give(1, words(y_back), head_out.at[1], y=y_back)
+    give(0, words(y_ahead), pair_out.at[1], y=y_ahead)
+    give(1, words(y_back), other_out, y=y_back)
+    keep[2].wait()
+    keep.append(pltpu.make_async_copy(quarter, pair_out.at[0], local_sem.at[3]))
+    keep[3].start()
 
     row = lax.broadcasted_iota(jnp.int32, (rows, 1), 0)
     offset = row
@@ -283,9 +287,10 @@
         wait(0, z_far, py)
     for pz, come, go in far_y:
         wait(1, pz, y_far)
-    for i in range(2):
-        arrived(head_out.at[i], wrecv.at[i])
+    arrived(pair_out.at[1], wrecv.at[0])
+    arrived(other_out, wrecv.at[1])
     keep[0].wait()
+    keep[3].wait()
     gather.finish()
     for copy in sent + given:
         copy.wait_send()
@@ -312,16 +317,17 @@
     return pl.pallas_call(
         functools.partial(entry_kernel, lengths.shape[1], size ** (-0.5)),
         in_specs=[smem()] + [vmem()] * 7 + [hbm()],
-        out_specs=[vmem(), vmem(), hbm(), hbm()],
+        out_specs=[vmem(), vmem(), hbm(), hbm(), hbm()],
         out_shape=[jax.ShapeDtypeStruct((rows // BLOCK, heads * BLOCK, 2 * size), BF16),
                    jax.ShapeDtypeStruct((rows, 2 * size), BF16),
                    jax.ShapeDtypeStruct((count,) + prefix_kv.shape[1:], BF16),
-                   jax.ShapeDtypeStruct((2,) + quarter, BF16)],
-        scratch_shapes=[pltpu.VMEM((8, rows, width), BF16), pltpu.VMEM((rows, 8 * width), BF16),
+                   jax.ShapeDtypeStruct((2,) + quarter, BF16),
+                   jax.ShapeDtypeStruct(quarter, BF16)],
+        scratch_shapes=[pltpu.VMEM(quarter, BF16), pltpu.VMEM((8, rows, width), BF16), pltpu.VMEM((rows, 8 * width), BF16),
                         pltpu.SemaphoreType.DMA((7,)), pltpu.SemaphoreType.DMA((8,)),
                         pltpu.SemaphoreType.DMA((30,)), pltpu.SemaphoreType.DMA((2, count)),
                         pltpu.SemaphoreType.DMA((2,)), pltpu.SemaphoreType.DMA((2,)),
-                        pltpu.SemaphoreType.DMA((2,))],
+                        pltpu.SemaphoreType.DMA((4,))],
         compiler_params=pltpu.CompilerParams(collective_id=1, has_side_effects=True),
         cost_estimate=pl.CostEstimate(flops=30 << 30, bytes_accessed=8 << 20, transcendentals=0),
         name="entry",
@@ -405,7 +411,7 @@
 
 
 def finish_kernel(att_ref, tok_ref, gain_ref, wo_ref, last_gain_ref, target_ref, wg_hbm, wu_hbm, wd_hbm,
-                  head_hbm, near_hbm, back_hbm, ahead_hbm, out_ref, log_ref,
+                  head_hbm, pair_hbm, other_hbm, back_hbm, ahead_hbm, out_ref, log_ref,
                   wg, wu, wd, stage, paired, inbox, stage2, paired2, inbox2, mid, normed, inner,
                   weight, hidden, logits, wanted, stat, stat_y, stat_m,
                   load, send, pair_sem, in_sem, send2, pair_sem2, in_sem2, msend, mrecv,
@@ -413,7 +419,7 @@
                   zsend, zrecv, passing, wsend, wrecv, fsend, frecv):
     core = lax.axis_index("c")
     rows, width = tok_ref.shape
-    depth, vocab = near_hbm.shape[1:]
+    depth, vocab = other_hbm.shape
     x, x_ahead, x_back, x_far = ring_of("x", core)
     y, y_ahead, y_back, y_far = ring_of("y", core)
     z, z_ahead, z_back, z_far = ring_of("z", core)
@@ -442,8 +448,8 @@
     fetch(wu_hbm, wu)
     fetch(wd_hbm, wd)
     fetch(head_hbm.at[:, columns(y, vocab)], place(z, y))
-    for i, py in enumerate((y_back, y_ahead)):
-        fetch(near_hbm.at[i], place(z, py))
+    fetch(pair_hbm.at[1], place(z, y_back))
+    fetch(other_hbm, place(z, y_ahead))
     for i, py in enumerate((y, y_back)):
         fetch(back_hbm.at[pl.ds(i * depth, depth)], place(z_back, py))
         fetch(ahead_hbm.at[pl.ds(i * depth, depth)], place(z_ahead, py))
@@ -457,7 +463,7 @@
         push(source, to, zsend.at[i, 1], zrecv.at[i, 1], z=z_back)
 
     push(head_hbm.at[:, columns(y_far, vocab)], passing, wsend.at[0], wrecv.at[0], y=y_ahead)
-    head_open(0, near_hbm.at[1])
+    head_open(0, other_hbm)
     for i, py in enumerate((y, y_back)):
         push(back_hbm.at[pl.ds(i * depth, depth)], place(z_back, py), fsend.at[i], frecv.at[i], z=z_ahead)
     for i, to in enumerate((y_ahead, y_back, y_far)):
@@ -608,12 +614,12 @@
         copy.wait_send()
 
 
-def finish(attended, tokens, mlp_gain, w_out, final_gain, targets, w_gate, w_up, w_down, w_head, near,
+def finish(attended, tokens, mlp_gain, w_out, final_gain, targets, w_gate, w_up, w_down, w_head, pair, other,
            from_back, from_ahead):
     rows, width = tokens.shape
     units = w_gate.shape[1]
     block = (rows, width)
-    vocab = near.shape[2]
+    vocab = other.shape[1]
     dma = pltpu.SemaphoreType.DMA
     stats = (8, rows)
 
@@ -622,7 +628,7 @@
 
     return pl.pallas_call(
         finish_kernel,
-        in_specs=[vmem()] * 6 + [hbm()] * 7,
+        in_specs=[vmem()] * 6 + [hbm()] * 8,
         out_specs=[vmem(), vmem()],
         out_shape=[jax.ShapeDtypeStruct(block, BF16), jax.ShapeDtypeStruct((1, rows), F32)],
         scratch_shapes=[pltpu.VMEM(w_gate.shape, BF16), pltpu.VMEM(w_up.shape, BF16),
@@ -643,7 +649,7 @@
                                              vmem_limit_bytes=56 << 20),
         cost_estimate=pl.CostEstimate(flops=60 << 30, bytes_accessed=24 << 20, transcendentals=0),
         name="finish",
-    )(attended, tokens, mlp_gain, w_out, final_gain, targets, w_gate, w_up, w_down, w_head, near,
+    )(attended, tokens, mlp_gain, w_out, final_gain, targets, w_gate, w_up, w_down, w_head, pair, other,
       from_back, from_ahead)
 
 
@@ -664,18 +670,16 @@
 
 def body(tokens, attn_gain, mlp_gain, final_gain, q_gain, k_gain, w_query, w_keyval, w_out, w_gate,
          w_up, w_down, w_head, targets, req_lengths, req_tenant, prefix_piece, prefix_kv):
-    queries, own, pieces, near = entry(
+    queries, own, pieces, pair, other = entry(
         req_lengths, tokens, attn_gain[None], q_gain[None], k_gain[None], w_query, w_keyval,
         prefix_kv, w_head)
-    words = w_head.shape[1] // RING
-    mine = lax.dynamic_slice_in_dim(w_head, lax.axis_index("y") * words, words, 1)
-    pair = jnp.concatenate([mine, near[0]], axis=0)
+    slab = pair.reshape(-1, pair.shape[2])
     ahead = [(2 * z + c, 2 * ((z + 1 + 2 * c) % RING) + c) for z in range(RING) for c in range(2)]
-    from_back = lax.ppermute(pair, ("z", "c"), ahead)
-    from_ahead = lax.ppermute(pair, ("z", "c"), [(b, a) for a, b in ahead])
+    from_back = lax.ppermute(slab, ("z", "c"), ahead)
+    from_ahead = lax.ppermute(slab, ("z", "c"), [(b, a) for a, b in ahead])
     attended = attention(req_lengths, req_tenant, prefix_piece, queries, own, pieces)
     share, logprob = finish(attended, tokens, mlp_gain[None], w_out, final_gain[None], targets[None],
-                            w_gate, w_up, w_down, w_head, near, from_back, from_ahead)
+                            w_gate, w_up, w_down, w_head, pair, other, from_back, from_ahead)
     return tuple(results(share, logprob))
 
 

time: 150 us -> 149 us (level)
  waiting for transfers between devices: 8.66 us -> 4.99 us
  Pallas kernels: 137 us -> 139 us
    ppermute x2, waiting for transfers between devices: 8.66 us -> 4.99 us  [the longest x1 2.62 us: body(): from_back = lax.ppermute(slab, ('z', 'c'), ahead)]
    pallas_call x1, Pallas kernels: 79.4 us -> 81.5 us  [finish(): pl.pallas_call(finish_kernel, in_specs=[vmem()] * 6 + [hbm()] * 8, out_sp...]
where the time goes in v9:
time: 149 us; the launch traced here: 148 us
  Pallas kernels  139 us (93%)
  waiting for transfers between devices  4.99 us (3%)
  starting transfers between devices  2.75 us (2%)
    pallas_call x1, Pallas kernels, finish(): pl.pallas_call(finish_kernel, in_specs=[vmem()] * 6 + [hbm()] * 8, out_sp...  81.5 us
    pallas_call x1, Pallas kernels, entry(): pl.pallas_call(functools.partial(entry_kernel, lengths.shape[1], size **...  38.3 us
    pallas_call x1, Pallas kernels, attention(): pl.pallas_call(functools.partial(attention_kernel, lengths.shape[1], piec...  17.3 us
  transfers between devices with their start and end apart: 2, of which 2 were waited for; matrix products, arithmetic and copies ran while one was open for 0% of the time, Pallas kernels for 12%

profile of v9, /device:TPU:1, one launch (start us, length us, event | category | flops | bytes accessed | tf_op | source)
XLA Modules:
  0.0 148.1 jit_solution(329464124743813486)
XLA Ops:
  0.6 38.3 %entry.1 = (bf16[4,256,128]{2,1,0:T(8,128)(2,1)}, bf16[256,128]{1,0:T(8,128)(2,1)}, bf16[16,1024,128]{2,1,0:T(8,128)(2,1)}, bf16[2,128,2048]{2,1,0:T(8,128)(2,1)}, bf16[128,2048]{1,0:T(8,128)(2,1)}) custom-call(s32[1,4]{1,0:T(1,128)} %length_ref.3, bf16[256,256]{1,0:T(8,128)(2,1)} %tok_ref.3, f32[1,2048]{1,0:T(1,128)} %bitcast.9, f32[1,64]{1,0:T(1,128)} %bitcast.13, ...), custom_call_target="tpu_custom_call" | custom-call | flops 32212254720 | bytes 8388608 | tf_op jit(solution)/shard_map/entry/pallas_call | solution.py:317
  39.0 0.7 collective-permute-start.1
  39.7 2.1 %collective-permute-start = (bf16[256,2048]{1,0:T(8,128)(2,1)}, bf16[256,2048]{1,0:T(8,128)(2,1)S(1)}, u32[]{:S(2)}, u32[]{:S(2)}) collective-permute-start(bf16[256,2048]{1,0:T(8,128)(2,1)} %bitcast.8), channel_id=1, source_target_pairs={{0,32},{1,97},{32,64},{33,1},{64,96},{65,33},{96,0},{97,65},{2,34}... | collective-permute-start | bytes 3145736 | tf_op jit(solution)/shard_map/ppermute | solution.py:678
  41.7 17.3 %attention.1.att_ref = bf16[256,256]{1,0:T(8,128)(2,1)} custom-call(s32[1,4]{1,0:T(1,128)} %length_ref.3, s32[1,4]{1,0:T(1,128)} %tenant_ref.1, s32[16]{0:T(128)} %piece_ref.1, bf16[4,256,128]{2,1,0:T(8,128)(2,1)} %get-tuple-element.9.q_ref, bf16[256,128]{1,0:T(8,128)(2,1)} %get-tuple-element.10.own_ref, bf16[16,1024,128]{2,1,0:T(8,128)(2,1)} %get-tuple-element.11.kv_ref), custom_call_target="tpu_custom_call" | custom-call | flops 25769803776 | bytes 5242880 | tf_op jit(solution)/shard_map/attention/pallas_call | solution.py:397
  59.0 2.4 %collective-permute-done.1.ahead_hbm = bf16[256,2048]{1,0:T(8,128)(2,1)S(1)} collective-permute-done((bf16[256,2048]{1,0:T(8,128)(2,1)}, bf16[256,2048]{1,0:T(8,128)(2,1)S(1)}, u32[]{:S(2)}, u32[]{:S(2)}) %collective-permute-start.1) | collective-permute-done | bytes 1048608 | tf_op jit(solution)/shard_map/ppermute | solution.py:679
  61.4 0.0 copy-start
  61.4 2.6 %collective-permute-done.back_hbm = bf16[256,2048]{1,0:T(8,128)(2,1)S(1)} collective-permute-done((bf16[256,2048]{1,0:T(8,128)(2,1)}, bf16[256,2048]{1,0:T(8,128)(2,1)S(1)}, u32[]{:S(2)}, u32[]{:S(2)}) %collective-permute-start) | collective-permute-done | bytes 1048608 | tf_op jit(solution)/shard_map/ppermute | solution.py:678
  64.0 0.0 copy-start.1
  64.0 0.0 copy-done
  64.0 1.0 copy-done.1
  65.0 81.5 %finish.1 = (bf16[256,256]{1,0:T(8,128)(2,1)}, f32[1,256]{1,0:T(1,128)}) custom-call(bf16[256,256]{1,0:T(8,128)(2,1)} %attention.1.att_ref, bf16[256,256]{1,0:T(8,128)(2,1)} %tok_ref.3, f32[1,2048]{1,0:T(1,128)} %bitcast.10, bf16[256,2048]{1,0:T(8,128)(2,1)} %wo_ref.1, f32[1,2048]{1,0:T(1,128)} %bitcast.11, s32[1,256]{1,0:T(1,128)} %bitcast.12, ...), custom_call_target="tpu_custom_call" | custom-call | flops 64424509440 | bytes 25165824 | tf_op jit(solution)/shard_map/finish/pallas_call | solution.py:629
  146.5 1.6 %results.1 = (bf16[256,256]{1,0:T(8,128)(2,1)}, f32[256]{0:T(256)}) custom-call(bf16[256,256]{1,0:T(8,128)(2,1)} %get-tuple-element.14.share_ref, f32[1,256]{1,0:T(1,128)} %get-tuple-element.15.log_ref), custom_call_target="tpu_custom_call" | custom-call | tf_op jit(solution)/shard_map/results/pallas_call | solution.py:662
Async XLA Ops:
  39.0 22.4 %collective-permute-start.1 = (bf16[256,2048]{1,0:T(8,128)(2,1)}, bf16[256,2048]{1,0:T(8,128)(2,1)S(1)}, u32[]{:S(2)}, u32[]{:S(2)}) collective-permute-start(bf16[256,2048]{1,0:T(8,128)(2,1)} %bitcast.7), channel_id=1, source_target_pairs={{32,0},{97,1},{64,32},{1,33},{96,64},{33,65},{0,96},{65,97},{34,2}... | collective-permute-start | bytes 3145736 | tf_op jit(solution)/shard_map/ppermute | solution.py:679
  39.7 24.4 %collective-permute-start = (bf16[256,2048]{1,0:T(8,128)(2,1)}, bf16[256,2048]{1,0:T(8,128)(2,1)S(1)}, u32[]{:S(2)}, u32[]{:S(2)}) collective-permute-start(bf16[256,2048]{1,0:T(8,128)(2,1)} %bitcast.8), channel_id=1, source_target_pairs={{0,32},{1,97},{32,64},{33,1},{64,96},{65,33},{96,0},{97,65},{2,34}... | collective-permute-start | bytes 3145736 | tf_op jit(solution)/shard_map/ppermute | solution.py:678
  61.4 2.6 %copy-start = (bf16[256,2048]{1,0:T(8,128)(2,1)}, bf16[256,2048]{1,0:T(8,128)(2,1)S(1)}, u32[]{:S(2)}) copy-start(bf16[256,2048]{1,0:T(8,128)(2,1)S(1)} %collective-permute-done.1.ahead_hbm) | copy-start | bytes 3145732
  64.0 1.0 copy-start.1

commit v10 on v9

--- a/solution.py
+++ b/solution.py
@@ -554,12 +554,12 @@
     def to_row(value):
         return jnp.sum(jnp.where(eye, value, 0.0), axis=0, keepdims=True)
 
-    for index, group in enumerate((y, y_down, y_up, y_far)):
-        if index in (1, 2):
+    for index, group in enumerate((y, y_far, y_down, y_up)):
+        if index > 1:
             for to in range(RING):
                 slot = 2 * to + 1 - core
                 arrived(hidden.at[group, slot], grecv.at[group, slot])
-        if index == 3:
+        if index == 1:
             distant.rest()
         normalise(hidden.at[group], last_gain_ref, normed)
         for t in range(vocab // tile):

time: 149 us -> 151 us (1.013)
  Pallas kernels: 139 us -> 141 us
    pallas_call x1, Pallas kernels: 81.5 us -> 84.2 us  [finish(): pl.pallas_call(finish_kernel, in_specs=[vmem()] * 6 + [hbm()] * 8, out_sp...]
  transfers between devices with their start and end apart: 2 -> 2, of which waited for: 2 -> 2; matrix products, arithmetic and copies ran while one was open for 0% -> 0% of each run, Pallas kernels for 12% -> 11%
where the time goes in v10:
time: 151 us
  Pallas kernels  141 us (93%)
  waiting for transfers between devices  4.99 us (3%)
  starting transfers between devices  2.75 us (2%)
    pallas_call x1, Pallas kernels, finish(): pl.pallas_call(finish_kernel, in_specs=[vmem()] * 6 + [hbm()] * 8, out_sp...  84.2 us
    pallas_call x1, Pallas kernels, entry(): pl.pallas_call(functools.partial(entry_kernel, lengths.shape[1], size **...  38.3 us
    pallas_call x1, Pallas kernels, attention(): pl.pallas_call(functools.partial(attention_kernel, lengths.shape[1], piec...  17.3 us
  transfers between devices with their start and end apart: 2, of which 2 were waited for; matrix products, arithmetic and copies ran while one was open for 0% of the time, Pallas kernels for 11%

profile of v10, /device:TPU:1, one launch (start us, length us, event | category | flops | bytes accessed | tf_op | source)
XLA Modules:
  0.0 150.8 jit_solution(13748735954187689912)
XLA Ops:
  0.6 38.3 %entry.1 = (bf16[4,256,128]{2,1,0:T(8,128)(2,1)}, bf16[256,128]{1,0:T(8,128)(2,1)}, bf16[16,1024,128]{2,1,0:T(8,128)(2,1)}, bf16[2,128,2048]{2,1,0:T(8,128)(2,1)}, bf16[128,2048]{1,0:T(8,128)(2,1)}) custom-call(s32[1,4]{1,0:T(1,128)} %length_ref.3, bf16[256,256]{1,0:T(8,128)(2,1)} %tok_ref.3, f32[1,2048]{1,0:T(1,128)} %bitcast.9, f32[1,64]{1,0:T(1,128)} %bitcast.13, ...), custom_call_target="tpu_custom_call" | custom-call | flops 32212254720 | bytes 8388608 | tf_op jit(solution)/shard_map/entry/pallas_call | solution.py:317
  39.0 0.7 collective-permute-start.1
  39.7 2.1 %collective-permute-start = (bf16[256,2048]{1,0:T(8,128)(2,1)}, bf16[256,2048]{1,0:T(8,128)(2,1)S(1)}, u32[]{:S(2)}, u32[]{:S(2)}) collective-permute-start(bf16[256,2048]{1,0:T(8,128)(2,1)} %bitcast.8), channel_id=1, source_target_pairs={{0,32},{1,97},{32,64},{33,1},{64,96},{65,33},{96,0},{97,65},{2,34}... | collective-permute-start | bytes 3145736 | tf_op jit(solution)/shard_map/ppermute | solution.py:678
  41.7 17.3 %attention.1.att_ref = bf16[256,256]{1,0:T(8,128)(2,1)} custom-call(s32[1,4]{1,0:T(1,128)} %length_ref.3, s32[1,4]{1,0:T(1,128)} %tenant_ref.1, s32[16]{0:T(128)} %piece_ref.1, bf16[4,256,128]{2,1,0:T(8,128)(2,1)} %get-tuple-element.9.q_ref, bf16[256,128]{1,0:T(8,128)(2,1)} %get-tuple-element.10.own_ref, bf16[16,1024,128]{2,1,0:T(8,128)(2,1)} %get-tuple-element.11.kv_ref), custom_call_target="tpu_custom_call" | custom-call | flops 25769803776 | bytes 5242880 | tf_op jit(solution)/shard_map/attention/pallas_call | solution.py:397
  59.0 2.4 %collective-permute-done.1.ahead_hbm = bf16[256,2048]{1,0:T(8,128)(2,1)S(1)} collective-permute-done((bf16[256,2048]{1,0:T(8,128)(2,1)}, bf16[256,2048]{1,0:T(8,128)(2,1)S(1)}, u32[]{:S(2)}, u32[]{:S(2)}) %collective-permute-start.1) | collective-permute-done | bytes 1048608 | tf_op jit(solution)/shard_map/ppermute | solution.py:679
  61.4 0.0 copy-start
  61.4 2.6 %collective-permute-done.back_hbm = bf16[256,2048]{1,0:T(8,128)(2,1)S(1)} collective-permute-done((bf16[256,2048]{1,0:T(8,128)(2,1)}, bf16[256,2048]{1,0:T(8,128)(2,1)S(1)}, u32[]{:S(2)}, u32[]{:S(2)}) %collective-permute-start) | collective-permute-done | bytes 1048608 | tf_op jit(solution)/shard_map/ppermute | solution.py:678
  64.0 0.0 copy-start.1
  64.0 0.0 copy-done
  64.0 1.0 copy-done.1
  65.0 84.2 %finish.1 = (bf16[256,256]{1,0:T(8,128)(2,1)}, f32[1,256]{1,0:T(1,128)}) custom-call(bf16[256,256]{1,0:T(8,128)(2,1)} %attention.1.att_ref, bf16[256,256]{1,0:T(8,128)(2,1)} %tok_ref.3, f32[1,2048]{1,0:T(1,128)} %bitcast.10, bf16[256,2048]{1,0:T(8,128)(2,1)} %wo_ref.1, f32[1,2048]{1,0:T(1,128)} %bitcast.11, s32[1,256]{1,0:T(1,128)} %bitcast.12, ...), custom_call_target="tpu_custom_call" | custom-call | flops 64424509440 | bytes 25165824 | tf_op jit(solution)/shard_map/finish/pallas_call | solution.py:629
  149.2 1.6 %results.1 = (bf16[256,256]{1,0:T(8,128)(2,1)}, f32[256]{0:T(256)}) custom-call(bf16[256,256]{1,0:T(8,128)(2,1)} %get-tuple-element.14.share_ref, f32[1,256]{1,0:T(1,128)} %get-tuple-element.15.log_ref), custom_call_target="tpu_custom_call" | custom-call | tf_op jit(solution)/shard_map/results/pallas_call | solution.py:662
Async XLA Ops:
  39.0 22.4 %collective-permute-start.1 = (bf16[256,2048]{1,0:T(8,128)(2,1)}, bf16[256,2048]{1,0:T(8,128)(2,1)S(1)}, u32[]{:S(2)}, u32[]{:S(2)}) collective-permute-start(bf16[256,2048]{1,0:T(8,128)(2,1)} %bitcast.7), channel_id=1, source_target_pairs={{32,0},{97,1},{64,32},{1,33},{96,64},{33,65},{0,96},{65,97},{34,2}... | collective-permute-start | bytes 3145736 | tf_op jit(solution)/shard_map/ppermute | solution.py:679
  39.7 24.4 %collective-permute-start = (bf16[256,2048]{1,0:T(8,128)(2,1)}, bf16[256,2048]{1,0:T(8,128)(2,1)S(1)}, u32[]{:S(2)}, u32[]{:S(2)}) collective-permute-start(bf16[256,2048]{1,0:T(8,128)(2,1)} %bitcast.8), channel_id=1, source_target_pairs={{0,32},{1,97},{32,64},{33,1},{64,96},{65,33},{96,0},{97,65},{2,34}... | collective-permute-start | bytes 3145736 | tf_op jit(solution)/shard_map/ppermute | solution.py:678
  61.4 2.6 %copy-start = (bf16[256,2048]{1,0:T(8,128)(2,1)}, bf16[256,2048]{1,0:T(8,128)(2,1)S(1)}, u32[]{:S(2)}) copy-start(bf16[256,2048]{1,0:T(8,128)(2,1)S(1)} %collective-permute-done.1.ahead_hbm) | copy-start | bytes 3145732
  64.0 1.0 copy-start.1
